TPU v7x, 512 devices: a whole 4x8x8 slice. The times are simulated.
512 devices in a mesh: pair: 2 (over x_lo), row: 16 (over y, x_hi), col: 16 (over z, core).
Axes of the slice: x: 4 (x_hi: 2, x_lo: 2; x = x_hi * 2 + x_lo), y: 8, z: 8, core: 2. Of those that a mesh axis runs over, the one named last changes fastest.
Arguments:
- features: bfloat16 [2, 64, 256, 2048], P('pair', None, 'row', 'col'), may hold values from -6 to 6
- offsets: int32 [2, 2, 256, 2048], P('pair', None, 'row', 'col'), may hold values from -8 to 7
- fractions: int32 [2, 2, 256, 2048], P('pair', None, 'row', 'col'), may hold values from 0 to 255
- tissue: int32 [2, 32, 256], P('pair', 'row', 'col'), may hold values 0 or 1
- w_first: bfloat16 [9, 64, 128], replicated, may hold values from -0.1875 to 0.1875
- w_second: bfloat16 [9, 64, 64], replicated, may hold values from -0.25 to 0.25
- head_weight: bfloat16 [2, 64], replicated, may hold values from -0.75 to 0.75
Outputs:
- warped_features: bfloat16 [2, 64, 256, 2048], P('pair', None, 'row', 'col')
- motion_field: float32 [2, 2, 256, 2048], P('pair', None, 'row', 'col')
All inputs are finite; a program needn't handle non-finite values. No bound on the sum of `tissue` on one device may be relied on, other than what follows from the above.
Results may differ from a plain program's by a relative error of at most 0.0056.
Values may be sent and summed in bfloat16 or wider, within the bound.
No kernel may reach another device: no remote copies, remote signals or barrier semaphores. Data moves between devices by JAX's collectives and lax.ppermute only.
A program may use at most 64 MiB of HBM per device.

v0:
```python
import jax
import jax.numpy as jnp
from jax import lax
from jax.sharding import PartitionSpec as P

MAXS = 8
BLK = 8


frac_scale = 256.0


def swapped(value, axis, bit):
    mask = 2**bit
    pairs = [(source, source ^ mask) for source in range(lax.axis_size(axis))]
    return lax.ppermute(value, axis, pairs)


def padded_2(shard, sides, width):
    for axis, dim in sides:
        peers, length = (lax.axis_size(axis), shard.shape[dim])
        up = [(i, (i + 1) % peers) for i in range(peers - 1)]
        down = [(j, i) for i, j in up]
        last = lax.slice_in_dim(shard, length - width, length, axis=dim)
        leading = lax.slice_in_dim(shard, 0, width, axis=dim)
        before = lax.ppermute(last, axis, up)
        after = lax.ppermute(leading, axis, down)
        shard = jnp.concatenate([before, shard, after], axis=dim)
    return shard


def convolve(padded, weights, height, columns):
    summed = None
    for tap_index in range(9):
        row_shift = tap_index // 3
        col_shift = tap_index % 3
        window = padded[:, row_shift : row_shift + height, col_shift : col_shift + columns]
        window = window.reshape(padded.shape[0], height * columns)
        product = jnp.dot(weights[tap_index], window, preferred_element_type=jnp.float32)
        summed = product if summed is None else summed + product
    return summed.reshape(weights.shape[1], height, columns)


def sample(source, motion, margin, height, columns):
    stride = columns + 2 * margin
    grid_rows = lax.broadcasted_iota(jnp.int32, (height, columns), 0).astype(jnp.float32)
    grid_cols = lax.broadcasted_iota(jnp.int32, (height, columns), 1).astype(jnp.float32)
    place_row = grid_rows + motion[0] + margin
    place_col = grid_cols + motion[1] + margin
    floor_row = jnp.floor(place_row)
    floor_col = jnp.floor(place_col)
    frac_row = place_row - floor_row
    frac_col = place_col - floor_col
    base_index = floor_row.astype(jnp.int32) * stride + floor_col.astype(jnp.int32)
    flat_source = source.reshape(source.shape[0], -1)

    def fetch(step_size):
        picked = jnp.take(flat_source, (base_index + step_size).reshape(-1), axis=1, mode="clip")
        return picked.reshape(source.shape[0], height, columns).astype(jnp.float32)

    blended = (1.0 - frac_row) * (1.0 - frac_col) * fetch(0) + (1.0 - frac_row) * frac_col * fetch(
        1
    )
    blended = blended + frac_row * (1.0 - frac_col) * fetch(stride)
    blended = blended + frac_row * frac_col * fetch(stride + 1)
    return blended.astype(jnp.bfloat16)


def shards(features, offsets, fractions, tissue, w_first, w_second, head_weight):
    channels = features.shape[1]
    height = features.shape[2]
    columns = features.shape[3]
    margin = MAXS + 1
    own_features = features[0]
    partner = swapped(own_features, "pair", 0)
    joined = jnp.concatenate([own_features, partner], axis=0)
    source_band = padded_2(own_features, (("row", 1), ("col", 2)), margin)
    hidden_one = jax.nn.relu(
        convolve(padded_2(joined, (("row", 1), ("col", 2)), 1), w_first, height, columns)
    ).astype(jnp.bfloat16)
    padded_hidden = padded_2(hidden_one, (("row", 1), ("col", 2)), 1)
    hidden_two = jax.nn.relu(convolve(padded_hidden, w_second, height, columns)).astype(
        jnp.bfloat16
    )
    residual = jnp.tanh(
        jnp.dot(
            head_weight,
            hidden_two.reshape(channels, height * columns),
            preferred_element_type=jnp.float32,
        )
    )
    residual = residual.reshape(2, height, columns)
    coverage = jnp.repeat(jnp.repeat(tissue[0], BLK, axis=0), BLK, axis=1).astype(jnp.float32)
    motion = offsets[0].astype(jnp.float32) + fractions[0].astype(jnp.float32) / frac_scale
    motion = motion + coverage[None] * residual
    warped = sample(source_band, motion, margin, height, columns)
    return (warped[None], motion[None])


def solution(mesh):
    return jax.shard_map(
        shards,
        mesh=mesh,
        in_specs=(
            P("pair", None, "row", "col"),
            P("pair", None, "row", "col"),
            P("pair", None, "row", "col"),
            P("pair", "row", "col"),
            P(),
            P(),
            P(),
        ),
        out_specs=(P("pair", None, "row", "col"), P("pair", None, "row", "col")),
        check_vma=False,
    )
```

profile of v0, /device:TPU:217, one launch (start us, length us, event | category | flops | bytes accessed | tf_op | source)
XLA Modules:
  0.0 132.3 jit_solution(16149549492064868573)
XLA Ops:
  0.7 1.3 copy.55
  1.9 3.1 %collective-permute-start = (bf16[64,16,128]{0,2,1:T(8,128)(2,1)S(1)}, bf16[64,16,128]{0,2,1:T(8,128)(2,1)S(1)}, u32[]{:S(2)}, u32[]{:S(2)}) collective-permute-start(bf16[64,16,128]{0,2,1:T(8,128)(2,1)S(1)} %bitcast.167), channel_id=1, source_target_pairs={{0,256},{256,0},{1,257},{257,1},{2,258},{258,2},{3,259},{259,3},{4... | collective-permute-start | bytes 786440 | tf_op jit(solution)/shard_map/ppermute | solution.py:16
  5.1 4.2 %collective-permute-start.10 = (bf16[64,9,128]{0,2,1:T(8,128)(2,1)S(1)}, bf16[64,9,128]{0,2,1:T(8,128)(2,1)S(1)}, u32[]{:S(2)}, u32[]{:S(2)}) collective-permute-start(bf16[64,9,128]{0,2,1:T(8,128)(2,1)S(1)} %get-tuple-element.27), channel_id=1, source_target_pairs={{16,0},{32,16},{48,32},{64,48},{80,64},{96,80},{112,96},{128,112},... | collective-permute-start | bytes 442376 | tf_op jit(solution)/shard_map/ppermute | solution.py:27
  9.4 2.5 %collective-permute-start.9 = (bf16[64,9,128]{0,2,1:T(8,128)(2,1)S(1)}, bf16[64,9,128]{0,2,1:T(8,128)(2,1)S(1)}, u32[]{:S(2)}, u32[]{:S(2)}) collective-permute-start(bf16[64,9,128]{0,2,1:T(8,128)(2,1)S(1)} %get-tuple-element.26), channel_id=1, source_target_pairs={{0,16},{16,32},{32,48},{48,64},{64,80},{80,96},{96,112},{112,128},... | collective-permute-start | bytes 442376 | tf_op jit(solution)/shard_map/ppermute | solution.py:26
  12.1 19.4 %collective-permute-done.10 = bf16[64,9,128]{0,2,1:T(8,128)(2,1)S(1)} collective-permute-done((bf16[64,9,128]{0,2,1:T(8,128)(2,1)S(1)}, bf16[64,9,128]{0,2,1:T(8,128)(2,1)S(1)}, u32[]{:S(2)}, u32[]{:S(2)}) %collective-permute-start.10) | collective-permute-done | bytes 147488 | tf_op jit(solution)/shard_map/ppermute | solution.py:27
  31.6 6.6 %collective-permute-start.11 = (bf16[64,34,9]{0,1,2:T(8,128)(2,1)S(1)}, bf16[64,34,9]{0,1,2:T(8,128)(2,1)S(1)}, u32[]{:S(2)}, u32[]{:S(2)}) collective-permute-start(bf16[64,34,9]{0,1,2:T(8,128)(2,1)S(1)} %copy.61), channel_id=1, source_target_pairs={{0,1},{1,2},{2,3},{3,4},{4,5},{5,6},{6,7},{7,8},{8,9},{9,10},{10,1... | collective-permute-start | bytes 117512 | tf_op jit(solution)/shard_map/ppermute | solution.py:26
  38.3 1.9 %collective-permute-start.12 = (bf16[64,34,9]{0,1,2:T(8,128)(2,1)S(1)}, bf16[64,34,9]{0,1,2:T(8,128)(2,1)S(1)}, u32[]{:S(2)}, u32[]{:S(2)}) collective-permute-start(bf16[64,34,9]{0,1,2:T(8,128)(2,1)S(1)} %copy.62), channel_id=1, source_target_pairs={{1,0},{2,1},{3,2},{4,3},{5,4},{6,5},{7,6},{8,7},{9,8},{10,9},{11,1... | collective-permute-start | bytes 117512 | tf_op jit(solution)/shard_map/ppermute | solution.py:27
  40.3 2.4 %collective-permute-start.1 = (bf16[128,1,128]{0,2,1:T(8,128)(2,1)S(1)}, bf16[128,1,128]{0,2,1:T(8,128)(2,1)S(1)}, u32[]{:S(2)}, u32[]{:S(2)}) collective-permute-start(bf16[128,1,128]{0,2,1:T(8,128)(2,1)S(1)} %get-tuple-element.12), channel_id=1, source_target_pairs={{0,16},{16,32},{32,48},{48,64},{64,80},{80,96},{96,112},{112,128},... | collective-permute-start | bytes 98312 | tf_op jit(solution)/shard_map/ppermute | solution.py:26
  42.7 5.3 %collective-permute-start.2 = (bf16[128,1,128]{0,2,1:T(8,128)(2,1)S(1)}, bf16[128,1,128]{0,2,1:T(8,128)(2,1)S(1)}, u32[]{:S(2)}, u32[]{:S(2)}) collective-permute-start(bf16[128,1,128]{0,2,1:T(8,128)(2,1)S(1)} %get-tuple-element.13), channel_id=1, source_target_pairs={{16,0},{32,16},{48,32},{64,48},{80,64},{96,80},{112,96},{128,112},... | collective-permute-start | bytes 98312 | tf_op jit(solution)/shard_map/ppermute | solution.py:27
  48.2 0.7 copy.63
  48.9 0.7 copy.64
  49.8 0.8 collective-permute-done.2
  50.7 6.0 %collective-permute-start.3 = (bf16[128,18,1]{0,1,2:T(8,128)(2,1)S(1)}, bf16[128,18,1]{0,1,2:T(8,128)(2,1)S(1)}, u32[]{:S(2)}, u32[]{:S(2)}) collective-permute-start(bf16[128,18,1]{0,1,2:T(8,128)(2,1)S(1)} %copy.56), channel_id=1, source_target_pairs={{0,1},{1,2},{2,3},{3,4},{4,5},{5,6},{6,7},{7,8},{8,9},{9,10},{10,1... | collective-permute-start | bytes 13832 | tf_op jit(solution)/shard_map/ppermute | solution.py:26
  56.8 1.9 %collective-permute-start.4 = (bf16[128,18,1]{0,1,2:T(8,128)(2,1)S(1)}, bf16[128,18,1]{0,1,2:T(8,128)(2,1)S(1)}, u32[]{:S(2)}, u32[]{:S(2)}) collective-permute-start(bf16[128,18,1]{0,1,2:T(8,128)(2,1)S(1)} %copy.58), channel_id=1, source_target_pairs={{1,0},{2,1},{3,2},{4,3},{5,4},{6,5},{7,6},{8,7},{9,8},{10,9},{11,1... | collective-permute-start | bytes 13832 | tf_op jit(solution)/shard_map/ppermute | solution.py:27
  58.7 0.4 pad_maximum_fusion.3
  59.1 3.8 %collective-permute-done.4 = bf16[128,18,1]{0,1,2:T(8,128)(2,1)S(1)} collective-permute-done((bf16[128,18,1]{0,1,2:T(8,128)(2,1)S(1)}, bf16[128,18,1]{0,1,2:T(8,128)(2,1)S(1)}, u32[]{:S(2)}, u32[]{:S(2)}) %collective-permute-start.4) | collective-permute-done | bytes 4640 | tf_op jit(solution)/shard_map/ppermute | solution.py:27
  62.9 0.6 maximum_maximum_fusion.1
  63.6 0.6 fusion.79
  64.2 0.3 copy-done.7
  64.5 0.3 fusion.54
  64.8 0.3 fusion.46
  65.1 0.3 fusion.48
  65.4 0.3 fusion.43
  65.7 0.3 convolution_add_fusion.12
  66.0 0.3 convolution_add_fusion.11
  66.3 0.3 convolution_add_fusion.10
  66.6 0.2 fusion.3
  66.9 0.3 fusion.6
  67.2 0.7 fusion.83
  67.9 7.2 %collective-permute-start.5 = (bf16[64,1,128]{2,1,0:T(2,128)(2,1)}, bf16[64,1,128]{2,1,0:T(2,128)(2,1)S(1)}, u32[]{:S(2)}, u32[]{:S(2)}) collective-permute-start(bf16[64,1,128]{2,1,0:T(2,128)(2,1)} %get-tuple-element.34), channel_id=1, source_target_pairs={{0,16},{16,32},{32,48},{48,64},{64,80},{80,96},{96,112},{112,128},... | collective-permute-start | bytes 49160 | tf_op jit(solution)/shard_map/ppermute | solution.py:26
  75.1 1.9 %collective-permute-start.6 = (bf16[64,1,128]{2,1,0:T(2,128)(2,1)S(1)}, bf16[64,1,128]{2,1,0:T(2,128)(2,1)S(1)}, u32[]{:S(2)}, u32[]{:S(2)}) collective-permute-start(bf16[64,1,128]{2,1,0:T(2,128)(2,1)S(1)} %get-tuple-element.35), channel_id=1, source_target_pairs={{16,0},{32,16},{48,32},{64,48},{80,64},{96,80},{112,96},{128,112},... | collective-permute-start | bytes 49160 | tf_op jit(solution)/shard_map/ppermute | solution.py:27
  77.1 0.5 pad_maximum_fusion
  77.6 0.5 reshape.402
  78.1 3.2 %collective-permute-done.6 = bf16[64,1,128]{2,1,0:T(2,128)(2,1)S(1)} collective-permute-done((bf16[64,1,128]{2,1,0:T(2,128)(2,1)S(1)}, bf16[64,1,128]{2,1,0:T(2,128)(2,1)S(1)}, u32[]{:S(2)}, u32[]{:S(2)}) %collective-permute-start.6) | collective-permute-done | bytes 16416 | tf_op jit(solution)/shard_map/ppermute | solution.py:27
  81.3 0.2 pad_maximum_fusion.7
  81.7 3.4 %collective-permute-start.7 = (bf16[64,18,1]{2,1,0:T(8,128)(2,1)S(1)}, bf16[64,18,1]{2,1,0:T(8,128)(2,1)S(1)}, u32[]{:S(2)}, u32[]{:S(2)}) collective-permute-start(bf16[64,18,1]{2,1,0:T(8,128)(2,1)S(1)} %get-tuple-element.29), channel_id=1, source_target_pairs={{0,1},{1,2},{2,3},{3,4},{4,5},{5,6},{6,7},{7,8},{8,9},{9,10},{10,1... | collective-permute-start | bytes 6920 | tf_op jit(solution)/shard_map/ppermute | solution.py:26
  85.1 2.1 %collective-permute-start.8 = (bf16[64,18,1]{2,1,0:T(8,128)(2,1)S(1)}, bf16[64,18,1]{2,1,0:T(8,128)(2,1)S(1)}, u32[]{:S(2)}, u32[]{:S(2)}) collective-permute-start(bf16[64,18,1]{2,1,0:T(8,128)(2,1)S(1)} %get-tuple-element.28), channel_id=1, source_target_pairs={{1,0},{2,1},{3,2},{4,3},{5,4},{6,5},{7,6},{8,7},{9,8},{10,9},{11,1... | collective-permute-start | bytes 6920 | tf_op jit(solution)/shard_map/ppermute | solution.py:27
  87.2 0.3 pad_maximum_fusion.8
  87.5 2.3 %collective-permute-done.7 = bf16[64,18,1]{2,1,0:T(8,128)(2,1)S(1)} collective-permute-done((bf16[64,18,1]{2,1,0:T(8,128)(2,1)S(1)}, bf16[64,18,1]{2,1,0:T(8,128)(2,1)S(1)}, u32[]{:S(2)}, u32[]{:S(2)}) %collective-permute-start.7) | collective-permute-done | bytes 2336 | tf_op jit(solution)/shard_map/ppermute | solution.py:26
  89.8 5.6 %collective-permute-done.8 = bf16[64,18,1]{2,1,0:T(8,128)(2,1)S(1)} collective-permute-done((bf16[64,18,1]{2,1,0:T(8,128)(2,1)S(1)}, bf16[64,18,1]{2,1,0:T(8,128)(2,1)S(1)}, u32[]{:S(2)}, u32[]{:S(2)}) %collective-permute-start.8) | collective-permute-done | bytes 2336 | tf_op jit(solution)/shard_map/ppermute | solution.py:27
  95.4 1.1 pad_maximum_fusion.1
  96.7 0.4 fusion.77
  97.2 0.3 copy-done.8
  97.5 0.2 fusion.27
  97.7 0.2 convolution_add_fusion.7
  97.9 0.2 convolution_add_fusion.6
  98.1 0.2 convolution_add_fusion.5
  98.3 0.2 convolution_add_fusion.4
  98.6 0.2 convolution_add_fusion.3
  98.8 0.2 convolution_add_fusion.2
  99.0 0.2 convolution_add_fusion.1
  99.2 0.3 fusion.7
  99.7 0.6 fusion.31
  100.6 6.2 %gather_fusion = bf16[2048,64]{1,0:T(8,128)(2,1)S(1)} fusion(bf16[64,4964]{0,1:T(8,128)(2,1)S(1)} %reshape.402, s32[2048]{0:T(1024)S(1)} %broadcast_clamp_fusion.3), kind=kCustom, calls=%fused_computation | custom fusion | bytes 532480 | tf_op jit(solution)/shard_map/jit(_take)/gather | solution.py:58
  106.8 0.4 copy.67
  107.3 6.2 %gather_fusion.1 = bf16[2048,64]{1,0:T(8,128)(2,1)S(1)} fusion(bf16[64,4964]{0,1:T(8,128)(2,1)S(1)} %reshape.402, s32[2048]{0:T(1024)S(1)} %broadcast_clamp_fusion.2), kind=kCustom, calls=%fused_computation.1 | custom fusion | bytes 532480 | tf_op jit(solution)/shard_map/jit(_take)/gather | solution.py:58
  113.5 0.4 copy.69
  113.9 8.0 %gather_fusion.2 = bf16[2048,64]{1,0:T(8,128)(2,1)} fusion(bf16[64,4964]{0,1:T(8,128)(2,1)S(1)} %reshape.402, s32[2048]{0:T(1024)S(1)} %broadcast_clamp_fusion.1), kind=kCustom, calls=%fused_computation.2 | custom fusion | bytes 532480 | tf_op jit(solution)/shard_map/jit(_take)/gather | solution.py:58
  122.0 1.1 convert_element_type.187
  123.1 1.1 copy.71
  124.2 6.2 %gather_fusion.3 = bf16[2048,64]{1,0:T(8,128)(2,1)S(1)} fusion(bf16[64,4964]{0,1:T(8,128)(2,1)S(1)} %reshape.402, s32[2048]{0:T(1024)S(1)} %broadcast_clamp_fusion), kind=kCustom, calls=%fused_computation.3 | custom fusion | bytes 532480 | tf_op jit(solution)/shard_map/jit(_take)/gather | solution.py:58
  130.5 0.4 copy.73
  130.9 0.6 copy-done.1
  131.4 0.9 add_convert_fusion
  (63 shorter events, 1.9 us)
Async XLA Ops:
  0.6 98.6 %copy-start = (bf16[2,64]{1,0:T(2,128)(2,1)S(1)}, bf16[2,64]{1,0:T(2,128)(2,1)}, u32[]{:S(2)}) copy-start(bf16[2,64]{1,0:T(2,128)(2,1)} %param.13) | copy-start | bytes 772
  0.6 11.3 %copy-start.11 = (s32[1,2,16]{2,1,0:T(2,128)S(1)}, s32[1,2,16]{2,1,0:T(2,128)}, u32[]{:S(2)}) copy-start(s32[1,2,16]{2,1,0:T(2,128)} %param.10) | copy-start | bytes 388
  1.9 38.3 %collective-permute-start = (bf16[64,16,128]{0,2,1:T(8,128)(2,1)S(1)}, bf16[64,16,128]{0,2,1:T(8,128)(2,1)S(1)}, u32[]{:S(2)}, u32[]{:S(2)}) collective-permute-start(bf16[64,16,128]{0,2,1:T(8,128)(2,1)S(1)} %bitcast.167), channel_id=1, source_target_pairs={{0,256},{256,0},{1,257},{257,1},{2,258},{258,2},{3,259},{259,3},{4... | collective-permute-start | bytes 786440 | tf_op jit(solution)/shard_map/ppermute | solution.py:16
  5.1 26.3 %collective-permute-start.10 = (bf16[64,9,128]{0,2,1:T(8,128)(2,1)S(1)}, bf16[64,9,128]{0,2,1:T(8,128)(2,1)S(1)}, u32[]{:S(2)}, u32[]{:S(2)}) collective-permute-start(bf16[64,9,128]{0,2,1:T(8,128)(2,1)S(1)} %get-tuple-element.27), channel_id=1, source_target_pairs={{16,0},{32,16},{48,32},{64,48},{80,64},{96,80},{112,96},{128,112},... | collective-permute-start | bytes 442376 | tf_op jit(solution)/shard_map/ppermute | solution.py:27
  9.4 22.1 %collective-permute-start.9 = (bf16[64,9,128]{0,2,1:T(8,128)(2,1)S(1)}, bf16[64,9,128]{0,2,1:T(8,128)(2,1)S(1)}, u32[]{:S(2)}, u32[]{:S(2)}) collective-permute-start(bf16[64,9,128]{0,2,1:T(8,128)(2,1)S(1)} %get-tuple-element.26), channel_id=1, source_target_pairs={{0,16},{16,32},{32,48},{48,64},{64,80},{80,96},{96,112},{112,128},... | collective-permute-start | bytes 442376 | tf_op jit(solution)/shard_map/ppermute | solution.py:26
  12.1 36.0 %copy-start.4 = (bf16[1,64,16,128]{3,2,1,0:T(8,128)(2,1)S(1)}, bf16[1,64,16,128]{3,2,1,0:T(8,128)(2,1)}, u32[]{:S(2)}) copy-start(bf16[1,64,16,128]{3,2,1,0:T(8,128)(2,1)} %param.7) | copy-start | bytes 786436
  31.5 8.8 %copy-start.2 = (bf16[64,9,128]{0,2,1:T(8,128)(2,1)}, bf16[64,9,128]{0,2,1:T(8,128)(2,1)S(1)}, u32[]{:S(2)}) copy-start(bf16[64,9,128]{0,2,1:T(8,128)(2,1)S(1)} %collective-permute-done.9) | copy-start | bytes 442372
  31.6 16.6 %collective-permute-start.11 = (bf16[64,34,9]{0,1,2:T(8,128)(2,1)S(1)}, bf16[64,34,9]{0,1,2:T(8,128)(2,1)S(1)}, u32[]{:S(2)}, u32[]{:S(2)}) collective-permute-start(bf16[64,34,9]{0,1,2:T(8,128)(2,1)S(1)} %copy.61), channel_id=1, source_target_pairs={{0,1},{1,2},{2,3},{3,4},{4,5},{5,6},{6,7},{7,8},{8,9},{9,10},{10,1... | collective-permute-start | bytes 117512 | tf_op jit(solution)/shard_map/ppermute | solution.py:26
  38.3 10.6 %collective-permute-start.12 = (bf16[64,34,9]{0,1,2:T(8,128)(2,1)S(1)}, bf16[64,34,9]{0,1,2:T(8,128)(2,1)S(1)}, u32[]{:S(2)}, u32[]{:S(2)}) collective-permute-start(bf16[64,34,9]{0,1,2:T(8,128)(2,1)S(1)} %copy.62), channel_id=1, source_target_pairs={{1,0},{2,1},{3,2},{4,3},{5,4},{6,5},{7,6},{8,7},{9,8},{10,9},{11,1... | collective-permute-start | bytes 117512 | tf_op jit(solution)/shard_map/ppermute | solution.py:27
  40.3 9.5 %collective-permute-start.1 = (bf16[128,1,128]{0,2,1:T(8,128)(2,1)S(1)}, bf16[128,1,128]{0,2,1:T(8,128)(2,1)S(1)}, u32[]{:S(2)}, u32[]{:S(2)}) collective-permute-start(bf16[128,1,128]{0,2,1:T(8,128)(2,1)S(1)} %get-tuple-element.12), channel_id=1, source_target_pairs={{0,16},{16,32},{32,48},{48,64},{64,80},{80,96},{96,112},{112,128},... | collective-permute-start | bytes 98312 | tf_op jit(solution)/shard_map/ppermute | solution.py:26
  42.7 7.9 %collective-permute-start.2 = (bf16[128,1,128]{0,2,1:T(8,128)(2,1)S(1)}, bf16[128,1,128]{0,2,1:T(8,128)(2,1)S(1)}, u32[]{:S(2)}, u32[]{:S(2)}) collective-permute-start(bf16[128,1,128]{0,2,1:T(8,128)(2,1)S(1)} %get-tuple-element.13), channel_id=1, source_target_pairs={{16,0},{32,16},{48,32},{64,48},{80,64},{96,80},{112,96},{128,112},... | collective-permute-start | bytes 98312 | tf_op jit(solution)/shard_map/ppermute | solution.py:27
  50.7 8.4 %collective-permute-start.3 = (bf16[128,18,1]{0,1,2:T(8,128)(2,1)S(1)}, bf16[128,18,1]{0,1,2:T(8,128)(2,1)S(1)}, u32[]{:S(2)}, u32[]{:S(2)}) collective-permute-start(bf16[128,18,1]{0,1,2:T(8,128)(2,1)S(1)} %copy.56), channel_id=1, source_target_pairs={{0,1},{1,2},{2,3},{3,4},{4,5},{5,6},{6,7},{7,8},{8,9},{9,10},{10,1... | collective-permute-start | bytes 13832 | tf_op jit(solution)/shard_map/ppermute | solution.py:26
  56.8 6.2 %collective-permute-start.4 = (bf16[128,18,1]{0,1,2:T(8,128)(2,1)S(1)}, bf16[128,18,1]{0,1,2:T(8,128)(2,1)S(1)}, u32[]{:S(2)}, u32[]{:S(2)}) collective-permute-start(bf16[128,18,1]{0,1,2:T(8,128)(2,1)S(1)} %copy.58), channel_id=1, source_target_pairs={{1,0},{2,1},{3,2},{4,3},{5,4},{6,5},{7,6},{8,7},{9,8},{10,9},{11,1... | collective-permute-start | bytes 13832 | tf_op jit(solution)/shard_map/ppermute | solution.py:27
  63.6 0.9 copy-start.7
  66.9 10.2 %copy-start.3 = (bf16[64,9,128]{0,2,1:T(8,128)(2,1)S(1)}, bf16[64,9,128]{0,2,1:T(8,128)(2,1)}, u32[]{:S(2)}) copy-start(bf16[64,9,128]{0,2,1:T(8,128)(2,1)} %copy-done.2) | copy-start | bytes 442372
  66.9 10.2 %copy-start.5 = (bf16[64,34,9]{0,2,1:T(8,128)(2,1)S(1)}, bf16[64,34,9]{0,2,1:T(8,128)(2,1)}, u32[]{:S(2)}) copy-start(bf16[64,34,9]{0,2,1:T(8,128)(2,1)} %copy.63) | copy-start | bytes 117508
  66.9 10.2 %copy-start.6 = (bf16[64,34,9]{0,2,1:T(8,128)(2,1)S(1)}, bf16[64,34,9]{0,2,1:T(8,128)(2,1)}, u32[]{:S(2)}) copy-start(bf16[64,34,9]{0,2,1:T(8,128)(2,1)} %copy.64) | copy-start | bytes 117508
  67.9 10.2 %collective-permute-start.5 = (bf16[64,1,128]{2,1,0:T(2,128)(2,1)}, bf16[64,1,128]{2,1,0:T(2,128)(2,1)S(1)}, u32[]{:S(2)}, u32[]{:S(2)}) collective-permute-start(bf16[64,1,128]{2,1,0:T(2,128)(2,1)} %get-tuple-element.34), channel_id=1, source_target_pairs={{0,16},{16,32},{32,48},{48,64},{64,80},{80,96},{96,112},{112,128},... | collective-permute-start | bytes 49160 | tf_op jit(solution)/shard_map/ppermute | solution.py:26
  75.1 6.2 %collective-permute-start.6 = (bf16[64,1,128]{2,1,0:T(2,128)(2,1)S(1)}, bf16[64,1,128]{2,1,0:T(2,128)(2,1)S(1)}, u32[]{:S(2)}, u32[]{:S(2)}) collective-permute-start(bf16[64,1,128]{2,1,0:T(2,128)(2,1)S(1)} %get-tuple-element.35), channel_id=1, source_target_pairs={{16,0},{32,16},{48,32},{64,48},{80,64},{96,80},{112,96},{128,112},... | collective-permute-start | bytes 49160 | tf_op jit(solution)/shard_map/ppermute | solution.py:27
  81.7 8.1 %collective-permute-start.7 = (bf16[64,18,1]{2,1,0:T(8,128)(2,1)S(1)}, bf16[64,18,1]{2,1,0:T(8,128)(2,1)S(1)}, u32[]{:S(2)}, u32[]{:S(2)}) collective-permute-start(bf16[64,18,1]{2,1,0:T(8,128)(2,1)S(1)} %get-tuple-element.29), channel_id=1, source_target_pairs={{0,1},{1,2},{2,3},{3,4},{4,5},{5,6},{6,7},{7,8},{8,9},{9,10},{10,1... | collective-permute-start | bytes 6920 | tf_op jit(solution)/shard_map/ppermute | solution.py:26
  85.1 10.3 %collective-permute-start.8 = (bf16[64,18,1]{2,1,0:T(8,128)(2,1)S(1)}, bf16[64,18,1]{2,1,0:T(8,128)(2,1)S(1)}, u32[]{:S(2)}, u32[]{:S(2)}) collective-permute-start(bf16[64,18,1]{2,1,0:T(8,128)(2,1)S(1)} %get-tuple-element.28), channel_id=1, source_target_pairs={{1,0},{2,1},{3,2},{4,3},{5,4},{6,5},{7,6},{8,7},{9,8},{10,9},{11,1... | collective-permute-start | bytes 6920 | tf_op jit(solution)/shard_map/ppermute | solution.py:27
  96.5 0.9 copy-start.8
  99.0 0.7 copy-start.9
  99.0 0.7 copy-start.10
  130.4 1.0 copy-start.1
where the time goes:
time: 133 us; the launch traced here: 132 us
  starting transfers between devices  48.7 us (37%)
  local copies, waits for them, and re-layouts  36.1 us (27%)
  waiting for transfers between devices  35.2 us (26%)
  other arithmetic  6.34 us (5%)
  matrix products  4.66 us (4%)
    ppermute x6, waiting for transfers between devices, padded_2(): after = lax.ppermute(leading, axis, down)  32.9 us
    ppermute x6, starting transfers between devices, padded_2(): before = lax.ppermute(last, axis, up)  28.2 us
    gather x4, local copies, waits for them, and re-layouts, fetch(): jnp.take(flat_source, (base_index + step_size).reshape(-1), axis=1, mode=...  26.6 us
    ppermute x6, starting transfers between devices, padded_2(): after = lax.ppermute(leading, axis, down)  17.4 us
    dot_general x17, matrix products, convolve(): jnp.dot(weights[tap_index], window, preferred_element_type=jnp.float32)  4.33 us
    concatenate x6, other arithmetic, padded_2(): shard = jnp.concatenate([before, shard, after], axis=dim)  3.12 us
    ppermute x1, starting transfers between devices, swapped(): return lax.ppermute(value, axis, pairs)  3.12 us
    unnamed x27, local copies, waits for them, and re-layouts  2.8 us
  transfers between devices with their start and end apart: 13, of which 6 were waited for; matrix products, arithmetic and copies ran while one was open for 3% of the time, Pallas kernels for 0%

commit v1 on v0

v1 whole, which is shorter than its diff:
```python
import functools

import jax
import jax.numpy as jnp
from jax import lax
from jax.experimental import pallas as pl
from jax.experimental.pallas import tpu as pltpu
from jax.sharding import PartitionSpec as P

MAXS = 8
BLK = 8
CH = 64
HALO = MAXS + 1
LANES = 128
RING = 2 * LANES
PITCH = 2 * HALO
GROUPS = ((0, 7), (7, 9), (9, 16))
frac_scale = 256.0


def lane_iota(shape):
    return lax.broadcasted_iota(jnp.int32, shape, len(shape) - 1)


def pack_kernel(feat_ref, tile_ref, edge_ref, rows_ref):
    channels, height, lanes = feat_ref.shape
    for ch in range(channels):
        rows_ref[pl.ds(ch * height, height), :] = feat_ref[ch].astype(jnp.float32)
    lane = lane_iota((channels, lanes))
    for group, (first, last) in enumerate(GROUPS):
        packed = jnp.zeros((channels, lanes), jnp.float32)
        for row in range(first, last):
            value = rows_ref[pl.ds(row, channels, stride=height), :]
            tile_ref[row] = value.astype(jnp.bfloat16)
            at = PITCH * (row - first)
            turned = pltpu.roll(value, (at + HALO) % lanes, 1)
            packed = jnp.where((lane >= at) & (lane < at + PITCH), turned, packed)
        edge_ref[group] = packed.astype(jnp.bfloat16)


def band_kernel(tile_ref, edge_ref, above_ref, below_ref, band_ref, send_ref):
    height, channels, lanes = tile_ref.shape
    lane = lane_iota((channels, lanes))
    reach = 2
    row_of = []
    for row in range(-HALO, height + HALO):
        if row < 0:
            ref, center, part = above_ref, row + HALO, row + height
            base, groups = HALO, (1, 2)
        elif row < height:
            ref, center, part = tile_ref, row, row
            base, groups = 0, (0, 1, 2)
        else:
            ref, center, part = below_ref, row - height, row - height
            base, groups = HALO, (0, 1)
        group = next(g for g in groups if GROUPS[g][0] <= part < GROUPS[g][1])
        source = edge_ref if ref is tile_ref else ref
        row_of.append((row, ref, center, source, base + groups.index(group), part - GROUPS[group][0]))
    packed = jnp.zeros((channels, lanes), jnp.float32)
    for index, (row, ref, center, source, slot, place) in enumerate(row_of):
        block = pl.ds(index * channels, channels)
        band_ref[block, :lanes] = ref[center]
        at = PITCH * place + HALO
        border = pltpu.roll(source[slot].astype(jnp.float32), (-at) % lanes, 1)
        band_ref[block, lanes:] = border.astype(jnp.bfloat16)
        if -reach <= row < height + reach:
            send_ref[row + reach] = ref[center]
            at = 2 * reach * (row + reach)
            turned = pltpu.roll(border, (at + reach) % lanes, 1)
            packed = jnp.where((lane >= at) & (lane < at + 2 * reach), turned, packed)
    send_ref[height + 2 * reach] = packed.astype(jnp.bfloat16)


def shifted_sum(stacked):
    count = stacked.shape[0] // 3
    left = pltpu.roll(stacked[:count], 1, 1)
    right = pltpu.roll(stacked[2 * count :], RING - 1, 1)
    return left + stacked[count : 2 * count] + right


def main_kernel(
    edges_ref, band_ref, other_ref, own_w_ref, other_w_ref, second_w_ref, head_ref, base_ref, cover_ref,
    warped_ref, motion_ref, window_ref, hidden_ref, residual_ref, rows_ref,
):
    channels, height, lanes = warped_ref.shape
    reach = 2
    window = height + 2 * reach
    border_pack = other_ref[window].astype(jnp.float32)
    for index in range(window):
        block = pl.ds(index * channels, channels)
        window_ref[block, :lanes] = other_ref[index]
        at = 2 * reach * index + reach
        window_ref[block, lanes:] = pltpu.roll(border_pack, (-at) % lanes, 1).astype(jnp.bfloat16)

    lane = lane_iota((1, RING))
    outside = ((edges_ref[2] != 0) & (lane == RING - 1)) | ((edges_ref[3] != 0) & (lane == lanes))
    inside = jnp.where(outside, 0.0, 1.0)
    for row in range(-1, height + 1):
        own = band_ref[pl.ds((row - 1 + HALO) * channels, 3 * channels), :]
        other = window_ref[pl.ds((row - 1 + reach) * channels, 3 * channels), :]
        total = jnp.dot(own_w_ref[...], own, preferred_element_type=jnp.float32)
        total = total + jnp.dot(other_w_ref[...], other, preferred_element_type=jnp.float32)
        keep = inside
        if row == -1:
            keep = jnp.where(edges_ref[0] != 0, 0.0, inside)
        elif row == height:
            keep = jnp.where(edges_ref[1] != 0, 0.0, inside)
        value = jnp.maximum(shifted_sum(total), 0.0) * keep
        hidden_ref[pl.ds((row + 1) * channels, channels), :] = value.astype(jnp.bfloat16)

    for row in range(height):
        taken = hidden_ref[pl.ds(row * channels, 3 * channels), :]
        total = jnp.dot(second_w_ref[...], taken, preferred_element_type=jnp.float32)
        value = jnp.maximum(shifted_sum(total)[:, :lanes], 0.0).astype(jnp.bfloat16)
        pair = jnp.dot(head_ref[...], value, preferred_element_type=jnp.float32)
        for k in range(2):
            residual_ref[k, pl.ds(row, 1), :] = pair[k : k + 1]

    motion = base_ref[...] + cover_ref[...][None] * jnp.tanh(residual_ref[...])
    motion_ref[...] = motion

    at = lax.broadcasted_iota(jnp.int32, (RING, RING), 0)
    column = jnp.where(at < RING - LANES // 2, at, at - RING).astype(jnp.float32)
    grid = (lane & (lanes - 1)).astype(jnp.float32)
    for row in range(0, height, 2):
        move = [jnp.concatenate([motion_ref[k, row : row + 1, :], motion_ref[k, row + 1 : row + 2, :]], axis=1) for k in range(2)]
        place_col = grid + move[1]
        hat = jnp.maximum(1.0 - jnp.abs(place_col - column), 0.0).astype(jnp.bfloat16)
        span = 2 * HALO + 2
        mixed = jnp.dot(band_ref[pl.ds(row * channels, span * channels), :], hat, preferred_element_type=jnp.float32)
        place_row = jnp.where(lane < lanes, 0.0, 1.0) + move[0]
        total = None
        for step in range(span):
            weight = jnp.maximum(1.0 - jnp.abs(place_row - (step - HALO)), 0.0)
            term = weight * mixed[step * channels : (step + 1) * channels]
            total = term if total is None else total + term
        rows_ref[pl.ds(row * channels, channels), :] = total[:, :lanes]
        rows_ref[pl.ds((row + 1) * channels, channels), :] = total[:, lanes:]
    for ch in range(channels):
        warped_ref[ch] = rows_ref[pl.ds(ch, height, stride=channels), :].astype(jnp.bfloat16)


VMEM = pl.BlockSpec(memory_space=pltpu.VMEM)
SMEM = pl.BlockSpec(memory_space=pltpu.SMEM)


def call(body, outputs, scratch, *operands, scalars=0, flops=0):
    moved = sum(x.size * x.dtype.itemsize for x in (*operands, *outputs))
    return pl.pallas_call(
        body,
        out_shape=outputs,
        in_specs=[SMEM] * scalars + [VMEM] * (len(operands) - scalars),
        out_specs=[VMEM] * len(outputs),
        scratch_shapes=scratch,
        compiler_params=pltpu.CompilerParams(vmem_limit_bytes=40 * 2**20),
        cost_estimate=pl.CostEstimate(flops=flops, bytes_accessed=moved, transcendentals=0),
    )(*operands)


def of(shape, dtype=jnp.bfloat16):
    return jax.ShapeDtypeStruct(shape, dtype)


def taps(weights):
    outputs, inputs = weights.shape[1:]
    cube = weights.reshape(3, 3, outputs, inputs).transpose(1, 2, 0, 3)
    return cube.reshape(3 * outputs, 3 * inputs)


def ring(value, axis, step):
    peers = lax.axis_size(axis)
    return lax.ppermute(value, axis, [(i, (i + step) % peers) for i in range(peers)])


def chain(value, axis, step):
    peers = lax.axis_size(axis)
    return lax.ppermute(value, axis, [(i, i + step) for i in range(peers) if 0 <= i + step < peers])


def shards(features, offsets, fractions, tissue, w_first, w_second, head_weight):
    _, channels, height, columns = features.shape
    f32, bf16 = jnp.float32, jnp.bfloat16
    row, col = lax.axis_index("row"), lax.axis_index("col")
    rows, cols = lax.axis_size("row"), lax.axis_size("col")
    edges = jnp.stack([row == 0, row == rows - 1, col == 0, col == cols - 1]).astype(jnp.int32)

    tile, edge = call(
        pack_kernel,
        [of((height, channels, columns)), of((3, channels, columns))],
        [pltpu.VMEM((height * channels, columns), f32)],
        features[0],
    )
    from_left = ring(edge, "col", 1)
    from_right = ring(edge, "col", -1)
    place = jnp.arange(columns) % PITCH
    is_left = place < HALO
    joined = jnp.where(
        is_left,
        jnp.where(col == 0, jnp.zeros_like(from_left), from_left),
        jnp.where(col == cols - 1, jnp.zeros_like(from_right), from_right),
    )
    above = chain(jnp.concatenate([tile[height - HALO :], joined[1:]]), "row", 1)
    below = chain(jnp.concatenate([tile[:HALO], joined[:2]]), "row", -1)
    band_rows = height + 2 * HALO
    band, send = call(
        band_kernel,
        [of((band_rows * channels, RING)), of((height + 5, channels, columns))],
        [],
        tile, joined, above, below,
    )
    other = lax.ppermute(send, "pair", [(0, 1), (1, 0)])

    coverage = jnp.repeat(jnp.repeat(tissue[0], BLK, axis=0), BLK, axis=1).astype(f32)
    base = offsets[0].astype(f32) + fractions[0].astype(f32) / frac_scale
    head = jnp.concatenate([head_weight, jnp.zeros((6, channels), bf16)])
    warped, motion = call(
        main_kernel,
        [of((channels, height, columns)), of((2, height, columns), f32)],
        [
            pltpu.VMEM(((height + 4) * channels, RING), bf16),
            pltpu.VMEM(((height + 2) * channels, RING), bf16),
            pltpu.VMEM((2, height, columns), f32),
            pltpu.VMEM((height * channels, columns), f32),
        ],
        edges, band, other, taps(w_first[:, :, :channels]), taps(w_first[:, :, channels:]), taps(w_second),
        head, base, coverage,
        scalars=1,
    )
    return (warped[None], motion[None])


def solution(mesh):
    return jax.shard_map(
        shards,
        mesh=mesh,
        in_specs=(
            P("pair", None, "row", "col"),
            P("pair", None, "row", "col"),
            P("pair", None, "row", "col"),
            P("pair", "row", "col"),
            P(),
            P(),
            P(),
        ),
        out_specs=(P("pair", None, "row", "col"), P("pair", None, "row", "col")),
        check_vma=False,
    )
```

time: 133 us -> 50.8 us (0.38)
  the two profiles are of different devices: /device:TPU:217 before, /device:TPU:30 now
where the time goes in v1:
time: 50.8 us; the launch traced here: 50.6 us
  waiting for transfers between devices  19 us (37%)
  starting transfers between devices  18 us (35%)
  Pallas kernels  9.82 us (19%)
  local copies, waits for them, and re-layouts  2.15 us (4%)
  other arithmetic  0.83 us (2%)
  between operations  0.82 us (2%)
    pallas_call x3, Pallas kernels, call(): pl.pallas_call(body, out_shape=outputs, in_specs=[SMEM] * scalars + [VMEM...  9.82 us
    ppermute x2, waiting for transfers between devices, chain(): lax.ppermute(value, axis, [(i, i + step) for i in range(peers) if 0 <= i...  8.93 us
    ppermute x2, starting transfers between devices, ring(): lax.ppermute(value, axis, [(i, (i + step) % peers) for i in range(peers)])  8.49 us
    ppermute x2, starting transfers between devices, chain(): lax.ppermute(value, axis, [(i, i + step) for i in range(peers) if 0 <= i...  7.46 us
    ppermute x1, waiting for transfers between devices, shards(): other = lax.ppermute(send, 'pair', [(0, 1), (1, 0)])  6.11 us
    ppermute x2, waiting for transfers between devices, ring(): lax.ppermute(value, axis, [(i, (i + step) % peers) for i in range(peers)])  3.91 us
    ppermute x1, starting transfers between devices, shards(): other = lax.ppermute(send, 'pair', [(0, 1), (1, 0)])  2.05 us
  transfers between devices with their start and end apart: 5, of which 5 were waited for; matrix products, arithmetic and copies ran while one was open for 4% of the time, Pallas kernels for 0%

profile of v1, /device:TPU:30, one launch (start us, length us, event | category | flops | bytes accessed | tf_op | source)
XLA Modules:
  0.0 50.6 jit_solution(6969466024241590465)
XLA Ops:
  0.6 0.0 copy-start
  0.6 0.9 %copy-done = bf16[1,64,16,128]{3,2,1,0:T(8,128)(2,1)S(1)} copy-done((bf16[1,64,16,128]{3,2,1,0:T(8,128)(2,1)S(1)}, bf16[1,64,16,128]{3,2,1,0:T(8,128)(2,1)}, u32[]{:S(2)}) %copy-start) | copy-done | bytes 262168
  1.6 0.0 copy-start.1
  1.6 0.3 shard_map.86
  1.8 8.5 %collective-permute-start.1 = (bf16[3,64,128]{2,1,0:T(8,128)(2,1)S(1)}, bf16[3,64,128]{2,1,0:T(8,128)(2,1)S(1)}, u32[]{:S(2)}, u32[]{:S(2)}) collective-permute-start(bf16[3,64,128]{2,1,0:T(8,128)(2,1)S(1)} %get-tuple-element.9), channel_id=1, source_target_pairs={{0,15},{1,0},{2,1},{3,2},{4,3},{5,4},{6,5},{7,6},{8,7},{9,8},{10,9... | collective-permute-start | bytes 147464 | tf_op jit(solution)/shard_map/ppermute | solution.py:172
  10.3 0.0 collective-permute-start
  10.4 0.7 %convert_bitcast_fusion = f32[2,16]{1,0:T(2,128)S(1)} fusion(s32[1,2,16]{2,1,0:T(2,128)} %param.10), kind=kLoop, calls=%fused_computation.11 | loop fusion | flops 32 | bytes 256 | tf_op jit(solution)/shard_map/convert_element_type | solution.py:213
  11.1 0.1 copy.20
  11.1 0.9 %collective-permute-done.1 = bf16[3,64,128]{2,1,0:T(8,128)(2,1)S(1)} collective-permute-done((bf16[3,64,128]{2,1,0:T(8,128)(2,1)S(1)}, bf16[3,64,128]{2,1,0:T(8,128)(2,1)S(1)}, u32[]{:S(2)}, u32[]{:S(2)}) %collective-permute-start.1) | collective-permute-done | bytes 49184 | tf_op jit(solution)/shard_map/ppermute | solution.py:172
  12.1 3.0 %collective-permute-done = bf16[3,64,128]{2,1,0:T(8,128)(2,1)S(1)} collective-permute-done((bf16[3,64,128]{2,1,0:T(8,128)(2,1)S(1)}, bf16[3,64,128]{2,1,0:T(8,128)(2,1)S(1)}, u32[]{:S(2)}, u32[]{:S(2)}) %collective-permute-start) | collective-permute-done | bytes 49184 | tf_op jit(solution)/shard_map/ppermute | solution.py:172
  15.1 5.5 %collective-permute-start.2 = (bf16[11,64,128]{2,1,0:T(8,128)(2,1)S(1)}, bf16[11,64,128]{2,1,0:T(8,128)(2,1)S(1)}, u32[]{:S(2)}, u32[]{:S(2)}) collective-permute-start(bf16[11,64,128]{2,1,0:T(8,128)(2,1)S(1)} %pad_maximum_fusion), channel_id=1, source_target_pairs={{0,16},{16,32},{32,48},{48,64},{64,80},{80,96},{96,112},{112,128},... | collective-permute-start | bytes 540680 | tf_op jit(solution)/shard_map/ppermute | solution.py:177
  20.7 1.9 %collective-permute-start.3 = (bf16[11,64,128]{2,1,0:T(8,128)(2,1)S(1)}, bf16[11,64,128]{2,1,0:T(8,128)(2,1)S(1)}, u32[]{:S(2)}, u32[]{:S(2)}) collective-permute-start(bf16[11,64,128]{2,1,0:T(8,128)(2,1)S(1)} %pad_maximum_fusion.1), channel_id=1, source_target_pairs={{16,0},{32,16},{48,32},{64,48},{80,64},{96,80},{112,96},{128,112},... | collective-permute-start | bytes 540680 | tf_op jit(solution)/shard_map/ppermute | solution.py:177
  22.6 0.0 copy-done.1
  22.6 0.1 fusion.2
  22.8 0.0 copy-start.2
  22.8 1.2 %collective-permute-done.2.above_ref = bf16[11,64,128]{2,1,0:T(8,128)(2,1)S(1)} collective-permute-done((bf16[11,64,128]{2,1,0:T(8,128)(2,1)S(1)}, bf16[11,64,128]{2,1,0:T(8,128)(2,1)S(1)}, u32[]{:S(2)}, u32[]{:S(2)}) %collective-permute-start.2) | collective-permute-done | bytes 180256 | tf_op jit(solution)/shard_map/ppermute | solution.py:177
  24.0 7.7 %collective-permute-done.3.below_ref = bf16[11,64,128]{2,1,0:T(8,128)(2,1)S(1)} collective-permute-done((bf16[11,64,128]{2,1,0:T(8,128)(2,1)S(1)}, bf16[11,64,128]{2,1,0:T(8,128)(2,1)S(1)}, u32[]{:S(2)}, u32[]{:S(2)}) %collective-permute-start.3) | collective-permute-done | bytes 180256 | tf_op jit(solution)/shard_map/ppermute | solution.py:177
  31.7 1.3 %shard_map.87 = (bf16[2176,256]{1,0:T(8,128)(2,1)S(1)}, bf16[21,64,128]{2,1,0:T(8,128)(2,1)S(1)}) custom-call(bf16[16,64,128]{2,1,0:T(8,128)(2,1)S(1)} %get-tuple-element.8.tile_ref, bf16[3,64,128]{2,1,0:T(8,128)(2,1)S(1)} %select_select_fusion.edge_ref, bf16[11,64,128]{2,1,0:T(8,128)(2,1)S(1)} %collective-permute-done.2.above_ref, ...), custom_call_target="tpu_custom_call" | custom-call | bytes 2129920 | tf_op jit(solution)/shard_map/pallas_call | solution.py:149
  33.0 0.0 copy-start.5
  33.0 0.0 copy-start.3
  33.0 0.0 copy-start.4
  33.0 2.1 %collective-permute-start.4 = (bf16[21,64,128]{2,1,0:T(8,128)(2,1)S(1)}, bf16[21,64,128]{2,1,0:T(8,128)(2,1)S(1)}, u32[]{:S(2)}, u32[]{:S(2)}) collective-permute-start(bf16[21,64,128]{2,1,0:T(8,128)(2,1)S(1)} %get-tuple-element.11), channel_id=1, source_target_pairs={{0,256},{256,0},{1,257},{257,1},{2,258},{258,2},{3,259},{259,3},{4... | collective-permute-start | bytes 1032200 | tf_op jit(solution)/shard_map/ppermute | solution.py:211
  35.1 0.1 copy.27
  35.2 0.2 reshape.33.own_w_ref
  35.4 0.1 copy.26
  35.5 0.2 reshape.35.other_w_ref
  35.7 0.0 copy-done.2
  35.7 0.1 copy.25
  35.9 0.2 reshape.37.second_w_ref
  36.1 0.0 copy-done.5
  36.1 0.1 add_convert_fusion.edges_ref
  36.2 0.0 copy-done.3
  36.2 0.0 copy-done.4
  36.2 6.1 %collective-permute-done.4.other_ref = bf16[21,64,128]{2,1,0:T(8,128)(2,1)S(1)} collective-permute-done((bf16[21,64,128]{2,1,0:T(8,128)(2,1)S(1)}, bf16[21,64,128]{2,1,0:T(8,128)(2,1)S(1)}, u32[]{:S(2)}, u32[]{:S(2)}) %collective-permute-start.4) | collective-permute-done | bytes 344096 | tf_op jit(solution)/shard_map/ppermute | solution.py:211
  42.3 8.3 %shard_map.88 = (bf16[64,16,128]{2,1,0:T(8,128)(2,1)}, f32[2,16,128]{2,1,0:T(8,128)}) custom-call(s32[4]{0:T(128)S(1)} %add_convert_fusion.edges_ref, bf16[2176,256]{1,0:T(8,128)(2,1)S(1)} %get-tuple-element.10.band_ref, bf16[21,64,128]{2,1,0:T(8,128)(2,1)S(1)} %collective-permute-done.4.other_ref, bf16[192,192]{1,0:T(8,128)(2,1)S(1)} %reshape.33.own_w_ref, ...), custom_call_target="tpu_custom_call" | custom-call | bytes 1983504 | tf_op jit(solution)/shard_map/pallas_call | solution.py:149
  (11 shorter events, 0.2 us)
Async XLA Ops:
  0.6 1.0 %copy-start = (bf16[1,64,16,128]{3,2,1,0:T(8,128)(2,1)S(1)}, bf16[1,64,16,128]{3,2,1,0:T(8,128)(2,1)}, u32[]{:S(2)}) copy-start(bf16[1,64,16,128]{3,2,1,0:T(8,128)(2,1)} %param.7) | copy-start | bytes 786436
  1.6 21.0 %copy-start.1 = (bf16[9,64,128]{2,1,0:T(8,128)(2,1)S(1)}, bf16[9,64,128]{2,1,0:T(8,128)(2,1)}, u32[]{:S(2)}) copy-start(bf16[9,64,128]{2,1,0:T(8,128)(2,1)} %param.11) | copy-start | bytes 442372
  1.8 10.2 %collective-permute-start.1 = (bf16[3,64,128]{2,1,0:T(8,128)(2,1)S(1)}, bf16[3,64,128]{2,1,0:T(8,128)(2,1)S(1)}, u32[]{:S(2)}, u32[]{:S(2)}) collective-permute-start(bf16[3,64,128]{2,1,0:T(8,128)(2,1)S(1)} %get-tuple-element.9), channel_id=1, source_target_pairs={{0,15},{1,0},{2,1},{3,2},{4,3},{5,4},{6,5},{7,6},{8,7},{9,8},{10,9... | collective-permute-start | bytes 147464 | tf_op jit(solution)/shard_map/ppermute | solution.py:172
  10.3 4.7 %collective-permute-start = (bf16[3,64,128]{2,1,0:T(8,128)(2,1)S(1)}, bf16[3,64,128]{2,1,0:T(8,128)(2,1)S(1)}, u32[]{:S(2)}, u32[]{:S(2)}) collective-permute-start(bf16[3,64,128]{2,1,0:T(8,128)(2,1)S(1)} %get-tuple-element.9), channel_id=1, source_target_pairs={{0,1},{1,2},{2,3},{3,4},{4,5},{5,6},{6,7},{7,8},{8,9},{9,10},{10,1... | collective-permute-start | bytes 147464 | tf_op jit(solution)/shard_map/ppermute | solution.py:172
  15.1 8.9 %collective-permute-start.2 = (bf16[11,64,128]{2,1,0:T(8,128)(2,1)S(1)}, bf16[11,64,128]{2,1,0:T(8,128)(2,1)S(1)}, u32[]{:S(2)}, u32[]{:S(2)}) collective-permute-start(bf16[11,64,128]{2,1,0:T(8,128)(2,1)S(1)} %pad_maximum_fusion), channel_id=1, source_target_pairs={{0,16},{16,32},{32,48},{48,64},{64,80},{80,96},{96,112},{112,128},... | collective-permute-start | bytes 540680 | tf_op jit(solution)/shard_map/ppermute | solution.py:177
  20.7 11.0 %collective-permute-start.3 = (bf16[11,64,128]{2,1,0:T(8,128)(2,1)S(1)}, bf16[11,64,128]{2,1,0:T(8,128)(2,1)S(1)}, u32[]{:S(2)}, u32[]{:S(2)}) collective-permute-start(bf16[11,64,128]{2,1,0:T(8,128)(2,1)S(1)} %pad_maximum_fusion.1), channel_id=1, source_target_pairs={{16,0},{32,16},{48,32},{64,48},{80,64},{96,80},{112,96},{128,112},... | collective-permute-start | bytes 540680 | tf_op jit(solution)/shard_map/ppermute | solution.py:177
  22.8 13.0 %copy-start.2 = (bf16[9,64,64]{2,1,0:T(8,128)(2,1)S(1)}, bf16[9,64,64]{2,1,0:T(8,128)(2,1)}, u32[]{:S(2)}) copy-start(bf16[9,64,64]{2,1,0:T(8,128)(2,1)} %param.12) | copy-start | bytes 221188
  33.0 3.1 %copy-start.5 = (bf16[2,64]{1,0:T(2,128)(2,1)S(1)}, bf16[2,64]{1,0:T(2,128)(2,1)}, u32[]{:S(2)}) copy-start(bf16[2,64]{1,0:T(2,128)(2,1)} %param.13) | copy-start | bytes 772
  33.0 3.2 %copy-start.3 = (s32[1,2,16,128]{3,2,1,0:T(8,128)S(1)}, s32[1,2,16,128]{3,2,1,0:T(8,128)}, u32[]{:S(2)}) copy-start(s32[1,2,16,128]{3,2,1,0:T(8,128)} %param.9) | copy-start | bytes 49156
  33.0 3.2 %copy-start.4 = (s32[1,2,16,128]{3,2,1,0:T(8,128)S(1)}, s32[1,2,16,128]{3,2,1,0:T(8,128)}, u32[]{:S(2)}) copy-start(s32[1,2,16,128]{3,2,1,0:T(8,128)} %param.8) | copy-start | bytes 49156
  33.0 9.3 %collective-permute-start.4 = (bf16[21,64,128]{2,1,0:T(8,128)(2,1)S(1)}, bf16[21,64,128]{2,1,0:T(8,128)(2,1)S(1)}, u32[]{:S(2)}, u32[]{:S(2)}) collective-permute-start(bf16[21,64,128]{2,1,0:T(8,128)(2,1)S(1)} %get-tuple-element.11), channel_id=1, source_target_pairs={{0,256},{256,0},{1,257},{257,1},{2,258},{258,2},{3,259},{259,3},{4... | collective-permute-start | bytes 1032200 | tf_op jit(solution)/shard_map/ppermute | solution.py:211

commit v2 on v1

v2 whole, which is shorter than its diff:
```python
import functools

import jax
import jax.numpy as jnp
from jax import lax
from jax.experimental import pallas as pl
from jax.experimental.pallas import tpu as pltpu
from jax.sharding import PartitionSpec as P

MAXS = 8
BLK = 8
CH = 64
HALO = MAXS + 1
LANES = 128
RING = 2 * LANES
PITCH = 2 * HALO
GROUPS = ((0, 7), (7, 9), (9, 16))
frac_scale = 256.0


def lane_iota(shape):
    return lax.broadcasted_iota(jnp.int32, shape, len(shape) - 1)


def packed_edge(value, slot):
    return pltpu.roll(value, (PITCH * slot + HALO) % LANES, 1)


def in_slot(lane, slot):
    return (lane >= PITCH * slot) & (lane < PITCH * (slot + 1))


def border_of(vector, slot):
    return pltpu.roll(vector, (-PITCH * slot - HALO) % LANES, 1)


def own_pack_kernel(feat_ref, tile_ref, edge_ref, rows_ref):
    channels, height, lanes = feat_ref.shape
    for ch in range(channels):
        rows_ref[pl.ds(ch * height, height), :] = feat_ref[ch].astype(jnp.float32)
    lane = lane_iota((channels, lanes))
    for group, (first, last) in enumerate(GROUPS):
        packed = jnp.zeros((channels, lanes), jnp.float32)
        for row in range(first, last):
            value = rows_ref[pl.ds(row, channels, stride=height), :]
            tile_ref[row] = value.astype(jnp.bfloat16)
            packed = jnp.where(in_slot(lane, row - first), packed_edge(value, row - first), packed)
        edge_ref[group] = packed.astype(jnp.bfloat16)


def other_pack_kernel(feat_ref, own_tile_ref, own_edge_ref, tile_ref, edge_ref, rows_ref):
    channels, height, lanes = feat_ref.shape
    edge_ref[: len(GROUPS)] = own_edge_ref[...]
    own_pack_kernel(feat_ref, tile_ref, edge_ref.at[pl.ds(len(GROUPS), len(GROUPS))], rows_ref)
    lane = lane_iota((channels, lanes))
    packed = edge_ref[len(GROUPS) + 1].astype(jnp.float32)
    for slot, row in enumerate((0, 1, height - 2, height - 1), 2):
        value = own_tile_ref[row].astype(jnp.float32)
        packed = jnp.where(in_slot(lane, slot), packed_edge(value, slot), packed)
    edge_ref[len(GROUPS) + 1] = packed.astype(jnp.bfloat16)


def lay(target_ref, index, center, vector, slot):
    channels, lanes = center.shape
    block = pl.ds(index * channels, channels)
    target_ref[block, :lanes] = center
    target_ref[block, lanes:] = border_of(vector, slot).astype(jnp.bfloat16)


def hidden_row(own, other, own_w_ref, other_w_ref, keep):
    total = jnp.dot(own_w_ref[...], own, preferred_element_type=jnp.float32)
    total = total + jnp.dot(other_w_ref[...], other, preferred_element_type=jnp.float32)
    return (jnp.maximum(shifted_sum(total), 0.0) * keep).astype(jnp.bfloat16)


def residual_row(taken, second_w_ref, head_ref):
    total = jnp.dot(second_w_ref[...], taken, preferred_element_type=jnp.float32)
    value = jnp.maximum(shifted_sum(total)[:, :LANES], 0.0).astype(jnp.bfloat16)
    return jnp.dot(head_ref[...], value, preferred_element_type=jnp.float32)


def inside_columns(edges_ref):
    lane = lane_iota((1, RING))
    outside = ((edges_ref[2] != 0) & (lane == RING - 1)) | ((edges_ref[3] != 0) & (lane == LANES))
    return jnp.where(outside, 0.0, 1.0)


def middle_kernel(
    edges_ref, own_tile_ref, other_tile_ref, joined_ref, own_w_ref, other_w_ref, second_w_ref, head_ref,
    band_ref, window_ref, near_ref, residual_ref, hidden_ref,
):
    height, channels, lanes = own_tile_ref.shape
    for part, (tile_ref, target_ref) in enumerate(((own_tile_ref, band_ref), (other_tile_ref, window_ref))):
        for group, (first, last) in enumerate(GROUPS):
            vector = joined_ref[part * len(GROUPS) + group].astype(jnp.float32)
            for row in range(first, last):
                lay(target_ref, row, tile_ref[row], vector, row - first)
    keep = inside_columns(edges_ref)
    for row in range(1, height - 1):
        block = pl.ds((row - 1) * channels, 3 * channels)
        value = hidden_row(band_ref[block, :], window_ref[block, :], own_w_ref, other_w_ref, keep)
        hidden_ref[pl.ds((row - 1) * channels, channels), :] = value
    near_ref[: 2 * channels] = hidden_ref[: 2 * channels]
    near_ref[2 * channels :] = hidden_ref[(height - 4) * channels :]
    for row in range(2, height - 2):
        pair = residual_row(hidden_ref[pl.ds((row - 2) * channels, 3 * channels), :], second_w_ref, head_ref)
        for k in range(2):
            residual_ref[k, pl.ds(row, 1), :] = pair[k : k + 1]
    for row in (0, 1, height - 2, height - 1):
        for k in range(2):
            residual_ref[k, pl.ds(row, 1), :] = jnp.zeros((1, lanes), jnp.float32)


def shifted_sum(stacked):
    count = stacked.shape[0] // 3
    left = pltpu.roll(stacked[:count], 1, 1)
    right = pltpu.roll(stacked[2 * count :], RING - 1, 1)
    return left + stacked[count : 2 * count] + right


def last_kernel(
    edges_ref, inner_ref, window_ref, near_ref, part_ref, above_ref, below_ref,
    own_w_ref, other_w_ref, second_w_ref, head_ref, base_ref, cover_ref,
    warped_ref, motion_ref, band_ref, side_ref, hidden_ref, residual_ref, rows_ref,
):
    channels, height, lanes = warped_ref.shape
    start, stop = HALO * channels, (HALO + height) * channels
    band_ref[start:stop, :] = inner_ref[...]
    first, middle = (above_ref[HALO + 3].astype(jnp.float32), above_ref[HALO + 2].astype(jnp.float32))
    for index in range(HALO):
        lay(band_ref, index, above_ref[index], *((middle, index) if index < 2 else (first, index - 2)))
    lay(side_ref, 0, above_ref[HALO], middle, 4)
    lay(side_ref, 1, above_ref[HALO + 1], middle, 5)
    first, middle = (below_ref[HALO + 2].astype(jnp.float32), below_ref[HALO + 3].astype(jnp.float32))
    for index in range(HALO):
        lay(band_ref, HALO + height + index, below_ref[index], *((first, index) if index < 7 else (middle, index - 7)))
    lay(side_ref, 6, below_ref[HALO], middle, 2)
    lay(side_ref, 7, below_ref[HALO + 1], middle, 3)
    half = 2 * channels
    for side, at in ((0, 0), (4, height - 2)):
        side_ref[pl.ds((side + 2 if side == 0 else side) * channels, half), :] = window_ref[pl.ds(at * channels, half), :]
    hidden_ref[half : 2 * half, :] = near_ref[:half, :]
    hidden_ref[2 * half : 3 * half, :] = near_ref[half:, :]
    inside = inside_columns(edges_ref)
    for row, side, spot in ((-1, 0, 0), (0, 1, 1), (height - 1, 4, 6), (height, 5, 7)):
        own = band_ref[pl.ds((row - 1 + HALO) * channels, 3 * channels), :]
        other = side_ref[pl.ds(side * channels, 3 * channels), :]
        keep = inside
        if row == -1:
            keep = jnp.where(edges_ref[0] != 0, 0.0, inside)
        elif row == height:
            keep = jnp.where(edges_ref[1] != 0, 0.0, inside)
        hidden_ref[pl.ds(spot * channels, channels), :] = hidden_row(own, other, own_w_ref, other_w_ref, keep)
    residual_ref[...] = part_ref[...]
    for row, spot in ((0, 0), (1, 1), (height - 2, 4), (height - 1, 5)):
        pair = residual_row(hidden_ref[pl.ds(spot * channels, 3 * channels), :], second_w_ref, head_ref)
        for k in range(2):
            residual_ref[k, pl.ds(row, 1), :] = pair[k : k + 1]

    motion = base_ref[...] + cover_ref[...][None] * jnp.tanh(residual_ref[...])
    motion_ref[...] = motion
    lane = lane_iota((1, RING))

    at = lax.broadcasted_iota(jnp.int32, (RING, RING), 0)
    column = jnp.where(at < RING - LANES // 2, at, at - RING).astype(jnp.float32)
    grid = (lane & (lanes - 1)).astype(jnp.float32)
    for row in range(0, height, 2):
        move = [jnp.concatenate([motion_ref[k, row : row + 1, :], motion_ref[k, row + 1 : row + 2, :]], axis=1) for k in range(2)]
        place_col = grid + move[1]
        hat = jnp.maximum(1.0 - jnp.abs(place_col - column), 0.0).astype(jnp.bfloat16)
        span = 2 * HALO + 2
        mixed = jnp.dot(band_ref[pl.ds(row * channels, span * channels), :], hat, preferred_element_type=jnp.float32)
        place_row = jnp.where(lane < lanes, 0.0, 1.0) + move[0]
        total = None
        for step in range(span):
            weight = jnp.maximum(1.0 - jnp.abs(place_row - (step - HALO)), 0.0)
            term = weight * mixed[step * channels : (step + 1) * channels]
            total = term if total is None else total + term
        rows_ref[pl.ds(row * channels, channels), :] = total[:, :lanes]
        rows_ref[pl.ds((row + 1) * channels, channels), :] = total[:, lanes:]
    for ch in range(channels):
        warped_ref[ch] = rows_ref[pl.ds(ch, height, stride=channels), :].astype(jnp.bfloat16)


VMEM = pl.BlockSpec(memory_space=pltpu.VMEM)
SMEM = pl.BlockSpec(memory_space=pltpu.SMEM)


def call(body, outputs, scratch, *operands, scalars=0, flops=0):
    moved = sum(x.size * x.dtype.itemsize for x in (*operands, *outputs))
    return pl.pallas_call(
        body,
        out_shape=outputs,
        in_specs=[SMEM] * scalars + [VMEM] * (len(operands) - scalars),
        out_specs=[VMEM] * len(outputs),
        scratch_shapes=scratch,
        compiler_params=pltpu.CompilerParams(vmem_limit_bytes=40 * 2**20),
        cost_estimate=pl.CostEstimate(flops=flops, bytes_accessed=moved, transcendentals=0),
    )(*operands)


def of(shape, dtype=jnp.bfloat16):
    return jax.ShapeDtypeStruct(shape, dtype)


def taps(weights):
    outputs, inputs = weights.shape[1:]
    cube = weights.reshape(3, 3, outputs, inputs).transpose(1, 2, 0, 3)
    return cube.reshape(3 * outputs, 3 * inputs)


def ring(value, axis, step):
    peers = lax.axis_size(axis)
    return lax.ppermute(value, axis, [(i, (i + step) % peers) for i in range(peers)])


def across(value, step):
    rows, cols = lax.axis_size("row"), lax.axis_size("col")
    place = lambda pair, row, col: (pair * rows + row) * cols + col
    pairs = [
        (place(pair, row, col), place(1 - pair, row + step, col))
        for pair in range(2)
        for row in range(rows)
        if 0 <= row + step < rows
        for col in range(cols)
    ]
    return lax.ppermute(value, ("pair", "row", "col"), pairs)


def shards(features, offsets, fractions, tissue, w_first, w_second, head_weight):
    _, channels, height, columns = features.shape
    f32, bf16 = jnp.float32, jnp.bfloat16
    row, col = lax.axis_index("row"), lax.axis_index("col")
    rows, cols = lax.axis_size("row"), lax.axis_size("col")
    edges = jnp.stack([row == 0, row == rows - 1, col == 0, col == cols - 1]).astype(jnp.int32)

    partner = lax.ppermute(features[0], "pair", [(0, 1), (1, 0)])
    tile_shape = (height, channels, columns)
    scratch = [pltpu.VMEM((height * channels, columns), f32)]
    own_tile, own_edge = call(own_pack_kernel, [of(tile_shape), of((3, channels, columns))], scratch, features[0])
    other_tile, edge = call(
        other_pack_kernel, [of(tile_shape), of((6, channels, columns))], scratch, partner, own_tile, own_edge
    )
    from_left = ring(edge, "col", 1)
    from_right = ring(edge, "col", -1)
    is_left = jnp.arange(columns) % PITCH < HALO
    joined = jnp.where(
        is_left,
        jnp.where(col == 0, jnp.zeros_like(from_left), from_left),
        jnp.where(col == cols - 1, jnp.zeros_like(from_right), from_right),
    )
    above = across(jnp.concatenate([other_tile[height - HALO :], own_tile[height - 2 :], joined[4:6]]), 1)
    below = across(jnp.concatenate([other_tile[:HALO], own_tile[:2], joined[3:5]]), -1)

    coverage = jnp.repeat(jnp.repeat(tissue[0], BLK, axis=0), BLK, axis=1).astype(f32)
    base = offsets[0].astype(f32) + fractions[0].astype(f32) / frac_scale
    weights = (
        taps(w_first[:, :, :channels]),
        taps(w_first[:, :, channels:]),
        taps(w_second),
        jnp.concatenate([head_weight, jnp.zeros((6, channels), bf16)]),
    )
    inner, window, near, part = call(
        middle_kernel,
        [
            of((height * channels, RING)),
            of((height * channels, RING)),
            of((4 * channels, RING)),
            of((2, height, columns), f32),
        ],
        [pltpu.VMEM(((height - 2) * channels, RING), bf16)],
        edges, own_tile, other_tile, joined, *weights,
        scalars=1, flops=3 * 10**9,
    )
    warped, motion = call(
        last_kernel,
        [of((channels, height, columns)), of((2, height, columns), f32)],
        [
            pltpu.VMEM(((height + 2 * HALO) * channels, RING), bf16),
            pltpu.VMEM((8 * channels, RING), bf16),
            pltpu.VMEM((8 * channels, RING), bf16),
            pltpu.VMEM((2, height, columns), f32),
            pltpu.VMEM((height * channels, columns), f32),
        ],
        edges, inner, window, near, part, above, below, *weights, base, coverage,
        scalars=1, flops=3 * 10**9,
    )
    return (warped[None], motion[None])


def solution(mesh):
    return jax.shard_map(
        shards,
        mesh=mesh,
        in_specs=(
            P("pair", None, "row", "col"),
            P("pair", None, "row", "col"),
            P("pair", None, "row", "col"),
            P("pair", "row", "col"),
            P(),
            P(),
            P(),
        ),
        out_specs=(P("pair", None, "row", "col"), P("pair", None, "row", "col")),
        check_vma=False,
    )
```

time: 50.8 us -> 44.6 us (0.88)
  waiting for transfers between devices: 19 us -> 12.1 us
  local copies, waits for them, and re-layouts: 2.15 us -> 4.27 us
  other arithmetic: 0.83 us -> 0.18 us
  starting transfers between devices: 18 us -> 17.4 us
    ppermute x3, waiting for transfers between devices: 15 us -> 6.92 us  [the longest x2 4.21 us: across(): return lax.ppermute(value, ('pair', 'row', 'col'), pairs)]
    ppermute x2, waiting for transfers between devices: 3.91 us -> 5.22 us  [ring(): lax.ppermute(value, axis, [(i, (i + step) % peers) for i in range(peers)])]
    unnamed x12, local copies, waits for them, and re-layouts: 0.97 us -> 2.08 us
    slice x1, local copies, waits for them, and re-layouts: 0.11 us -> 1.13 us  [shards(): w_first[:, :, channels:]]
    ppermute x2, starting transfers between devices: 8.49 us -> 7.62 us  [ring(): lax.ppermute(value, axis, [(i, (i + step) % peers) for i in range(peers)])]
    convert_element_type x1, other arithmetic: 0.69 us -> 0.01 us  [shards(): jnp.repeat(jnp.repeat(tissue[0], BLK, axis=0), BLK, axis=1).astype(f32)]
    pallas_call x3 -> x4, Pallas kernels: 9.82 us -> 9.47 us  [call(): pl.pallas_call(body, out_shape=outputs, in_specs=[SMEM] * scalars + [VMEM...]
  transfers between devices with their start and end apart: 5 -> 5, of which waited for: 5 -> 4; matrix products, arithmetic and copies ran while one was open for 4% -> 5% of each run, Pallas kernels for 0% -> 11%
where the time goes in v2:
time: 44.6 us; the launch traced here: 44.3 us
  starting transfers between devices  17.4 us (39%)
  waiting for transfers between devices  12.1 us (27%)
  Pallas kernels  9.47 us (21%)
  local copies, waits for them, and re-layouts  4.27 us (10%)
  between operations  0.8 us (2%)
    pallas_call x4, Pallas kernels, call(): pl.pallas_call(body, out_shape=outputs, in_specs=[SMEM] * scalars + [VMEM...  9.47 us
    ppermute x2, starting transfers between devices, ring(): lax.ppermute(value, axis, [(i, (i + step) % peers) for i in range(peers)])  7.62 us
    ppermute x2, starting transfers between devices, across(): return lax.ppermute(value, ('pair', 'row', 'col'), pairs)  7.05 us
    ppermute x2, waiting for transfers between devices, ring(): lax.ppermute(value, axis, [(i, (i + step) % peers) for i in range(peers)])  5.22 us
    ppermute x2, waiting for transfers between devices, across(): return lax.ppermute(value, ('pair', 'row', 'col'), pairs)  4.21 us
    ppermute x1, starting transfers between devices, shards(): partner = lax.ppermute(features[0], 'pair', [(0, 1), (1, 0)])  2.74 us
    ppermute x1, waiting for transfers between devices, shards(): partner = lax.ppermute(features[0], 'pair', [(0, 1), (1, 0)])  2.71 us
    unnamed x12, local copies, waits for them, and re-layouts  2.08 us
  transfers between devices with their start and end apart: 5, of which 4 were waited for; matrix products, arithmetic and copies ran while one was open for 5% of the time, Pallas kernels for 11%

profile of v2, /device:TPU:30, one launch (start us, length us, event | category | flops | bytes accessed | tf_op | source)
XLA Modules:
  0.0 44.3 jit_solution(1380064163779606351)
XLA Ops:
  0.6 2.7 %collective-permute-start = (bf16[64,16,128]{2,1,0:T(8,128)(2,1)}, bf16[64,16,128]{2,1,0:T(8,128)(2,1)S(1)}, u32[]{:S(2)}, u32[]{:S(2)}) collective-permute-start(bf16[64,16,128]{2,1,0:T(8,128)(2,1)} %bitcast.27), channel_id=1, source_target_pairs={{0,256},{256,0},{1,257},{257,1},{2,258},{258,2},{3,259},{259,3},{4... | collective-permute-start | bytes 786440 | tf_op jit(solution)/shard_map/ppermute | solution.py:237
  3.4 0.0 copy-start.4
  3.4 0.0 copy-start
  3.4 1.1 %fusion.3 = (bf16[9,64,64]{2,1,0:T(8,128)(2,1)S(1)}, bf16[9,64,64]{2,1,0:T(8,128)(2,1)S(1)}) fusion(bf16[9,64,128]{2,1,0:T(8,128)(2,1)} %param.11), kind=kLoop, calls=%fused_computation.15 | loop fusion | bytes 294912 | tf_op jit(solution)/shard_map/slice | solution.py:259
  4.6 0.0 copy-done.4
  4.6 0.1 copy.20
  4.7 0.0 copy-start.2
  4.7 0.0 copy-start.3
  4.7 0.7 %copy-done.2 = s32[1,2,16,128]{3,2,1,0:T(8,128)S(1)} copy-done((s32[1,2,16,128]{3,2,1,0:T(8,128)S(1)}, s32[1,2,16,128]{3,2,1,0:T(8,128)}, u32[]{:S(2)}) %copy-start.2) | copy-done | bytes 16408
  5.4 0.0 copy-done.3
  5.4 0.1 add_convert_fusion.edges_ref
  5.5 0.0 copy-done
  5.5 0.3 shard_map.86
  5.8 0.1 copy.27
  5.9 0.2 reshape.33.own_w_ref
  6.1 0.1 copy.26
  6.2 0.0 copy-start.1
  6.2 0.2 reshape.35.other_w_ref
  6.4 0.7 %copy-done.1 = bf16[9,64,64]{2,1,0:T(8,128)(2,1)S(1)} copy-done((bf16[9,64,64]{2,1,0:T(8,128)(2,1)S(1)}, bf16[9,64,64]{2,1,0:T(8,128)(2,1)}, u32[]{:S(2)}) %copy-start.1) | copy-done | bytes 73752
  7.1 0.1 copy.25
  7.2 0.2 reshape.37.second_w_ref
  7.4 0.0 copy-start.5
  7.4 0.1 copy.21.cover_ref
  7.5 0.6 %copy-done.5 = bf16[2,64]{1,0:T(2,128)(2,1)S(1)} copy-done((bf16[2,64]{1,0:T(2,128)(2,1)S(1)}, bf16[2,64]{1,0:T(2,128)(2,1)}, u32[]{:S(2)}) %copy-start.5) | copy-done | bytes 280
  8.1 2.7 %collective-permute-done.feat_ref = bf16[64,16,128]{2,1,0:T(8,128)(2,1)S(1)} collective-permute-done((bf16[64,16,128]{2,1,0:T(8,128)(2,1)}, bf16[64,16,128]{2,1,0:T(8,128)(2,1)S(1)}, u32[]{:S(2)}, u32[]{:S(2)}) %collective-permute-start) | collective-permute-done | bytes 262176 | tf_op jit(solution)/shard_map/ppermute | solution.py:237
  10.8 0.3 shard_map.87
  11.1 7.6 %collective-permute-start.2 = (bf16[6,64,128]{2,1,0:T(8,128)(2,1)S(1)}, bf16[6,64,128]{2,1,0:T(8,128)(2,1)S(1)}, u32[]{:S(2)}, u32[]{:S(2)}) collective-permute-start(bf16[6,64,128]{2,1,0:T(8,128)(2,1)S(1)} %get-tuple-element.15), channel_id=1, source_target_pairs={{0,15},{1,0},{2,1},{3,2},{4,3},{5,4},{6,5},{7,6},{8,7},{9,8},{10,9... | collective-permute-start | bytes 294920 | tf_op jit(solution)/shard_map/ppermute | solution.py:214
  18.7 0.0 collective-permute-start.1
  18.7 2.2 %collective-permute-done.2 = bf16[6,64,128]{2,1,0:T(8,128)(2,1)S(1)} collective-permute-done((bf16[6,64,128]{2,1,0:T(8,128)(2,1)S(1)}, bf16[6,64,128]{2,1,0:T(8,128)(2,1)S(1)}, u32[]{:S(2)}, u32[]{:S(2)}) %collective-permute-start.2) | collective-permute-done | bytes 98336 | tf_op jit(solution)/shard_map/ppermute | solution.py:214
  20.9 3.0 %collective-permute-done.1 = bf16[6,64,128]{2,1,0:T(8,128)(2,1)S(1)} collective-permute-done((bf16[6,64,128]{2,1,0:T(8,128)(2,1)S(1)}, bf16[6,64,128]{2,1,0:T(8,128)(2,1)S(1)}, u32[]{:S(2)}, u32[]{:S(2)}) %collective-permute-start.1) | collective-permute-done | bytes 98336 | tf_op jit(solution)/shard_map/ppermute | solution.py:214
  24.0 4.6 %collective-permute-start.3 = (bf16[13,64,128]{2,1,0:T(8,128)(2,1)S(1)}, bf16[13,64,128]{2,1,0:T(8,128)(2,1)S(1)}, u32[]{:S(2)}, u32[]{:S(2)}) collective-permute-start(bf16[13,64,128]{2,1,0:T(8,128)(2,1)S(1)} %pad_maximum_fusion), channel_id=1, source_target_pairs={{0,272},{1,273},{2,274},{3,275},{4,276},{5,277},{6,278},{7,279},{8... | collective-permute-start | bytes 638984 | tf_op jit(solution)/shard_map/ppermute | solution.py:227
  28.7 2.4 %collective-permute-start.4 = (bf16[13,64,128]{2,1,0:T(8,128)(2,1)S(1)}, bf16[13,64,128]{2,1,0:T(8,128)(2,1)S(1)}, u32[]{:S(2)}, u32[]{:S(2)}) collective-permute-start(bf16[13,64,128]{2,1,0:T(8,128)(2,1)S(1)} %pad_maximum_fusion.1), channel_id=1, source_target_pairs={{16,256},{17,257},{18,258},{19,259},{20,260},{21,261},{22,262},{23... | collective-permute-start | bytes 638984 | tf_op jit(solution)/shard_map/ppermute | solution.py:227
  31.1 4.4 %shard_map.88 = (bf16[1024,256]{1,0:T(8,128)(2,1)S(1)}, bf16[1024,256]{1,0:T(8,128)(2,1)S(1)}, bf16[256,256]{1,0:T(8,128)(2,1)S(1)}, f32[2,16,128]{2,1,0:T(8,128)S(1)}) custom-call(s32[4]{0:T(128)S(1)} %add_convert_fusion.edges_ref, bf16[16,64,128]{2,1,0:T(8,128)(2,1)S(1)} %get-tuple-element.12.own_tile_ref, ...), custom_call_target="tpu_custom_call" | custom-call | flops 3000000000 | bytes 2040848 | tf_op jit(solution)/shard_map/pallas_call | solution.py:191
  35.5 0.0 collective-permute-done.3.above_ref
  35.5 4.2 %collective-permute-done.4.below_ref = bf16[13,64,128]{2,1,0:T(8,128)(2,1)S(1)} collective-permute-done((bf16[13,64,128]{2,1,0:T(8,128)(2,1)S(1)}, bf16[13,64,128]{2,1,0:T(8,128)(2,1)S(1)}, u32[]{:S(2)}, u32[]{:S(2)}) %collective-permute-start.4) | collective-permute-done | bytes 213024 | tf_op jit(solution)/shard_map/ppermute | solution.py:227
  39.7 4.5 %shard_map.89 = (bf16[64,16,128]{2,1,0:T(8,128)(2,1)}, f32[2,16,128]{2,1,0:T(8,128)}) custom-call(s32[4]{0:T(128)S(1)} %add_convert_fusion.edges_ref, bf16[1024,256]{1,0:T(8,128)(2,1)S(1)} %get-tuple-element.16.inner_ref, bf16[1024,256]{1,0:T(8,128)(2,1)S(1)} %get-tuple-element.17.window_ref, bf16[256,256]{1,0:T(8,128)(2,1)S(1)} %get-tuple-element.18.near_ref, ...), custom_call_target="tpu_custom_call" | custom-call | flops 3000000000 | bytes 2147344 | tf_op jit(solution)/shard_map/pallas_call | solution.py:191
  (12 shorter events, 0.2 us)
Async XLA Ops:
  0.6 10.2 %collective-permute-start = (bf16[64,16,128]{2,1,0:T(8,128)(2,1)}, bf16[64,16,128]{2,1,0:T(8,128)(2,1)S(1)}, u32[]{:S(2)}, u32[]{:S(2)}) collective-permute-start(bf16[64,16,128]{2,1,0:T(8,128)(2,1)} %bitcast.27), channel_id=1, source_target_pairs={{0,256},{256,0},{1,257},{257,1},{2,258},{258,2},{3,259},{259,3},{4... | collective-permute-start | bytes 786440 | tf_op jit(solution)/shard_map/ppermute | solution.py:237
  3.4 1.2 %copy-start.4 = (s32[1,2,16]{2,1,0:T(2,128)S(1)}, s32[1,2,16]{2,1,0:T(2,128)}, u32[]{:S(2)}) copy-start(s32[1,2,16]{2,1,0:T(2,128)} %param.10) | copy-start | bytes 388
  3.4 2.1 %copy-start = (bf16[1,64,16,128]{3,2,1,0:T(8,128)(2,1)S(1)}, bf16[1,64,16,128]{3,2,1,0:T(8,128)(2,1)}, u32[]{:S(2)}) copy-start(bf16[1,64,16,128]{3,2,1,0:T(8,128)(2,1)} %param.7) | copy-start | bytes 786436
  4.7 0.7 %copy-start.2 = (s32[1,2,16,128]{3,2,1,0:T(8,128)S(1)}, s32[1,2,16,128]{3,2,1,0:T(8,128)}, u32[]{:S(2)}) copy-start(s32[1,2,16,128]{3,2,1,0:T(8,128)} %param.9) | copy-start | bytes 49156
  4.7 0.7 %copy-start.3 = (s32[1,2,16,128]{3,2,1,0:T(8,128)S(1)}, s32[1,2,16,128]{3,2,1,0:T(8,128)}, u32[]{:S(2)}) copy-start(s32[1,2,16,128]{3,2,1,0:T(8,128)} %param.8) | copy-start | bytes 49156
  6.2 0.9 %copy-start.1 = (bf16[9,64,64]{2,1,0:T(8,128)(2,1)S(1)}, bf16[9,64,64]{2,1,0:T(8,128)(2,1)}, u32[]{:S(2)}) copy-start(bf16[9,64,64]{2,1,0:T(8,128)(2,1)} %param.12) | copy-start | bytes 221188
  7.4 0.7 %copy-start.5 = (bf16[2,64]{1,0:T(2,128)(2,1)S(1)}, bf16[2,64]{1,0:T(2,128)(2,1)}, u32[]{:S(2)}) copy-start(bf16[2,64]{1,0:T(2,128)(2,1)} %param.13) | copy-start | bytes 772
  11.1 9.8 %collective-permute-start.2 = (bf16[6,64,128]{2,1,0:T(8,128)(2,1)S(1)}, bf16[6,64,128]{2,1,0:T(8,128)(2,1)S(1)}, u32[]{:S(2)}, u32[]{:S(2)}) collective-permute-start(bf16[6,64,128]{2,1,0:T(8,128)(2,1)S(1)} %get-tuple-element.15), channel_id=1, source_target_pairs={{0,15},{1,0},{2,1},{3,2},{4,3},{5,4},{6,5},{7,6},{8,7},{9,8},{10,9... | collective-permute-start | bytes 294920 | tf_op jit(solution)/shard_map/ppermute | solution.py:214
  18.7 5.3 %collective-permute-start.1 = (bf16[6,64,128]{2,1,0:T(8,128)(2,1)S(1)}, bf16[6,64,128]{2,1,0:T(8,128)(2,1)S(1)}, u32[]{:S(2)}, u32[]{:S(2)}) collective-permute-start(bf16[6,64,128]{2,1,0:T(8,128)(2,1)S(1)} %get-tuple-element.15), channel_id=1, source_target_pairs={{0,1},{1,2},{2,3},{3,4},{4,5},{5,6},{6,7},{7,8},{8,9},{9,10},{10,1... | collective-permute-start | bytes 294920 | tf_op jit(solution)/shard_map/ppermute | solution.py:214
  24.0 11.5 %collective-permute-start.3 = (bf16[13,64,128]{2,1,0:T(8,128)(2,1)S(1)}, bf16[13,64,128]{2,1,0:T(8,128)(2,1)S(1)}, u32[]{:S(2)}, u32[]{:S(2)}) collective-permute-start(bf16[13,64,128]{2,1,0:T(8,128)(2,1)S(1)} %pad_maximum_fusion), channel_id=1, source_target_pairs={{0,272},{1,273},{2,274},{3,275},{4,276},{5,277},{6,278},{7,279},{8... | collective-permute-start | bytes 638984 | tf_op jit(solution)/shard_map/ppermute | solution.py:227
  28.7 11.1 %collective-permute-start.4 = (bf16[13,64,128]{2,1,0:T(8,128)(2,1)S(1)}, bf16[13,64,128]{2,1,0:T(8,128)(2,1)S(1)}, u32[]{:S(2)}, u32[]{:S(2)}) collective-permute-start(bf16[13,64,128]{2,1,0:T(8,128)(2,1)S(1)} %pad_maximum_fusion.1), channel_id=1, source_target_pairs={{16,256},{17,257},{18,258},{19,259},{20,260},{21,261},{22,262},{23... | collective-permute-start | bytes 638984 | tf_op jit(solution)/shard_map/ppermute | solution.py:227

commit v3 on v2

v3 whole, which is shorter than its diff:
```python
import functools

import jax
import jax.numpy as jnp
from jax import lax
from jax.experimental import pallas as pl
from jax.experimental.pallas import tpu as pltpu
from jax.sharding import PartitionSpec as P

MAXS = 8
BLK = 8
CH = 64
HALO = MAXS + 1
LANES = 128
RING = 2 * LANES
PITCH = 2 * HALO
GROUPS = ((0, 7), (7, 9), (9, 16))


def EXTRA(height):
    return [0, 1, height - 2, height - 1]


frac_scale = 256.0


def lane_iota(shape):
    return lax.broadcasted_iota(jnp.int32, shape, len(shape) - 1)


def packed_edge(value, slot):
    return pltpu.roll(value, (PITCH * slot + HALO) % LANES, 1)


def in_slot(lane, slot):
    return (lane >= PITCH * slot) & (lane < PITCH * (slot + 1))


def border_of(vector, slot):
    return pltpu.roll(vector, (-PITCH * slot - HALO) % LANES, 1)


def pack_kernel(feat_ref, tile_ref, edge_ref, rows_ref):
    channels, height, lanes = feat_ref.shape
    for ch in range(channels):
        rows_ref[pl.ds(ch * height, height), :] = feat_ref[ch].astype(jnp.float32)
    lane = lane_iota((channels, lanes))
    for group, (first, last) in enumerate(GROUPS):
        packed = jnp.zeros((channels, lanes), jnp.float32)
        taken = list(range(first, last))
        if group == 1:
            taken += EXTRA(height)
        for slot, row in enumerate(taken):
            value = rows_ref[pl.ds(row, channels, stride=height), :]
            if slot < last - first:
                tile_ref[row] = value.astype(jnp.bfloat16)
            packed = jnp.where(in_slot(lane, slot), packed_edge(value, slot), packed)
        edge_ref[group] = packed.astype(jnp.bfloat16)


def shifted_sum(stacked):
    count = stacked.shape[0] // 3
    left = pltpu.roll(stacked[:count], 1, 1)
    right = pltpu.roll(stacked[2 * count :], RING - 1, 1)
    return left + stacked[count : 2 * count] + right


def transpose_kernel(feat_ref, tile_ref, rows_ref):
    channels, height, _ = feat_ref.shape
    for ch in range(channels):
        rows_ref[pl.ds(ch * height, height), :] = feat_ref[ch].astype(jnp.float32)
    for row in range(height):
        tile_ref[row] = rows_ref[pl.ds(row, channels, stride=height), :].astype(jnp.bfloat16)


def hidden_row(taken, first_w_ref, keep):
    total = jnp.dot(first_w_ref[...], taken, preferred_element_type=jnp.float32)
    return (jnp.maximum(shifted_sum(total), 0.0) * keep).astype(jnp.bfloat16)


def residual_row(taken, second_w_ref, head_ref):
    total = jnp.dot(second_w_ref[...], taken, preferred_element_type=jnp.float32)
    value = jnp.maximum(shifted_sum(total)[:, :LANES], 0.0).astype(jnp.bfloat16)
    return jnp.dot(head_ref[...], value, preferred_element_type=jnp.float32)


def inside_columns(edges_ref):
    lane = lane_iota((1, RING))
    outside = ((edges_ref[2] != 0) & (lane == RING - 1)) | ((edges_ref[3] != 0) & (lane == LANES))
    return jnp.where(outside, 0.0, 1.0)


def two_rows(motion_ref, k, row):
    return jnp.concatenate([motion_ref[k, row : row + 1, :], motion_ref[k, row + 1 : row + 2, :]], axis=1)


def column_weights(motion_ref, row):
    at = lax.broadcasted_iota(jnp.int32, (RING, RING), 0)
    column = jnp.where(at < RING - LANES // 2, at, at - RING).astype(jnp.float32)
    place = (lane_iota((1, RING)) & (LANES - 1)).astype(jnp.float32) + two_rows(motion_ref, 1, row)
    return jnp.maximum(1.0 - jnp.abs(place - column), 0.0).astype(jnp.bfloat16)


def warp_part(motion_ref, row, hat, source, first, count, total):
    mixed = jnp.dot(source, hat, preferred_element_type=jnp.float32)
    place = jnp.where(lane_iota((1, RING)) < LANES, 0.0, 1.0) + two_rows(motion_ref, 0, row)
    channels = source.shape[0] // count
    for step in range(count):
        weight = jnp.maximum(1.0 - jnp.abs(place - (first + step - row)), 0.0)
        term = weight * mixed[step * channels : (step + 1) * channels]
        total = term if total is None else total + term
    return total


def lay_both(tile, vector, slot, *targets):
    border = border_of(vector, slot).astype(jnp.bfloat16)
    for ref, start in targets:
        block = pl.ds(start, tile.shape[0])
        ref[block, :LANES] = tile
        ref[block, LANES:] = border


def middle_kernel(
    edges_ref, own_tile_ref, other_tile_ref, own_joined_ref, other_joined_ref,
    w_first_ref, w_second_ref, head_ref, offsets_ref, fractions_ref, tissue_ref,
    band_ref, side_ref, near_ref, part_ref, base_ref, cover_ref, first_w_ref, second_w_ref, sums_ref,
    window_ref, hidden_ref, motion_ref,
):
    height, channels, lanes = own_tile_ref.shape
    both = 2 * channels
    for b in range(3):
        block = pl.ds(b * channels, channels)
        for a in range(3):
            first_w_ref[block, a * both : (a + 1) * both] = w_first_ref[3 * a + b]
        second_w_ref[block, :both] = jnp.concatenate([w_second_ref[b], w_second_ref[3 + b]], axis=1)
        second_w_ref[block, both:] = w_second_ref[6 + b]
    for group, (first, last) in enumerate(GROUPS):
        own_vector = own_joined_ref[group].astype(jnp.float32)
        other_vector = other_joined_ref[group].astype(jnp.float32)
        for row in range(first, last):
            lay_both(own_tile_ref[row], own_vector, row - first, (band_ref, row * channels), (window_ref, row * both))
            lay_both(other_tile_ref[row], other_vector, row - first, (window_ref, row * both + channels))
    side_ref[: 2 * both] = window_ref[: 2 * both]
    side_ref[2 * both :] = window_ref[(height - 2) * both :]
    keep = inside_columns(edges_ref)
    for row in range(1, height - 1):
        taken = window_ref[pl.ds((row - 1) * both, 3 * both), :]
        hidden_ref[pl.ds((row - 1) * channels, channels), :] = hidden_row(taken, first_w_ref, keep)
    near_ref[:both] = hidden_ref[:both]
    near_ref[both:] = hidden_ref[(height - 4) * channels :]
    part_ref[...] = jnp.zeros_like(part_ref)
    for row in range(2, height - 2):
        pair = residual_row(hidden_ref[pl.ds((row - 2) * channels, 3 * channels), :], second_w_ref, head_ref)
        for k in range(2):
            part_ref[k, pl.ds(row, 1), :] = pair[k : k + 1]

    cells = tissue_ref[...].astype(jnp.float32)
    count = cells.shape[1]
    spread = lax.broadcasted_iota(jnp.int32, (count, lanes), 1) // BLK == lax.broadcasted_iota(jnp.int32, (count, lanes), 0)
    spread = jnp.dot(cells, spread.astype(jnp.float32), preferred_element_type=jnp.float32)
    for cell in range(cells.shape[0]):
        cover_ref[pl.ds(cell * BLK, BLK), :] = jnp.broadcast_to(spread[cell : cell + 1], (BLK, lanes))
    base_ref[...] = offsets_ref[...].astype(jnp.float32) + fractions_ref[...].astype(jnp.float32) / frac_scale
    motion_ref[...] = base_ref[...] + cover_ref[...][None] * jnp.tanh(part_ref[...])
    for row in range(2, height - 2, 2):
        first, last = max(0, row - HALO), min(height, row + HALO + 2)
        source = band_ref[pl.ds(first * channels, (last - first) * channels), :]
        hat = column_weights(motion_ref, row)
        sums_ref[pl.ds((row // 2 - 1) * channels, channels), :] = warp_part(
            motion_ref, row, hat, source, first, last - first, None
        )


def last_kernel(
    edges_ref, inner_ref, near_side_ref, near_ref, part_ref, base_ref, cover_ref, first_w_ref, second_w_ref, sums_ref,
    above_ref, below_ref, head_ref,
    warped_ref, motion_ref, band_ref, side_ref, hidden_ref, residual_ref, rows_ref,
):
    channels, height, lanes = warped_ref.shape
    both = 2 * channels
    start, stop = HALO * channels, (HALO + height) * channels
    band_ref[start:stop, :] = inner_ref[...]
    side_ref[2 * both : 4 * both, :] = near_side_ref[: 2 * both, :]
    side_ref[4 * both : 6 * both, :] = near_side_ref[2 * both :, :]
    middle, last = above_ref[HALO + 2].astype(jnp.float32), above_ref[HALO + 3].astype(jnp.float32)
    for index in range(HALO):
        targets = [(band_ref, index * channels)]
        if index >= HALO - 2:
            targets.append((side_ref, (index - HALO + 2) * both))
        lay_both(above_ref[index], *((middle, index) if index < 2 else (last, index - 2)), *targets)
    first, center = below_ref[HALO + 2].astype(jnp.float32), below_ref[HALO + 3].astype(jnp.float32)
    for index in range(HALO):
        targets = [(band_ref, stop + index * channels)]
        if index < 2:
            targets.append((side_ref, (6 + index) * both))
        lay_both(below_ref[index], *((first, index) if index < 7 else (center, index - 7)), *targets)
    for index in range(2):
        lay_both(above_ref[HALO + index], middle, 4 + index, (side_ref, index * both + channels))
        lay_both(below_ref[HALO + index], center, 2 + index, (side_ref, (6 + index) * both + channels))
    hidden_ref[both : 2 * both, :] = near_ref[:both, :]
    hidden_ref[2 * both : 3 * both, :] = near_ref[both:, :]
    inside = inside_columns(edges_ref)
    for row, side, spot in ((-1, 0, 0), (0, 1, 1), (height - 1, 4, 6), (height, 5, 7)):
        keep = inside
        if row == -1:
            keep = jnp.where(edges_ref[0] != 0, 0.0, inside)
        elif row == height:
            keep = jnp.where(edges_ref[1] != 0, 0.0, inside)
        taken = side_ref[pl.ds(side * both, 3 * both), :]
        hidden_ref[pl.ds(spot * channels, channels), :] = hidden_row(taken, first_w_ref, keep)
    residual_ref[...] = part_ref[...]
    for row, spot in ((0, 0), (1, 1), (height - 2, 4), (height - 1, 5)):
        pair = residual_row(hidden_ref[pl.ds(spot * channels, 3 * channels), :], second_w_ref, head_ref)
        for k in range(2):
            residual_ref[k, pl.ds(row, 1), :] = pair[k : k + 1]
    motion_ref[...] = base_ref[...] + cover_ref[...][None] * jnp.tanh(residual_ref[...])

    for row in range(0, height, 2):
        low, high = row - HALO, row + HALO + 2
        if 2 <= row < height - 2:
            total = sums_ref[pl.ds((row // 2 - 1) * channels, channels), :]
            spans = [(low, min(high, 0)), (max(low, height), high)]
        else:
            total = None
            spans = [(low, high)]
        hat = column_weights(motion_ref, row)
        for first, last in spans:
            if first < last:
                source = band_ref[pl.ds((first + HALO) * channels, (last - first) * channels), :]
                total = warp_part(motion_ref, row, hat, source, first, last - first, total)
        rows_ref[pl.ds(row * channels, channels), :] = total[:, :lanes]
        rows_ref[pl.ds((row + 1) * channels, channels), :] = total[:, lanes:]
    for ch in range(channels):
        warped_ref[ch] = rows_ref[pl.ds(ch, height, stride=channels), :].astype(jnp.bfloat16)


VMEM = pl.BlockSpec(memory_space=pltpu.VMEM)
SMEM = pl.BlockSpec(memory_space=pltpu.SMEM)


def call(body, outputs, scratch, *operands, scalars=0, flops=0):
    moved = sum(x.size * x.dtype.itemsize for x in (*operands, *outputs))
    return pl.pallas_call(
        body,
        out_shape=outputs,
        in_specs=[SMEM] * scalars + [VMEM] * (len(operands) - scalars),
        out_specs=[VMEM] * len(outputs),
        scratch_shapes=scratch,
        compiler_params=pltpu.CompilerParams(vmem_limit_bytes=40 * 2**20),
        cost_estimate=pl.CostEstimate(flops=flops, bytes_accessed=moved, transcendentals=0),
    )(*operands)


def of(shape, dtype=jnp.bfloat16):
    return jax.ShapeDtypeStruct(shape, dtype)


def ring(value, axis, step):
    peers = lax.axis_size(axis)
    return lax.ppermute(value, axis, [(i, (i + step) % peers) for i in range(peers)])


def across(value, step):
    rows, cols = lax.axis_size("row"), lax.axis_size("col")
    place = lambda pair, row, col: (pair * rows + row) * cols + col
    pairs = [
        (place(pair, row, col), place(1 - pair, row + step, col))
        for pair in range(2)
        for row in range(rows)
        if 0 <= row + step < rows
        for col in range(cols)
    ]
    return lax.ppermute(value, ("pair", "row", "col"), pairs)


def shards(features, offsets, fractions, tissue, w_first, w_second, head_weight):
    _, channels, height, columns = features.shape
    f32, bf16 = jnp.float32, jnp.bfloat16
    row, col = lax.axis_index("row"), lax.axis_index("col")
    rows, cols = lax.axis_size("row"), lax.axis_size("col")
    edges = jnp.stack([row == 0, row == rows - 1, col == 0, col == cols - 1]).astype(jnp.int32)

    swap = [(0, 1), (1, 0)]
    partner = lax.ppermute(features[0], "pair", swap)
    tile_shape = (height, channels, columns)
    scratch = [pltpu.VMEM((height * channels, columns), f32)]
    own_tile, edge = call(pack_kernel, [of(tile_shape), of((3, channels, columns))], scratch, features[0])
    from_left = ring(edge, "col", 1)
    from_right = ring(edge, "col", -1)
    lane = jnp.arange(columns)
    joined = jnp.where(
        lane % PITCH < HALO,
        jnp.where(col == 0, jnp.zeros_like(from_left), from_left),
        jnp.where(col == cols - 1, jnp.zeros_like(from_right), from_right),
    )
    other_joined = lax.ppermute(joined, "pair", swap)
    (other_tile,) = call(transpose_kernel, [of(tile_shape)], scratch, partner)
    mixed = jnp.where(lane < 2 * PITCH, other_joined[1], joined[1])[None]
    above = across(jnp.concatenate([other_tile[height - HALO :], own_tile[height - 2 :], mixed, other_joined[2:]]), 1)
    below = across(jnp.concatenate([other_tile[:HALO], own_tile[:2], other_joined[:1], mixed]), -1)

    wide = height * channels
    middle = call(
        middle_kernel,
        [
            of((wide, RING)),
            of((8 * channels, RING)),
            of((4 * channels, RING)),
            of((2, height, columns), f32),
            of((2, height, columns), f32),
            of((height, columns), f32),
            of((3 * channels, 6 * channels)),
            of((3 * channels, 3 * channels)),
            of(((height // 2 - 2) * channels, RING), f32),
        ],
        [
            pltpu.VMEM((2 * wide, RING), bf16),
            pltpu.VMEM(((height - 2) * channels, RING), bf16),
            pltpu.VMEM((2, height, columns), f32),
        ],
        edges, own_tile, other_tile, joined, other_joined,
        w_first, w_second, head_weight, offsets[0], fractions[0], tissue[0],
        scalars=1, flops=4 * 10**9,
    )
    warped, motion = call(
        last_kernel,
        [of((channels, height, columns)), of((2, height, columns), f32)],
        [
            pltpu.VMEM(((height + 2 * HALO) * channels, RING), bf16),
            pltpu.VMEM((16 * channels, RING), bf16),
            pltpu.VMEM((8 * channels, RING), bf16),
            pltpu.VMEM((2, height, columns), f32),
            pltpu.VMEM((wide, columns), f32),
        ],
        edges, *middle, above, below, head_weight,
        scalars=1, flops=2 * 10**9,
    )
    return (warped[None], motion[None])


def solution(mesh):
    return jax.shard_map(
        shards,
        mesh=mesh,
        in_specs=(
            P("pair", None, "row", "col"),
            P("pair", None, "row", "col"),
            P("pair", None, "row", "col"),
            P("pair", "row", "col"),
            P(),
            P(),
            P(),
        ),
        out_specs=(P("pair", None, "row", "col"), P("pair", None, "row", "col")),
        check_vma=False,
    )
```

time: 44.6 us -> 44.7 us (level)
  starting transfers between devices: 17.4 us -> 21.4 us
  local copies, waits for them, and re-layouts: 4.27 us -> 1.64 us
  waiting for transfers between devices: 12.1 us -> 10.7 us
    ppermute x1 -> x2, starting transfers between devices: 2.74 us -> 5.84 us  [the longest x1 3.11 us: shards(): other_joined = lax.ppermute(joined, 'pair', swap)]
    slice x2 -> x0, local copies, waits for them, and re-layouts: 1.14 us -> none  [the longest x1 1.13 us: shards(): w_first[:, :, channels:]]
    ppermute x2, waiting for transfers between devices: 4.21 us -> 3.19 us  [across(): return lax.ppermute(value, ('pair', 'row', 'col'), pairs)]
    reshape x6 -> x0, local copies, waits for them, and re-layouts: 0.88 us -> none  [the longest x3 0.49 us: taps(): return cube.reshape(3 * outputs, 3 * inputs)]
    ppermute x2, starting transfers between devices: 7.62 us -> 8.21 us  [ring(): lax.ppermute(value, axis, [(i, (i + step) % peers) for i in range(peers)])]
    ppermute x2, waiting for transfers between devices: 5.22 us -> 4.67 us  [ring(): lax.ppermute(value, axis, [(i, (i + step) % peers) for i in range(peers)])]
    unnamed x12 -> x14, local copies, waits for them, and re-layouts: 2.08 us -> 1.61 us
    ppermute x1 -> x2, waiting for transfers between devices: 2.71 us -> 2.79 us  [the longest x1 2.79 us: shards(): other_joined = lax.ppermute(joined, 'pair', swap)]
  transfers between devices with their start and end apart: 5 -> 6, of which waited for: 4 -> 4; matrix products, arithmetic and copies ran while one was open for 5% -> 0% of each run, Pallas kernels for 11% -> 12%
where the time goes in v3:
time: 44.7 us; the launch traced here: 44.4 us
  starting transfers between devices  21.4 us (48%)
  waiting for transfers between devices  10.7 us (24%)
  Pallas kernels  9.74 us (22%)
  local copies, waits for them, and re-layouts  1.64 us (4%)
  between operations  0.83 us (2%)
    pallas_call x4, Pallas kernels, call(): pl.pallas_call(body, out_shape=outputs, in_specs=[SMEM] * scalars + [VMEM...  9.74 us
    ppermute x2, starting transfers between devices, ring(): lax.ppermute(value, axis, [(i, (i + step) % peers) for i in range(peers)])  8.21 us
    ppermute x2, starting transfers between devices, across(): return lax.ppermute(value, ('pair', 'row', 'col'), pairs)  7.32 us
    ppermute x2, waiting for transfers between devices, ring(): lax.ppermute(value, axis, [(i, (i + step) % peers) for i in range(peers)])  4.67 us
    ppermute x2, waiting for transfers between devices, across(): return lax.ppermute(value, ('pair', 'row', 'col'), pairs)  3.19 us
    ppermute x1, starting transfers between devices, shards(): other_joined = lax.ppermute(joined, 'pair', swap)  3.11 us
    ppermute x1, waiting for transfers between devices, shards(): other_joined = lax.ppermute(joined, 'pair', swap)  2.79 us
    ppermute x1, starting transfers between devices, shards(): partner = lax.ppermute(features[0], 'pair', swap)  2.74 us
  transfers between devices with their start and end apart: 6, of which 4 were waited for; matrix products, arithmetic and copies ran while one was open for 0% of the time, Pallas kernels for 12%

profile of v3, /device:TPU:30, one launch (start us, length us, event | category | flops | bytes accessed | tf_op | source)
XLA Modules:
  0.0 44.4 jit_solution(14228228511646551989)
XLA Ops:
  0.6 2.7 %collective-permute-start = (bf16[64,16,128]{2,1,0:T(8,128)(2,1)}, bf16[64,16,128]{2,1,0:T(8,128)(2,1)S(1)}, u32[]{:S(2)}, u32[]{:S(2)}) collective-permute-start(bf16[64,16,128]{2,1,0:T(8,128)(2,1)} %bitcast.10), channel_id=1, source_target_pairs={{0,256},{256,0},{1,257},{257,1},{2,258},{258,2},{3,259},{259,3},{4... | collective-permute-start | bytes 786440 | tf_op jit(solution)/shard_map/ppermute | solution.py:284
  3.4 0.0 copy-start
  3.4 1.0 %copy-done = bf16[1,64,16,128]{3,2,1,0:T(8,128)(2,1)S(1)} copy-done((bf16[1,64,16,128]{3,2,1,0:T(8,128)(2,1)S(1)}, bf16[1,64,16,128]{3,2,1,0:T(8,128)(2,1)}, u32[]{:S(2)}) %copy-start) | copy-done | bytes 262168
  4.3 0.3 shard_map.86
  4.6 8.2 %collective-permute-start.2 = (bf16[3,64,128]{2,1,0:T(8,128)(2,1)S(1)}, bf16[3,64,128]{2,1,0:T(8,128)(2,1)S(1)}, u32[]{:S(2)}, u32[]{:S(2)}) collective-permute-start(bf16[3,64,128]{2,1,0:T(8,128)(2,1)S(1)} %get-tuple-element.16), channel_id=1, source_target_pairs={{0,15},{1,0},{2,1},{3,2},{4,3},{5,4},{6,5},{7,6},{8,7},{9,8},{10,9... | collective-permute-start | bytes 147464 | tf_op jit(solution)/shard_map/ppermute | solution.py:260
  12.9 0.0 collective-permute-start.1
  12.9 1.7 %collective-permute-done.2 = bf16[3,64,128]{2,1,0:T(8,128)(2,1)S(1)} collective-permute-done((bf16[3,64,128]{2,1,0:T(8,128)(2,1)S(1)}, bf16[3,64,128]{2,1,0:T(8,128)(2,1)S(1)}, u32[]{:S(2)}, u32[]{:S(2)}) %collective-permute-start.2) | collective-permute-done | bytes 49184 | tf_op jit(solution)/shard_map/ppermute | solution.py:260
  14.6 3.0 %collective-permute-done.1 = bf16[3,64,128]{2,1,0:T(8,128)(2,1)S(1)} collective-permute-done((bf16[3,64,128]{2,1,0:T(8,128)(2,1)S(1)}, bf16[3,64,128]{2,1,0:T(8,128)(2,1)S(1)}, u32[]{:S(2)}, u32[]{:S(2)}) %collective-permute-start.1) | collective-permute-done | bytes 49184 | tf_op jit(solution)/shard_map/ppermute | solution.py:260
  17.6 3.1 %collective-permute-start.3 = (bf16[3,64,128]{2,1,0:T(8,128)(2,1)S(1)}, bf16[3,64,128]{2,1,0:T(8,128)(2,1)S(1)}, u32[]{:S(2)}, u32[]{:S(2)}) collective-permute-start(bf16[3,64,128]{2,1,0:T(8,128)(2,1)S(1)} %select_select_fusion.own_joined_ref), channel_id=1, source_target_pairs={{0,256},{256,0},{1,257},{257,1},{2,258},{258,2},{3,259},{259,3},{4... | collective-permute-start | bytes 147464 | tf_op jit(solution)/shard_map/ppermute | solution.py:296
  20.7 0.1 add_convert_fusion.edges_ref
  20.8 2.8 %collective-permute-done.3.other_joined_ref = bf16[3,64,128]{2,1,0:T(8,128)(2,1)S(1)} collective-permute-done((bf16[3,64,128]{2,1,0:T(8,128)(2,1)S(1)}, bf16[3,64,128]{2,1,0:T(8,128)(2,1)S(1)}, u32[]{:S(2)}, u32[]{:S(2)}) %collective-permute-start.3) | collective-permute-done | bytes 49184 | tf_op jit(solution)/shard_map/ppermute | solution.py:296
  23.6 0.0 collective-permute-done.feat_ref
  23.6 0.2 shard_map.87.other_tile_ref
  23.8 0.0 copy-start.1
  23.8 0.0 copy-start.2
  23.8 0.0 copy-start.3
  23.9 0.0 copy-start.4
  23.9 0.1 pad_maximum_fusion.1
  23.9 5.4 %collective-permute-start.4 = (bf16[13,64,128]{2,1,0:T(8,128)(2,1)S(1)}, bf16[13,64,128]{2,1,0:T(8,128)(2,1)S(1)}, u32[]{:S(2)}, u32[]{:S(2)}) collective-permute-start(bf16[13,64,128]{2,1,0:T(8,128)(2,1)S(1)} %get-tuple-element.36), channel_id=1, source_target_pairs={{0,272},{1,273},{2,274},{3,275},{4,276},{5,277},{6,278},{7,279},{8... | collective-permute-start | bytes 638984 | tf_op jit(solution)/shard_map/ppermute | solution.py:273
  29.4 1.9 %collective-permute-start.5 = (bf16[13,64,128]{2,1,0:T(8,128)(2,1)S(1)}, bf16[13,64,128]{2,1,0:T(8,128)(2,1)S(1)}, u32[]{:S(2)}, u32[]{:S(2)}) collective-permute-start(bf16[13,64,128]{2,1,0:T(8,128)(2,1)S(1)} %get-tuple-element.35), channel_id=1, source_target_pairs={{16,256},{17,257},{18,258},{19,259},{20,260},{21,261},{22,262},{23... | collective-permute-start | bytes 638984 | tf_op jit(solution)/shard_map/ppermute | solution.py:273
  31.3 0.0 copy-start.5
  31.3 0.0 copy-start.6
  31.3 0.0 copy-done.1
  31.3 0.0 copy-done.2
  31.3 0.0 copy-done.3
  31.3 0.0 copy-done.4
  31.4 0.6 %copy-done.5 = s32[1,2,16]{2,1,0:T(2,128)S(1)} copy-done((s32[1,2,16]{2,1,0:T(2,128)S(1)}, s32[1,2,16]{2,1,0:T(2,128)}, u32[]{:S(2)}) %copy-start.5) | copy-done | bytes 152
  32.0 0.0 copy-done.6
  32.0 5.2 %shard_map.88 = (bf16[1024,256]{1,0:T(8,128)(2,1)S(1)}, bf16[512,256]{1,0:T(8,128)(2,1)S(1)}, bf16[256,256]{1,0:T(8,128)(2,1)S(1)}, f32[2,16,128]{2,1,0:T(8,128)...) custom-call(s32[4]{0:T(128)S(1)} %add_convert_fusion.edges_ref, ...), custom_call_target="tpu_custom_call" | custom-call | flops 4000000000 | bytes 2449808 | tf_op jit(solution)/shard_map/pallas_call | solution.py:243
  37.2 0.0 collective-permute-done.4.above_ref
  37.2 3.2 %collective-permute-done.5.below_ref = bf16[13,64,128]{2,1,0:T(8,128)(2,1)S(1)} collective-permute-done((bf16[13,64,128]{2,1,0:T(8,128)(2,1)S(1)}, bf16[13,64,128]{2,1,0:T(8,128)(2,1)S(1)}, u32[]{:S(2)}, u32[]{:S(2)}) %collective-permute-start.5) | collective-permute-done | bytes 213024 | tf_op jit(solution)/shard_map/ppermute | solution.py:273
  40.4 4.0 %shard_map.89 = (bf16[64,16,128]{2,1,0:T(8,128)(2,1)}, f32[2,16,128]{2,1,0:T(8,128)}) custom-call(s32[4]{0:T(128)S(1)} %add_convert_fusion.edges_ref, bf16[1024,256]{1,0:T(8,128)(2,1)S(1)} %get-tuple-element.17.inner_ref, bf16[512,256]{1,0:T(8,128)(2,1)S(1)} %get-tuple-element.18.near_side_ref, bf16[256,256]{1,0:T(8,128)(2,1)S(1)} %get-tuple-element.19.near_ref, ...), custom_call_target="tpu_custom_call" | custom-call | flops 2000000000 | bytes 2277648 | tf_op jit(solution)/shard_map/pallas_call | solution.py:243
  (6 shorter events, 0.1 us)
Async XLA Ops:
  0.6 23.0 %collective-permute-start = (bf16[64,16,128]{2,1,0:T(8,128)(2,1)}, bf16[64,16,128]{2,1,0:T(8,128)(2,1)S(1)}, u32[]{:S(2)}, u32[]{:S(2)}) collective-permute-start(bf16[64,16,128]{2,1,0:T(8,128)(2,1)} %bitcast.10), channel_id=1, source_target_pairs={{0,256},{256,0},{1,257},{257,1},{2,258},{258,2},{3,259},{259,3},{4... | collective-permute-start | bytes 786440 | tf_op jit(solution)/shard_map/ppermute | solution.py:284
  3.4 1.0 %copy-start = (bf16[1,64,16,128]{3,2,1,0:T(8,128)(2,1)S(1)}, bf16[1,64,16,128]{3,2,1,0:T(8,128)(2,1)}, u32[]{:S(2)}) copy-start(bf16[1,64,16,128]{3,2,1,0:T(8,128)(2,1)} %param.7) | copy-start | bytes 786436
  4.6 10.0 %collective-permute-start.2 = (bf16[3,64,128]{2,1,0:T(8,128)(2,1)S(1)}, bf16[3,64,128]{2,1,0:T(8,128)(2,1)S(1)}, u32[]{:S(2)}, u32[]{:S(2)}) collective-permute-start(bf16[3,64,128]{2,1,0:T(8,128)(2,1)S(1)} %get-tuple-element.16), channel_id=1, source_target_pairs={{0,15},{1,0},{2,1},{3,2},{4,3},{5,4},{6,5},{7,6},{8,7},{9,8},{10,9... | collective-permute-start | bytes 147464 | tf_op jit(solution)/shard_map/ppermute | solution.py:260
  12.9 4.7 %collective-permute-start.1 = (bf16[3,64,128]{2,1,0:T(8,128)(2,1)S(1)}, bf16[3,64,128]{2,1,0:T(8,128)(2,1)S(1)}, u32[]{:S(2)}, u32[]{:S(2)}) collective-permute-start(bf16[3,64,128]{2,1,0:T(8,128)(2,1)S(1)} %get-tuple-element.16), channel_id=1, source_target_pairs={{0,1},{1,2},{2,3},{3,4},{4,5},{5,6},{6,7},{7,8},{8,9},{9,10},{10,1... | collective-permute-start | bytes 147464 | tf_op jit(solution)/shard_map/ppermute | solution.py:260
  17.6 6.0 %collective-permute-start.3 = (bf16[3,64,128]{2,1,0:T(8,128)(2,1)S(1)}, bf16[3,64,128]{2,1,0:T(8,128)(2,1)S(1)}, u32[]{:S(2)}, u32[]{:S(2)}) collective-permute-start(bf16[3,64,128]{2,1,0:T(8,128)(2,1)S(1)} %select_select_fusion.own_joined_ref), channel_id=1, source_target_pairs={{0,256},{256,0},{1,257},{257,1},{2,258},{258,2},{3,259},{259,3},{4... | collective-permute-start | bytes 147464 | tf_op jit(solution)/shard_map/ppermute | solution.py:296
  23.8 7.5 %copy-start.1 = (bf16[9,64,128]{2,1,0:T(8,128)(2,1)S(1)}, bf16[9,64,128]{2,1,0:T(8,128)(2,1)}, u32[]{:S(2)}) copy-start(bf16[9,64,128]{2,1,0:T(8,128)(2,1)} %w_first_ref.1) | copy-start | bytes 442372
  23.8 7.5 %copy-start.2 = (bf16[9,64,64]{2,1,0:T(8,128)(2,1)S(1)}, bf16[9,64,64]{2,1,0:T(8,128)(2,1)}, u32[]{:S(2)}) copy-start(bf16[9,64,64]{2,1,0:T(8,128)(2,1)} %w_second_ref.1) | copy-start | bytes 221188
  23.8 7.5 %copy-start.3 = (s32[1,2,16,128]{3,2,1,0:T(8,128)S(1)}, s32[1,2,16,128]{3,2,1,0:T(8,128)}, u32[]{:S(2)}) copy-start(s32[1,2,16,128]{3,2,1,0:T(8,128)} %param.8) | copy-start | bytes 49156
  23.9 7.5 %copy-start.4 = (s32[1,2,16,128]{3,2,1,0:T(8,128)S(1)}, s32[1,2,16,128]{3,2,1,0:T(8,128)}, u32[]{:S(2)}) copy-start(s32[1,2,16,128]{3,2,1,0:T(8,128)} %param.9) | copy-start | bytes 49156
  23.9 13.3 %collective-permute-start.4 = (bf16[13,64,128]{2,1,0:T(8,128)(2,1)S(1)}, bf16[13,64,128]{2,1,0:T(8,128)(2,1)S(1)}, u32[]{:S(2)}, u32[]{:S(2)}) collective-permute-start(bf16[13,64,128]{2,1,0:T(8,128)(2,1)S(1)} %get-tuple-element.36), channel_id=1, source_target_pairs={{0,272},{1,273},{2,274},{3,275},{4,276},{5,277},{6,278},{7,279},{8... | collective-permute-start | bytes 638984 | tf_op jit(solution)/shard_map/ppermute | solution.py:273
  29.4 11.1 %collective-permute-start.5 = (bf16[13,64,128]{2,1,0:T(8,128)(2,1)S(1)}, bf16[13,64,128]{2,1,0:T(8,128)(2,1)S(1)}, u32[]{:S(2)}, u32[]{:S(2)}) collective-permute-start(bf16[13,64,128]{2,1,0:T(8,128)(2,1)S(1)} %get-tuple-element.35), channel_id=1, source_target_pairs={{16,256},{17,257},{18,258},{19,259},{20,260},{21,261},{22,262},{23... | collective-permute-start | bytes 638984 | tf_op jit(solution)/shard_map/ppermute | solution.py:273
  31.3 0.7 %copy-start.5 = (s32[1,2,16]{2,1,0:T(2,128)S(1)}, s32[1,2,16]{2,1,0:T(2,128)}, u32[]{:S(2)}) copy-start(s32[1,2,16]{2,1,0:T(2,128)} %param.10) | copy-start | bytes 388
  31.3 0.7 %copy-start.6 = (bf16[2,64]{1,0:T(2,128)(2,1)S(1)}, bf16[2,64]{1,0:T(2,128)(2,1)}, u32[]{:S(2)}) copy-start(bf16[2,64]{1,0:T(2,128)(2,1)} %head_ref.3) | copy-start | bytes 772

commit v4 on v3

--- a/solution.py
+++ b/solution.py
@@ -78,16 +78,16 @@
     return (jnp.maximum(shifted_sum(total), 0.0) * keep).astype(jnp.bfloat16)
 
 
-def residual_row(taken, second_w_ref, head_ref):
+def second_row(taken, second_w_ref):
     total = jnp.dot(second_w_ref[...], taken, preferred_element_type=jnp.float32)
-    value = jnp.maximum(shifted_sum(total)[:, :LANES], 0.0).astype(jnp.bfloat16)
-    return jnp.dot(head_ref[...], value, preferred_element_type=jnp.float32)
-
-
-def inside_columns(edges_ref):
-    lane = lane_iota((1, RING))
-    outside = ((edges_ref[2] != 0) & (lane == RING - 1)) | ((edges_ref[3] != 0) & (lane == LANES))
-    return jnp.where(outside, 0.0, 1.0)
+    return jnp.maximum(shifted_sum(total)[:, :LANES], 0.0).astype(jnp.bfloat16)
+
+
+def project(second_ref, rows, head_ref, residual_ref):
+    pairs = jnp.dot(head_ref[...], second_ref[...], preferred_element_type=jnp.float32)
+    for index, row in enumerate(rows):
+        for k in range(2):
+            residual_ref[k, pl.ds(row, 1), :] = pairs[k : k + 1, index * LANES : (index + 1) * LANES]
 
 
 def two_rows(motion_ref, k, row):
@@ -95,10 +95,12 @@
 
 
 def column_weights(motion_ref, row):
-    at = lax.broadcasted_iota(jnp.int32, (RING, RING), 0)
-    column = jnp.where(at < RING - LANES // 2, at, at - RING).astype(jnp.float32)
     place = (lane_iota((1, RING)) & (LANES - 1)).astype(jnp.float32) + two_rows(motion_ref, 1, row)
-    return jnp.maximum(1.0 - jnp.abs(place - column), 0.0).astype(jnp.bfloat16)
+    parts = []
+    for first, count in ((0, LANES + 16), (-16, 16)):
+        column = (lax.broadcasted_iota(jnp.int32, (count, RING), 0) + first).astype(jnp.float32)
+        parts.append(jnp.maximum(1.0 - jnp.abs(place - column), 0.0).astype(jnp.bfloat16))
+    return jnp.concatenate([parts[0], jnp.zeros((RING - LANES - 32, RING), jnp.bfloat16), parts[1]])
 
 
 def warp_part(motion_ref, row, hat, source, first, count, total):
@@ -121,10 +123,10 @@
 
 
 def middle_kernel(
-    edges_ref, own_tile_ref, other_tile_ref, own_joined_ref, other_joined_ref,
+    keep_ref, own_tile_ref, other_tile_ref, own_joined_ref, other_joined_ref,
     w_first_ref, w_second_ref, head_ref, offsets_ref, fractions_ref, tissue_ref,
-    band_ref, side_ref, near_ref, part_ref, base_ref, cover_ref, first_w_ref, second_w_ref, sums_ref,
-    window_ref, hidden_ref, motion_ref,
+    band_ref, side_ref, near_ref, base_ref, cover_ref, first_w_ref, second_w_ref, sums_ref, motion_ref, hats_ref,
+    window_ref, hidden_ref, second_ref, part_ref,
 ):
     height, channels, lanes = own_tile_ref.shape
     both = 2 * channels
@@ -142,17 +144,18 @@
             lay_both(other_tile_ref[row], other_vector, row - first, (window_ref, row * both + channels))
     side_ref[: 2 * both] = window_ref[: 2 * both]
     side_ref[2 * both :] = window_ref[(height - 2) * both :]
-    keep = inside_columns(edges_ref)
+    keep = keep_ref[0:1]
     for row in range(1, height - 1):
         taken = window_ref[pl.ds((row - 1) * both, 3 * both), :]
         hidden_ref[pl.ds((row - 1) * channels, channels), :] = hidden_row(taken, first_w_ref, keep)
     near_ref[:both] = hidden_ref[:both]
     near_ref[both:] = hidden_ref[(height - 4) * channels :]
     part_ref[...] = jnp.zeros_like(part_ref)
-    for row in range(2, height - 2):
-        pair = residual_row(hidden_ref[pl.ds((row - 2) * channels, 3 * channels), :], second_w_ref, head_ref)
-        for k in range(2):
-            part_ref[k, pl.ds(row, 1), :] = pair[k : k + 1]
+    inner = range(2, height - 2)
+    for index in range(len(inner)):
+        taken = hidden_ref[pl.ds(index * channels, 3 * channels), :]
+        second_ref[:, index * lanes : (index + 1) * lanes] = second_row(taken, second_w_ref)
+    project(second_ref, inner, head_ref, part_ref)
 
     cells = tissue_ref[...].astype(jnp.float32)
     count = cells.shape[1]
@@ -166,85 +169,139 @@
         first, last = max(0, row - HALO), min(height, row + HALO + 2)
         source = band_ref[pl.ds(first * channels, (last - first) * channels), :]
         hat = column_weights(motion_ref, row)
+        hats_ref[row // 2 - 1] = hat
         sums_ref[pl.ds((row // 2 - 1) * channels, channels), :] = warp_part(
             motion_ref, row, hat, source, first, last - first, None
         )
 
 
-def last_kernel(
-    edges_ref, inner_ref, near_side_ref, near_ref, part_ref, base_ref, cover_ref, first_w_ref, second_w_ref, sums_ref,
-    above_ref, below_ref, head_ref,
-    warped_ref, motion_ref, band_ref, side_ref, hidden_ref, residual_ref, rows_ref,
+def new_motion(side_ref, hidden_ref, second_ref, rows, keeps, spots, weights, field_refs, half, inner_motion_ref, residual_ref):
+    first_w_ref, second_w_ref, head_ref = weights
+    base_ref, cover_ref = field_refs
+    both = side_ref.shape[0] // 4
+    channels = both // 2
+    for index, (keep, spot) in enumerate(zip(keeps, spots)):
+        taken = side_ref[pl.ds(index * both, 3 * both), :]
+        hidden_ref[pl.ds(spot * channels, channels), :] = hidden_row(taken, first_w_ref, keep)
+    for index in range(2):
+        taken = hidden_ref[pl.ds(index * channels, 3 * channels), :]
+        second_ref[:, index * LANES : (index + 1) * LANES] = second_row(taken, second_w_ref)
+    residual_ref[...] = jnp.zeros_like(residual_ref)
+    project(second_ref, rows, head_ref, residual_ref)
+    count = residual_ref.shape[1]
+    block = pl.ds(half * count, count)
+    fresh = base_ref[:, block, :] + cover_ref[block, :][None] * jnp.tanh(residual_ref[...])
+    place = lax.broadcasted_iota(jnp.int32, fresh.shape, 1)
+    is_fresh = (place == rows[0]) | (place == rows[1])
+    return jnp.where(is_fresh, fresh, inner_motion_ref[:, block, :])
+
+
+def top_kernel(
+    keep_ref, band_ref, near_side_ref, near_ref, base_ref, cover_ref, first_w_ref, second_w_ref, sums_ref,
+    inner_motion_ref, hats_ref, above_ref, head_ref,
+    top_ref, motion_ref, halo_ref, side_ref, hidden_ref, second_ref, residual_ref,
+):
+    channels = above_ref.shape[1]
+    both = 2 * channels
+    middle, last = above_ref[HALO + 2].astype(jnp.float32), above_ref[HALO + 3].astype(jnp.float32)
+    for index in range(HALO):
+        targets = [(halo_ref, index * channels)]
+        if index >= HALO - 2:
+            targets.append((side_ref, (index - HALO + 2) * both))
+        lay_both(above_ref[index], *((middle, index) if index < 2 else (last, index - 2)), *targets)
+    for index in range(2):
+        lay_both(above_ref[HALO + index], middle, 4 + index, (side_ref, index * both + channels))
+    side_ref[2 * both :] = near_side_ref[: 2 * both]
+    hidden_ref[both:] = near_ref[:both]
+    keeps = (keep_ref[1:2], keep_ref[0:1])
+    weights = (first_w_ref, second_w_ref, head_ref)
+    motion_ref[...] = new_motion(
+        side_ref, hidden_ref, second_ref, (0, 1), keeps, (0, 1), weights, (base_ref, cover_ref), 0, inner_motion_ref, residual_ref
+    )
+    for row in (2, 4, 6, 8):
+        total = sums_ref[pl.ds((row // 2 - 1) * channels, channels), :]
+        source = halo_ref[row * channels :, :]
+        total = warp_part(inner_motion_ref, row, hats_ref[row // 2 - 1], source, row - HALO, HALO - row, total)
+        top_ref[pl.ds(row // 2 * channels, channels), :] = total
+    hat = column_weights(motion_ref, 0)
+    total = warp_part(motion_ref, 0, hat, halo_ref[...], -HALO, HALO, None)
+    top_ref[:channels, :] = warp_part(motion_ref, 0, hat, band_ref[: (HALO + 2) * channels, :], 0, HALO + 2, total)
+
+
+def bottom_kernel(
+    keep_ref, band_ref, near_side_ref, near_ref, base_ref, cover_ref, first_w_ref, second_w_ref, sums_ref,
+    inner_motion_ref, hats_ref, top_ref, top_motion_ref, below_ref, head_ref,
+    warped_ref, field_ref, halo_ref, side_ref, hidden_ref, second_ref, residual_ref, motion_ref, rows_ref, staged_ref, sems,
 ):
     channels, height, lanes = warped_ref.shape
     both = 2 * channels
-    start, stop = HALO * channels, (HALO + height) * channels
-    band_ref[start:stop, :] = inner_ref[...]
-    side_ref[2 * both : 4 * both, :] = near_side_ref[: 2 * both, :]
-    side_ref[4 * both : 6 * both, :] = near_side_ref[2 * both :, :]
-    middle, last = above_ref[HALO + 2].astype(jnp.float32), above_ref[HALO + 3].astype(jnp.float32)
-    for index in range(HALO):
-        targets = [(band_ref, index * channels)]
-        if index >= HALO - 2:
-            targets.append((side_ref, (index - HALO + 2) * both))
-        lay_both(above_ref[index], *((middle, index) if index < 2 else (last, index - 2)), *targets)
+    half = height // 2
     first, center = below_ref[HALO + 2].astype(jnp.float32), below_ref[HALO + 3].astype(jnp.float32)
     for index in range(HALO):
-        targets = [(band_ref, stop + index * channels)]
+        targets = [(halo_ref, index * channels)]
         if index < 2:
-            targets.append((side_ref, (6 + index) * both))
+            targets.append((side_ref, (2 + index) * both))
         lay_both(below_ref[index], *((first, index) if index < 7 else (center, index - 7)), *targets)
     for index in range(2):
-        lay_both(above_ref[HALO + index], middle, 4 + index, (side_ref, index * both + channels))
-        lay_both(below_ref[HALO + index], center, 2 + index, (side_ref, (6 + index) * both + channels))
-    hidden_ref[both : 2 * both, :] = near_ref[:both, :]
-    hidden_ref[2 * both : 3 * both, :] = near_ref[both:, :]
-    inside = inside_columns(edges_ref)
-    for row, side, spot in ((-1, 0, 0), (0, 1, 1), (height - 1, 4, 6), (height, 5, 7)):
-        keep = inside
-        if row == -1:
-            keep = jnp.where(edges_ref[0] != 0, 0.0, inside)
-        elif row == height:
-            keep = jnp.where(edges_ref[1] != 0, 0.0, inside)
-        taken = side_ref[pl.ds(side * both, 3 * both), :]
-        hidden_ref[pl.ds(spot * channels, channels), :] = hidden_row(taken, first_w_ref, keep)
-    residual_ref[...] = part_ref[...]
-    for row, spot in ((0, 0), (1, 1), (height - 2, 4), (height - 1, 5)):
-        pair = residual_row(hidden_ref[pl.ds(spot * channels, 3 * channels), :], second_w_ref, head_ref)
-        for k in range(2):
-            residual_ref[k, pl.ds(row, 1), :] = pair[k : k + 1]
-    motion_ref[...] = base_ref[...] + cover_ref[...][None] * jnp.tanh(residual_ref[...])
-
-    for row in range(0, height, 2):
-        low, high = row - HALO, row + HALO + 2
-        if 2 <= row < height - 2:
-            total = sums_ref[pl.ds((row // 2 - 1) * channels, channels), :]
-            spans = [(low, min(high, 0)), (max(low, height), high)]
-        else:
-            total = None
-            spans = [(low, high)]
-        hat = column_weights(motion_ref, row)
-        for first, last in spans:
-            if first < last:
-                source = band_ref[pl.ds((first + HALO) * channels, (last - first) * channels), :]
-                total = warp_part(motion_ref, row, hat, source, first, last - first, total)
+        lay_both(below_ref[HALO + index], center, 2 + index, (side_ref, (2 + index) * both + channels))
+    side_ref[: 2 * both] = near_side_ref[2 * both :]
+    hidden_ref[:both] = near_ref[both:]
+    keeps = (keep_ref[0:1], keep_ref[2:3])
+    weights = (first_w_ref, second_w_ref, head_ref)
+    motion_ref[:, :half, :] = top_motion_ref[...]
+    motion_ref[:, half:, :] = new_motion(
+        side_ref, hidden_ref, second_ref, (half - 2, half - 1), keeps, (2, 3), weights, (base_ref, cover_ref), 1,
+        inner_motion_ref, residual_ref,
+    )
+    field_copy = pltpu.make_async_copy(motion_ref, field_ref, sems.at[4])
+    field_copy.start()
+
+    def keep_rows(row, total):
         rows_ref[pl.ds(row * channels, channels), :] = total[:, :lanes]
         rows_ref[pl.ds((row + 1) * channels, channels), :] = total[:, lanes:]
-    for ch in range(channels):
-        warped_ref[ch] = rows_ref[pl.ds(ch, height, stride=channels), :].astype(jnp.bfloat16)
+
+    for row in (0, 2, 4):
+        keep_rows(row, top_ref[pl.ds(row // 2 * channels, channels), :])
+    for row in (6, 8, 10, 12):
+        if row < HALO:
+            total = top_ref[pl.ds(row // 2 * channels, channels), :]
+        else:
+            total = sums_ref[pl.ds((row // 2 - 1) * channels, channels), :]
+        count = row + HALO + 2 - height
+        source = halo_ref[: count * channels, :]
+        keep_rows(row, warp_part(inner_motion_ref, row, hats_ref[row // 2 - 1], source, height, count, total))
+        if row == 6:
+            for ch in range(channels):
+                value = rows_ref[pl.ds(ch, half, stride=channels), :]
+                staged_ref[ch, :half, :] = value.astype(jnp.bfloat16)
+    row = height - 2
+    start = row - HALO
+    hat = column_weights(motion_ref, row)
+    total = warp_part(motion_ref, row, hat, band_ref[start * channels :, :], start, HALO + 2, None)
+    keep_rows(row, warp_part(motion_ref, row, hat, halo_ref[...], height, HALO, total))
+    copies = []
+    piece = channels // 4
+    for part in range(4):
+        for ch in range(part * piece, (part + 1) * piece):
+            value = rows_ref[pl.ds(half * channels + ch, half, stride=channels), :]
+            staged_ref[ch, half:, :] = value.astype(jnp.bfloat16)
+        block = pl.ds(part * piece, piece)
+        copies.append(pltpu.make_async_copy(staged_ref.at[block], warped_ref.at[block], sems.at[part]))
+        copies[-1].start()
+    for copy in (field_copy, *copies):
+        copy.wait()
 
 
 VMEM = pl.BlockSpec(memory_space=pltpu.VMEM)
-SMEM = pl.BlockSpec(memory_space=pltpu.SMEM)
-
-
-def call(body, outputs, scratch, *operands, scalars=0, flops=0):
+
+
+def call(body, outputs, scratch, *operands, flops=0, placed=()):
     moved = sum(x.size * x.dtype.itemsize for x in (*operands, *outputs))
     return pl.pallas_call(
         body,
         out_shape=outputs,
-        in_specs=[SMEM] * scalars + [VMEM] * (len(operands) - scalars),
-        out_specs=[VMEM] * len(outputs),
+        in_specs=[VMEM] * len(operands),
+        out_specs=[pl.BlockSpec(memory_space=pl.ANY) if i in placed else VMEM for i in range(len(outputs))],
         scratch_shapes=scratch,
         compiler_params=pltpu.CompilerParams(vmem_limit_bytes=40 * 2**20),
         cost_estimate=pl.CostEstimate(flops=flops, bytes_accessed=moved, transcendentals=0),
@@ -278,7 +335,10 @@
     f32, bf16 = jnp.float32, jnp.bfloat16
     row, col = lax.axis_index("row"), lax.axis_index("col")
     rows, cols = lax.axis_size("row"), lax.axis_size("col")
-    edges = jnp.stack([row == 0, row == rows - 1, col == 0, col == cols - 1]).astype(jnp.int32)
+    ring_lane = jnp.arange(RING)[None]
+    inside = ((col > 0) | (ring_lane != RING - 1)) & ((col < cols - 1) | (ring_lane != LANES))
+    line = jnp.arange(8)[:, None]
+    keep = (inside & ((line != 1) | (row > 0)) & ((line != 2) | (row < rows - 1))).astype(f32)
 
     swap = [(0, 1), (1, 0)]
     partner = lax.ppermute(features[0], "pair", swap)
@@ -293,47 +353,65 @@
         jnp.where(col == 0, jnp.zeros_like(from_left), from_left),
         jnp.where(col == cols - 1, jnp.zeros_like(from_right), from_right),
     )
-    other_joined = lax.ppermute(joined, "pair", swap)
+    both_joined = lax.all_gather(joined, "pair")
+    other_joined = jnp.where(lax.axis_index("pair") == 0, both_joined[1], both_joined[0])
     (other_tile,) = call(transpose_kernel, [of(tile_shape)], scratch, partner)
     mixed = jnp.where(lane < 2 * PITCH, other_joined[1], joined[1])[None]
     above = across(jnp.concatenate([other_tile[height - HALO :], own_tile[height - 2 :], mixed, other_joined[2:]]), 1)
     below = across(jnp.concatenate([other_tile[:HALO], own_tile[:2], other_joined[:1], mixed]), -1)
 
     wide = height * channels
-    middle = call(
+    band, side, near, base, cover, first_w, second_w, sums, inner_motion, hats = call(
         middle_kernel,
         [
             of((wide, RING)),
             of((8 * channels, RING)),
             of((4 * channels, RING)),
             of((2, height, columns), f32),
-            of((2, height, columns), f32),
             of((height, columns), f32),
             of((3 * channels, 6 * channels)),
             of((3 * channels, 3 * channels)),
             of(((height // 2 - 2) * channels, RING), f32),
+            of((2, height, columns), f32),
+            of((height // 2 - 2, RING, RING)),
         ],
         [
             pltpu.VMEM((2 * wide, RING), bf16),
             pltpu.VMEM(((height - 2) * channels, RING), bf16),
+            pltpu.VMEM((channels, (height - 4) * columns), bf16),
             pltpu.VMEM((2, height, columns), f32),
         ],
-        edges, own_tile, other_tile, joined, other_joined,
+        keep, own_tile, other_tile, joined, other_joined,
         w_first, w_second, head_weight, offsets[0], fractions[0], tissue[0],
-        scalars=1, flops=4 * 10**9,
+        flops=4 * 10**9,
+    )
+    common = (keep, band, side, near, base, cover, first_w, second_w, sums, inner_motion, hats)
+    edge_scratch = [
+        pltpu.VMEM((HALO * channels, RING), bf16),
+        pltpu.VMEM((8 * channels, RING), bf16),
+        pltpu.VMEM((4 * channels, RING), bf16),
+        pltpu.VMEM((channels, 2 * columns), bf16),
+        pltpu.VMEM((2, height // 2, columns), f32),
+    ]
+    top, top_motion = call(
+        top_kernel,
+        [of((5 * channels, RING), f32), of((2, height // 2, columns), f32)],
+        edge_scratch,
+        *common, above, head_weight,
+        flops=10**9,
     )
     warped, motion = call(
-        last_kernel,
+        bottom_kernel,
         [of((channels, height, columns)), of((2, height, columns), f32)],
         [
-            pltpu.VMEM(((height + 2 * HALO) * channels, RING), bf16),
-            pltpu.VMEM((16 * channels, RING), bf16),
-            pltpu.VMEM((8 * channels, RING), bf16),
+            *edge_scratch,
             pltpu.VMEM((2, height, columns), f32),
             pltpu.VMEM((wide, columns), f32),
+            pltpu.VMEM((channels, height, columns), bf16),
+            pltpu.SemaphoreType.DMA((5,)),
         ],
-        edges, *middle, above, below, head_weight,
-        scalars=1, flops=2 * 10**9,
+        *common, top, top_motion, below, head_weight,
+        flops=10**9, placed=(0, 1),
     )
     return (warped[None], motion[None])
 

time: 44.7 us -> 41.6 us (0.931)
  blocking collectives: 0 us -> 4.77 us
  Pallas kernels: 9.74 us -> 6.39 us
  starting transfers between devices: 21.4 us -> 18.3 us
  waiting for transfers between devices: 10.7 us -> 9.23 us
    all_gather x0 -> x1, blocking collectives: none -> 4.77 us  [shards(): both_joined = lax.all_gather(joined, 'pair')]
    pallas_call x4 -> x5, Pallas kernels: 9.74 us -> 6.39 us  [call(): pl.pallas_call(body, out_shape=outputs, in_specs=[VMEM] * len(operands),...]
    ppermute x1 -> x0, starting transfers between devices: 3.11 us -> none  [shards(): other_joined = lax.ppermute(joined, 'pair', swap)]
    ppermute x1 -> x0, waiting for transfers between devices: 2.79 us -> none  [shards(): other_joined = lax.ppermute(joined, 'pair', swap)]
    ppermute x2, waiting for transfers between devices: 3.19 us -> 4.64 us  [across(): return lax.ppermute(value, ('pair', 'row', 'col'), pairs)]
  transfers between devices with their start and end apart: 6 -> 5, of which waited for: 4 -> 4; matrix products, arithmetic and copies ran while one was open for 0% -> 0% of each run, Pallas kernels for 12% -> 10%
where the time goes in v4:
time: 41.6 us; the launch traced here: 41.4 us
  starting transfers between devices  18.3 us (44%)
  waiting for transfers between devices  9.23 us (22%)
  Pallas kernels  6.39 us (15%)
  blocking collectives  4.77 us (11%)
  local copies, waits for them, and re-layouts  1.64 us (4%)
  between operations  0.84 us (2%)
    ppermute x2, starting transfers between devices, ring(): lax.ppermute(value, axis, [(i, (i + step) % peers) for i in range(peers)])  8.21 us
    ppermute x2, starting transfers between devices, across(): return lax.ppermute(value, ('pair', 'row', 'col'), pairs)  7.32 us
    pallas_call x5, Pallas kernels, call(): pl.pallas_call(body, out_shape=outputs, in_specs=[VMEM] * len(operands),...  6.39 us
    all_gather x1, blocking collectives, shards(): both_joined = lax.all_gather(joined, 'pair')  4.77 us
    ppermute x2, waiting for transfers between devices, across(): return lax.ppermute(value, ('pair', 'row', 'col'), pairs)  4.64 us
    ppermute x2, waiting for transfers between devices, ring(): lax.ppermute(value, axis, [(i, (i + step) % peers) for i in range(peers)])  4.59 us
    ppermute x1, starting transfers between devices, shards(): partner = lax.ppermute(features[0], 'pair', swap)  2.74 us
    unnamed x14, local copies, waits for them, and re-layouts  1.61 us
  transfers between devices with their start and end apart: 5, of which 4 were waited for; matrix products, arithmetic and copies ran while one was open for 0% of the time, Pallas kernels for 10%

profile of v4, /device:TPU:30, one launch (start us, length us, event | category | flops | bytes accessed | tf_op | source)
XLA Modules:
  0.0 41.4 jit_solution(2192812375975366450)
XLA Ops:
  0.6 2.7 %collective-permute-start = (bf16[64,16,128]{2,1,0:T(8,128)(2,1)}, bf16[64,16,128]{2,1,0:T(8,128)(2,1)S(1)}, u32[]{:S(2)}, u32[]{:S(2)}) collective-permute-start(bf16[64,16,128]{2,1,0:T(8,128)(2,1)} %bitcast.16), channel_id=1, source_target_pairs={{0,256},{256,0},{1,257},{257,1},{2,258},{258,2},{3,259},{259,3},{4... | collective-permute-start | bytes 786440 | tf_op jit(solution)/shard_map/ppermute | solution.py:344
  3.4 0.0 copy-start
  3.4 1.0 %copy-done = bf16[1,64,16,128]{3,2,1,0:T(8,128)(2,1)S(1)} copy-done((bf16[1,64,16,128]{3,2,1,0:T(8,128)(2,1)S(1)}, bf16[1,64,16,128]{3,2,1,0:T(8,128)(2,1)}, u32[]{:S(2)}) %copy-start) | copy-done | bytes 262168
  4.3 0.3 shard_map.86
  4.6 8.2 %collective-permute-start.2 = (bf16[3,64,128]{2,1,0:T(8,128)(2,1)S(1)}, bf16[3,64,128]{2,1,0:T(8,128)(2,1)S(1)}, u32[]{:S(2)}, u32[]{:S(2)}) collective-permute-start(bf16[3,64,128]{2,1,0:T(8,128)(2,1)S(1)} %get-tuple-element.19), channel_id=1, source_target_pairs={{0,15},{1,0},{2,1},{3,2},{4,3},{5,4},{6,5},{7,6},{8,7},{9,8},{10,9... | collective-permute-start | bytes 147464 | tf_op jit(solution)/shard_map/ppermute | solution.py:317
  12.9 0.0 collective-permute-start.1
  12.9 0.1 and_convert_fusion.keep_ref
  13.0 1.6 %collective-permute-done.2 = bf16[3,64,128]{2,1,0:T(8,128)(2,1)S(1)} collective-permute-done((bf16[3,64,128]{2,1,0:T(8,128)(2,1)S(1)}, bf16[3,64,128]{2,1,0:T(8,128)(2,1)S(1)}, u32[]{:S(2)}, u32[]{:S(2)}) %collective-permute-start.2) | collective-permute-done | bytes 49184 | tf_op jit(solution)/shard_map/ppermute | solution.py:317
  14.6 3.0 %collective-permute-done.1 = bf16[3,64,128]{2,1,0:T(8,128)(2,1)S(1)} collective-permute-done((bf16[3,64,128]{2,1,0:T(8,128)(2,1)S(1)}, bf16[3,64,128]{2,1,0:T(8,128)(2,1)S(1)}, u32[]{:S(2)}, u32[]{:S(2)}) %collective-permute-start.1) | collective-permute-done | bytes 49184 | tf_op jit(solution)/shard_map/ppermute | solution.py:317
  17.6 4.8 %all-gather = bf16[6,64,128]{2,1,0:T(8,128)(2,1)S(1)} all-gather(bf16[3,64,128]{2,1,0:T(8,128)(2,1)S(1)} %select_select_fusion.own_joined_ref), channel_id=2, replica_groups=mesh['pair'=2,'row'=16,'col'=16] {'pair'}, dimensions={0}, use_global_device_ids=true | all-gather | bytes 147456 | tf_op jit(solution)/shard_map/all_gather | solution.py:356
  22.4 0.0 collective-permute-done.feat_ref
  22.4 0.2 shard_map.87.other_tile_ref
  22.7 0.0 copy-start.1
  22.7 0.0 copy-start.2
  22.7 0.0 copy-start.3
  22.7 0.0 copy-start.4
  22.7 0.1 pad_maximum_fusion.1
  22.8 5.4 %collective-permute-start.3 = (bf16[13,64,128]{2,1,0:T(8,128)(2,1)S(1)}, bf16[13,64,128]{2,1,0:T(8,128)(2,1)S(1)}, u32[]{:S(2)}, u32[]{:S(2)}) collective-permute-start(bf16[13,64,128]{2,1,0:T(8,128)(2,1)S(1)} %get-tuple-element.41), channel_id=1, source_target_pairs={{0,272},{1,273},{2,274},{3,275},{4,276},{5,277},{6,278},{7,279},{8... | collective-permute-start | bytes 638984 | tf_op jit(solution)/shard_map/ppermute | solution.py:330
  28.2 1.9 %collective-permute-start.4 = (bf16[13,64,128]{2,1,0:T(8,128)(2,1)S(1)}, bf16[13,64,128]{2,1,0:T(8,128)(2,1)S(1)}, u32[]{:S(2)}, u32[]{:S(2)}) collective-permute-start(bf16[13,64,128]{2,1,0:T(8,128)(2,1)S(1)} %get-tuple-element.40), channel_id=1, source_target_pairs={{16,256},{17,257},{18,258},{19,259},{20,260},{21,261},{22,262},{23... | collective-permute-start | bytes 638984 | tf_op jit(solution)/shard_map/ppermute | solution.py:330
  30.1 0.0 copy-start.5
  30.1 0.0 copy-start.6
  30.2 0.0 copy-done.1
  30.2 0.0 copy-done.2
  30.2 0.0 copy-done.3
  30.2 0.0 copy-done.4
  30.2 0.6 %copy-done.5 = s32[1,2,16]{2,1,0:T(2,128)S(1)} copy-done((s32[1,2,16]{2,1,0:T(2,128)S(1)}, s32[1,2,16]{2,1,0:T(2,128)}, u32[]{:S(2)}) %copy-start.5) | copy-done | bytes 152
  30.8 0.0 copy-done.6
  30.8 2.5 %shard_map.88 = (bf16[1024,256]{1,0:T(8,128)(2,1)S(1)}, bf16[512,256]{1,0:T(8,128)(2,1)S(1)}, bf16[256,256]{1,0:T(8,128)(2,1)S(1)}, f32[2,16,128]{2,1,0:T(8,128)...) custom-call(f32[8,256]{1,0:T(8,128)S(1)} %and_convert_fusion.keep_re, ...), custom_call_target="tpu_custom_call" | custom-call | flops 4000000000 | bytes 3244416 | tf_op jit(solution)/shard_map/pallas_call | solution.py:300
  33.4 0.8 %collective-permute-done.3.above_ref = bf16[13,64,128]{2,1,0:T(8,128)(2,1)S(1)} collective-permute-done((bf16[13,64,128]{2,1,0:T(8,128)(2,1)S(1)}, bf16[13,64,128]{2,1,0:T(8,128)(2,1)S(1)}, u32[]{:S(2)}, u32[]{:S(2)}) %collective-permute-start.3) | collective-permute-done | bytes 213024 | tf_op jit(solution)/shard_map/ppermute | solution.py:330
  34.2 1.2 %shard_map.89 = (f32[320,256]{1,0:T(8,128)S(1)}, f32[2,8,128]{2,1,0:T(8,128)S(1)}) custom-call(f32[8,256]{1,0:T(8,128)S(1)} %and_convert_fusion.keep_ref, bf16[1024,256]{1,0:T(8,128)(2,1)S(1)} %get-tuple-element.20.band_ref, bf16[512,256]{1,0:T(8,128)(2,1)S(1)} %get-tuple-element.21.near_side_ref, bf16[256,256]{1,0:T(8,128)(2,1)S(1)} %get-tuple-element.22.near_ref, ...), custom_call_target="tpu_custom_call" | custom-call | flops 1000000000 | bytes 2916608 | tf_op jit(solution)/shard_map/pallas_call | solution.py:300
  35.4 3.9 %collective-permute-done.4.below_ref = bf16[13,64,128]{2,1,0:T(8,128)(2,1)S(1)} collective-permute-done((bf16[13,64,128]{2,1,0:T(8,128)(2,1)S(1)}, bf16[13,64,128]{2,1,0:T(8,128)(2,1)S(1)}, u32[]{:S(2)}, u32[]{:S(2)}) %collective-permute-start.4) | collective-permute-done | bytes 213024 | tf_op jit(solution)/shard_map/ppermute | solution.py:330
  39.3 2.1 %shard_map.90 = (bf16[64,16,128]{2,1,0:T(8,128)(2,1)}, f32[2,16,128]{2,1,0:T(8,128)}) custom-call(f32[8,256]{1,0:T(8,128)S(1)} %and_convert_fusion.keep_ref, bf16[1024,256]{1,0:T(8,128)(2,1)S(1)} %get-tuple-element.20.band_ref, bf16[512,256]{1,0:T(8,128)(2,1)S(1)} %get-tuple-element.21.near_side_ref, bf16[256,256]{1,0:T(8,128)(2,1)S(1)} %get-tuple-element.22.near_ref, ...), custom_call_target="tpu_custom_call" | custom-call | flops 1000000000 | bytes 3195136 | tf_op jit(solution)/shard_map/pallas_call | solution.py:300
  (11 shorter events, 0.1 us)
Async XLA Ops:
  0.6 21.8 %collective-permute-start = (bf16[64,16,128]{2,1,0:T(8,128)(2,1)}, bf16[64,16,128]{2,1,0:T(8,128)(2,1)S(1)}, u32[]{:S(2)}, u32[]{:S(2)}) collective-permute-start(bf16[64,16,128]{2,1,0:T(8,128)(2,1)} %bitcast.16), channel_id=1, source_target_pairs={{0,256},{256,0},{1,257},{257,1},{2,258},{258,2},{3,259},{259,3},{4... | collective-permute-start | bytes 786440 | tf_op jit(solution)/shard_map/ppermute | solution.py:344
  3.4 1.0 %copy-start = (bf16[1,64,16,128]{3,2,1,0:T(8,128)(2,1)S(1)}, bf16[1,64,16,128]{3,2,1,0:T(8,128)(2,1)}, u32[]{:S(2)}) copy-start(bf16[1,64,16,128]{3,2,1,0:T(8,128)(2,1)} %param.7) | copy-start | bytes 786436
  4.6 10.0 %collective-permute-start.2 = (bf16[3,64,128]{2,1,0:T(8,128)(2,1)S(1)}, bf16[3,64,128]{2,1,0:T(8,128)(2,1)S(1)}, u32[]{:S(2)}, u32[]{:S(2)}) collective-permute-start(bf16[3,64,128]{2,1,0:T(8,128)(2,1)S(1)} %get-tuple-element.19), channel_id=1, source_target_pairs={{0,15},{1,0},{2,1},{3,2},{4,3},{5,4},{6,5},{7,6},{8,7},{9,8},{10,9... | collective-permute-start | bytes 147464 | tf_op jit(solution)/shard_map/ppermute | solution.py:317
  12.9 4.7 %collective-permute-start.1 = (bf16[3,64,128]{2,1,0:T(8,128)(2,1)S(1)}, bf16[3,64,128]{2,1,0:T(8,128)(2,1)S(1)}, u32[]{:S(2)}, u32[]{:S(2)}) collective-permute-start(bf16[3,64,128]{2,1,0:T(8,128)(2,1)S(1)} %get-tuple-element.19), channel_id=1, source_target_pairs={{0,1},{1,2},{2,3},{3,4},{4,5},{5,6},{6,7},{7,8},{8,9},{9,10},{10,1... | collective-permute-start | bytes 147464 | tf_op jit(solution)/shard_map/ppermute | solution.py:317
  22.7 7.5 %copy-start.1 = (bf16[9,64,128]{2,1,0:T(8,128)(2,1)S(1)}, bf16[9,64,128]{2,1,0:T(8,128)(2,1)}, u32[]{:S(2)}) copy-start(bf16[9,64,128]{2,1,0:T(8,128)(2,1)} %w_first_ref.1) | copy-start | bytes 442372
  22.7 7.5 %copy-start.2 = (bf16[9,64,64]{2,1,0:T(8,128)(2,1)S(1)}, bf16[9,64,64]{2,1,0:T(8,128)(2,1)}, u32[]{:S(2)}) copy-start(bf16[9,64,64]{2,1,0:T(8,128)(2,1)} %w_second_ref.1) | copy-start | bytes 221188
  22.7 7.5 %copy-start.3 = (s32[1,2,16,128]{3,2,1,0:T(8,128)S(1)}, s32[1,2,16,128]{3,2,1,0:T(8,128)}, u32[]{:S(2)}) copy-start(s32[1,2,16,128]{3,2,1,0:T(8,128)} %param.8) | copy-start | bytes 49156
  22.7 7.5 %copy-start.4 = (s32[1,2,16,128]{3,2,1,0:T(8,128)S(1)}, s32[1,2,16,128]{3,2,1,0:T(8,128)}, u32[]{:S(2)}) copy-start(s32[1,2,16,128]{3,2,1,0:T(8,128)} %param.9) | copy-start | bytes 49156
  22.8 11.4 %collective-permute-start.3 = (bf16[13,64,128]{2,1,0:T(8,128)(2,1)S(1)}, bf16[13,64,128]{2,1,0:T(8,128)(2,1)S(1)}, u32[]{:S(2)}, u32[]{:S(2)}) collective-permute-start(bf16[13,64,128]{2,1,0:T(8,128)(2,1)S(1)} %get-tuple-element.41), channel_id=1, source_target_pairs={{0,272},{1,273},{2,274},{3,275},{4,276},{5,277},{6,278},{7,279},{8... | collective-permute-start | bytes 638984 | tf_op jit(solution)/shard_map/ppermute | solution.py:330
  28.2 11.1 %collective-permute-start.4 = (bf16[13,64,128]{2,1,0:T(8,128)(2,1)S(1)}, bf16[13,64,128]{2,1,0:T(8,128)(2,1)S(1)}, u32[]{:S(2)}, u32[]{:S(2)}) collective-permute-start(bf16[13,64,128]{2,1,0:T(8,128)(2,1)S(1)} %get-tuple-element.40), channel_id=1, source_target_pairs={{16,256},{17,257},{18,258},{19,259},{20,260},{21,261},{22,262},{23... | collective-permute-start | bytes 638984 | tf_op jit(solution)/shard_map/ppermute | solution.py:330
  30.1 0.7 %copy-start.5 = (s32[1,2,16]{2,1,0:T(2,128)S(1)}, s32[1,2,16]{2,1,0:T(2,128)}, u32[]{:S(2)}) copy-start(s32[1,2,16]{2,1,0:T(2,128)} %param.10) | copy-start | bytes 388
  30.1 0.7 %copy-start.6 = (bf16[2,64]{1,0:T(2,128)(2,1)S(1)}, bf16[2,64]{1,0:T(2,128)(2,1)}, u32[]{:S(2)}) copy-start(bf16[2,64]{1,0:T(2,128)(2,1)} %head_ref.5) | copy-start | bytes 772

commit v5 on v4

--- a/solution.py
+++ b/solution.py
@@ -63,14 +63,6 @@
     left = pltpu.roll(stacked[:count], 1, 1)
     right = pltpu.roll(stacked[2 * count :], RING - 1, 1)
     return left + stacked[count : 2 * count] + right
-
-
-def transpose_kernel(feat_ref, tile_ref, rows_ref):
-    channels, height, _ = feat_ref.shape
-    for ch in range(channels):
-        rows_ref[pl.ds(ch * height, height), :] = feat_ref[ch].astype(jnp.float32)
-    for row in range(height):
-        tile_ref[row] = rows_ref[pl.ds(row, channels, stride=height), :].astype(jnp.bfloat16)
 
 
 def hidden_row(taken, first_w_ref, keep):
@@ -341,12 +333,12 @@
     keep = (inside & ((line != 1) | (row > 0)) & ((line != 2) | (row < rows - 1))).astype(f32)
 
     swap = [(0, 1), (1, 0)]
-    partner = lax.ppermute(features[0], "pair", swap)
     tile_shape = (height, channels, columns)
     scratch = [pltpu.VMEM((height * channels, columns), f32)]
     own_tile, edge = call(pack_kernel, [of(tile_shape), of((3, channels, columns))], scratch, features[0])
     from_left = ring(edge, "col", 1)
     from_right = ring(edge, "col", -1)
+    other_tile = lax.ppermute(own_tile, "pair", swap)
     lane = jnp.arange(columns)
     joined = jnp.where(
         lane % PITCH < HALO,
@@ -355,7 +347,6 @@
     )
     both_joined = lax.all_gather(joined, "pair")
     other_joined = jnp.where(lax.axis_index("pair") == 0, both_joined[1], both_joined[0])
-    (other_tile,) = call(transpose_kernel, [of(tile_shape)], scratch, partner)
     mixed = jnp.where(lane < 2 * PITCH, other_joined[1], joined[1])[None]
     above = across(jnp.concatenate([other_tile[height - HALO :], own_tile[height - 2 :], mixed, other_joined[2:]]), 1)
     below = across(jnp.concatenate([other_tile[:HALO], own_tile[:2], other_joined[:1], mixed]), -1)

time: 41.6 us -> 38.3 us (0.921)
  waiting for transfers between devices: 9.23 us -> 5.95 us
    ppermute x2, waiting for transfers between devices: 4.59 us -> 1.83 us  [ring(): lax.ppermute(value, axis, [(i, (i + step) % peers) for i in range(peers)])]
    ppermute x2, waiting for transfers between devices: 4.64 us -> 4.12 us  [across(): return lax.ppermute(value, ('pair', 'row', 'col'), pairs)]
    pallas_call x5 -> x4, Pallas kernels: 6.39 us -> 6.19 us  [call(): pl.pallas_call(body, out_shape=outputs, in_specs=[VMEM] * len(operands),...]
  transfers between devices with their start and end apart: 5 -> 5, of which waited for: 4 -> 3; matrix products, arithmetic and copies ran while one was open for 0% -> 0% of each run, Pallas kernels for 10% -> 10%
where the time goes in v5:
time: 38.3 us; the launch traced here: 38 us
  starting transfers between devices  18.4 us (48%)
  Pallas kernels  6.19 us (16%)
  waiting for transfers between devices  5.95 us (16%)
  blocking collectives  4.77 us (12%)
  local copies, waits for them, and re-layouts  1.64 us (4%)
  between operations  0.86 us (2%)
    ppermute x2, starting transfers between devices, ring(): lax.ppermute(value, axis, [(i, (i + step) % peers) for i in range(peers)])  8.49 us
    ppermute x2, starting transfers between devices, across(): return lax.ppermute(value, ('pair', 'row', 'col'), pairs)  7.18 us
    pallas_call x4, Pallas kernels, call(): pl.pallas_call(body, out_shape=outputs, in_specs=[VMEM] * len(operands),...  6.19 us
    all_gather x1, blocking collectives, shards(): both_joined = lax.all_gather(joined, 'pair')  4.77 us
    ppermute x2, waiting for transfers between devices, across(): return lax.ppermute(value, ('pair', 'row', 'col'), pairs)  4.12 us
    ppermute x1, starting transfers between devices, shards(): other_tile = lax.ppermute(own_tile, 'pair', swap)  2.73 us
    ppermute x2, waiting for transfers between devices, ring(): lax.ppermute(value, axis, [(i, (i + step) % peers) for i in range(peers)])  1.83 us
    unnamed x14, local copies, waits for them, and re-layouts  1.6 us
  transfers between devices with their start and end apart: 5, of which 3 were waited for; matrix products, arithmetic and copies ran while one was open for 0% of the time, Pallas kernels for 10%

profile of v5, /device:TPU:30, one launch (start us, length us, event | category | flops | bytes accessed | tf_op | source)
XLA Modules:
  0.0 38.0 jit_solution(6050534734868682536)
XLA Ops:
  0.6 0.0 copy-start
  0.6 0.9 %copy-done = bf16[1,64,16,128]{3,2,1,0:T(8,128)(2,1)S(1)} copy-done((bf16[1,64,16,128]{3,2,1,0:T(8,128)(2,1)S(1)}, bf16[1,64,16,128]{3,2,1,0:T(8,128)(2,1)}, u32[]{:S(2)}) %copy-start) | copy-done | bytes 262168
  1.6 0.3 shard_map.86
  1.9 8.5 %collective-permute-start.2 = (bf16[3,64,128]{2,1,0:T(8,128)(2,1)S(1)}, bf16[3,64,128]{2,1,0:T(8,128)(2,1)S(1)}, u32[]{:S(2)}, u32[]{:S(2)}) collective-permute-start(bf16[3,64,128]{2,1,0:T(8,128)(2,1)S(1)} %get-tuple-element.19), channel_id=1, source_target_pairs={{0,15},{1,0},{2,1},{3,2},{4,3},{5,4},{6,5},{7,6},{8,7},{9,8},{10,9... | collective-permute-start | bytes 147464 | tf_op jit(solution)/shard_map/ppermute | solution.py:309
  10.4 0.0 collective-permute-start.1
  10.4 2.7 %collective-permute-start = (bf16[16,64,128]{2,1,0:T(8,128)(2,1)S(1)}, bf16[16,64,128]{2,1,0:T(8,128)(2,1)S(1)}, u32[]{:S(2)}, u32[]{:S(2)}) collective-permute-start(bf16[16,64,128]{2,1,0:T(8,128)(2,1)S(1)} %get-tuple-element.18.own_tile_ref), channel_id=1, source_target_pairs={{0,256},{256,0},{1,257},{257,1},{2,258},{258,2},{3,259},{259,3},{4... | collective-permute-start | bytes 786440 | tf_op jit(solution)/shard_map/ppermute | solution.py:341
  13.2 0.1 and_convert_fusion.keep_ref
  13.3 0.0 collective-permute-done.2
  13.3 1.8 %collective-permute-done.1 = bf16[3,64,128]{2,1,0:T(8,128)(2,1)S(1)} collective-permute-done((bf16[3,64,128]{2,1,0:T(8,128)(2,1)S(1)}, bf16[3,64,128]{2,1,0:T(8,128)(2,1)S(1)}, u32[]{:S(2)}, u32[]{:S(2)}) %collective-permute-start.1) | collective-permute-done | bytes 49184 | tf_op jit(solution)/shard_map/ppermute | solution.py:309
  15.1 4.8 %all-gather = bf16[6,64,128]{2,1,0:T(8,128)(2,1)S(1)} all-gather(bf16[3,64,128]{2,1,0:T(8,128)(2,1)S(1)} %select_select_fusion.own_joined_ref), channel_id=2, replica_groups=mesh['pair'=2,'row'=16,'col'=16] {'pair'}, dimensions={0}, use_global_device_ids=true | all-gather | bytes 147456 | tf_op jit(solution)/shard_map/all_gather | solution.py:348
  19.9 0.0 collective-permute-done.other_tile_ref
  20.0 0.0 copy-start.1
  20.0 0.0 copy-start.2
  20.0 0.0 copy-start.3
  20.0 0.0 copy-start.4
  20.0 0.1 pad_maximum_fusion.1
  20.1 4.7 %collective-permute-start.3 = (bf16[13,64,128]{2,1,0:T(8,128)(2,1)S(1)}, bf16[13,64,128]{2,1,0:T(8,128)(2,1)S(1)}, u32[]{:S(2)}, u32[]{:S(2)}) collective-permute-start(bf16[13,64,128]{2,1,0:T(8,128)(2,1)S(1)} %get-tuple-element.41), channel_id=1, source_target_pairs={{0,272},{1,273},{2,274},{3,275},{4,276},{5,277},{6,278},{7,279},{8... | collective-permute-start | bytes 638984 | tf_op jit(solution)/shard_map/ppermute | solution.py:322
  24.9 2.4 %collective-permute-start.4 = (bf16[13,64,128]{2,1,0:T(8,128)(2,1)S(1)}, bf16[13,64,128]{2,1,0:T(8,128)(2,1)S(1)}, u32[]{:S(2)}, u32[]{:S(2)}) collective-permute-start(bf16[13,64,128]{2,1,0:T(8,128)(2,1)S(1)} %get-tuple-element.40), channel_id=1, source_target_pairs={{16,256},{17,257},{18,258},{19,259},{20,260},{21,261},{22,262},{23... | collective-permute-start | bytes 638984 | tf_op jit(solution)/shard_map/ppermute | solution.py:322
  27.3 0.0 copy-start.5
  27.3 0.0 copy-start.6
  27.3 0.0 copy-done.1
  27.4 0.0 copy-done.2
  27.4 0.0 copy-done.3
  27.4 0.0 copy-done.4
  27.4 0.6 %copy-done.5 = s32[1,2,16]{2,1,0:T(2,128)S(1)} copy-done((s32[1,2,16]{2,1,0:T(2,128)S(1)}, s32[1,2,16]{2,1,0:T(2,128)}, u32[]{:S(2)}) %copy-start.5) | copy-done | bytes 152
  28.0 0.0 copy-done.6
  28.0 2.5 %shard_map.87 = (bf16[1024,256]{1,0:T(8,128)(2,1)S(1)}, bf16[512,256]{1,0:T(8,128)(2,1)S(1)}, bf16[256,256]{1,0:T(8,128)(2,1)S(1)}, f32[2,16,128]{2,1,0:T(8,128)...) custom-call(f32[8,256]{1,0:T(8,128)S(1)} %and_convert_fusion.keep_re, ...), custom_call_target="tpu_custom_call" | custom-call | flops 4000000000 | bytes 3244416 | tf_op jit(solution)/shard_map/pallas_call | solution.py:292
  30.6 0.9 %collective-permute-done.3.above_ref = bf16[13,64,128]{2,1,0:T(8,128)(2,1)S(1)} collective-permute-done((bf16[13,64,128]{2,1,0:T(8,128)(2,1)S(1)}, bf16[13,64,128]{2,1,0:T(8,128)(2,1)S(1)}, u32[]{:S(2)}, u32[]{:S(2)}) %collective-permute-start.3) | collective-permute-done | bytes 213024 | tf_op jit(solution)/shard_map/ppermute | solution.py:322
  31.5 1.2 %shard_map.88 = (f32[320,256]{1,0:T(8,128)S(1)}, f32[2,8,128]{2,1,0:T(8,128)S(1)}) custom-call(f32[8,256]{1,0:T(8,128)S(1)} %and_convert_fusion.keep_ref, bf16[1024,256]{1,0:T(8,128)(2,1)S(1)} %get-tuple-element.20.band_ref, bf16[512,256]{1,0:T(8,128)(2,1)S(1)} %get-tuple-element.21.near_side_ref, bf16[256,256]{1,0:T(8,128)(2,1)S(1)} %get-tuple-element.22.near_ref, ...), custom_call_target="tpu_custom_call" | custom-call | flops 1000000000 | bytes 2916608 | tf_op jit(solution)/shard_map/pallas_call | solution.py:292
  32.7 3.2 %collective-permute-done.4.below_ref = bf16[13,64,128]{2,1,0:T(8,128)(2,1)S(1)} collective-permute-done((bf16[13,64,128]{2,1,0:T(8,128)(2,1)S(1)}, bf16[13,64,128]{2,1,0:T(8,128)(2,1)S(1)}, u32[]{:S(2)}, u32[]{:S(2)}) %collective-permute-start.4) | collective-permute-done | bytes 213024 | tf_op jit(solution)/shard_map/ppermute | solution.py:322
  35.9 2.1 %shard_map.89 = (bf16[64,16,128]{2,1,0:T(8,128)(2,1)}, f32[2,16,128]{2,1,0:T(8,128)}) custom-call(f32[8,256]{1,0:T(8,128)S(1)} %and_convert_fusion.keep_ref, bf16[1024,256]{1,0:T(8,128)(2,1)S(1)} %get-tuple-element.20.band_ref, bf16[512,256]{1,0:T(8,128)(2,1)S(1)} %get-tuple-element.21.near_side_ref, bf16[256,256]{1,0:T(8,128)(2,1)S(1)} %get-tuple-element.22.near_ref, ...), custom_call_target="tpu_custom_call" | custom-call | flops 1000000000 | bytes 3195136 | tf_op jit(solution)/shard_map/pallas_call | solution.py:292
  (11 shorter events, 0.1 us)
Async XLA Ops:
  0.6 1.0 %copy-start = (bf16[1,64,16,128]{3,2,1,0:T(8,128)(2,1)S(1)}, bf16[1,64,16,128]{3,2,1,0:T(8,128)(2,1)}, u32[]{:S(2)}) copy-start(bf16[1,64,16,128]{3,2,1,0:T(8,128)(2,1)} %param.7) | copy-start | bytes 786436
  1.9 11.4 %collective-permute-start.2 = (bf16[3,64,128]{2,1,0:T(8,128)(2,1)S(1)}, bf16[3,64,128]{2,1,0:T(8,128)(2,1)S(1)}, u32[]{:S(2)}, u32[]{:S(2)}) collective-permute-start(bf16[3,64,128]{2,1,0:T(8,128)(2,1)S(1)} %get-tuple-element.19), channel_id=1, source_target_pairs={{0,15},{1,0},{2,1},{3,2},{4,3},{5,4},{6,5},{7,6},{8,7},{9,8},{10,9... | collective-permute-start | bytes 147464 | tf_op jit(solution)/shard_map/ppermute | solution.py:309
  10.4 4.7 %collective-permute-start.1 = (bf16[3,64,128]{2,1,0:T(8,128)(2,1)S(1)}, bf16[3,64,128]{2,1,0:T(8,128)(2,1)S(1)}, u32[]{:S(2)}, u32[]{:S(2)}) collective-permute-start(bf16[3,64,128]{2,1,0:T(8,128)(2,1)S(1)} %get-tuple-element.19), channel_id=1, source_target_pairs={{0,1},{1,2},{2,3},{3,4},{4,5},{5,6},{6,7},{7,8},{8,9},{9,10},{10,1... | collective-permute-start | bytes 147464 | tf_op jit(solution)/shard_map/ppermute | solution.py:309
  10.4 9.6 %collective-permute-start = (bf16[16,64,128]{2,1,0:T(8,128)(2,1)S(1)}, bf16[16,64,128]{2,1,0:T(8,128)(2,1)S(1)}, u32[]{:S(2)}, u32[]{:S(2)}) collective-permute-start(bf16[16,64,128]{2,1,0:T(8,128)(2,1)S(1)} %get-tuple-element.18.own_tile_ref), channel_id=1, source_target_pairs={{0,256},{256,0},{1,257},{257,1},{2,258},{258,2},{3,259},{259,3},{4... | collective-permute-start | bytes 786440 | tf_op jit(solution)/shard_map/ppermute | solution.py:341
  20.0 7.4 %copy-start.1 = (bf16[9,64,128]{2,1,0:T(8,128)(2,1)S(1)}, bf16[9,64,128]{2,1,0:T(8,128)(2,1)}, u32[]{:S(2)}) copy-start(bf16[9,64,128]{2,1,0:T(8,128)(2,1)} %w_first_ref.1) | copy-start | bytes 442372
  20.0 7.4 %copy-start.2 = (bf16[9,64,64]{2,1,0:T(8,128)(2,1)S(1)}, bf16[9,64,64]{2,1,0:T(8,128)(2,1)}, u32[]{:S(2)}) copy-start(bf16[9,64,64]{2,1,0:T(8,128)(2,1)} %w_second_ref.1) | copy-start | bytes 221188
  20.0 7.4 %copy-start.3 = (s32[1,2,16,128]{3,2,1,0:T(8,128)S(1)}, s32[1,2,16,128]{3,2,1,0:T(8,128)}, u32[]{:S(2)}) copy-start(s32[1,2,16,128]{3,2,1,0:T(8,128)} %param.8) | copy-start | bytes 49156
  20.0 7.3 %copy-start.4 = (s32[1,2,16,128]{3,2,1,0:T(8,128)S(1)}, s32[1,2,16,128]{3,2,1,0:T(8,128)}, u32[]{:S(2)}) copy-start(s32[1,2,16,128]{3,2,1,0:T(8,128)} %param.9) | copy-start | bytes 49156
  20.1 11.4 %collective-permute-start.3 = (bf16[13,64,128]{2,1,0:T(8,128)(2,1)S(1)}, bf16[13,64,128]{2,1,0:T(8,128)(2,1)S(1)}, u32[]{:S(2)}, u32[]{:S(2)}) collective-permute-start(bf16[13,64,128]{2,1,0:T(8,128)(2,1)S(1)} %get-tuple-element.41), channel_id=1, source_target_pairs={{0,272},{1,273},{2,274},{3,275},{4,276},{5,277},{6,278},{7,279},{8... | collective-permute-start | bytes 638984 | tf_op jit(solution)/shard_map/ppermute | solution.py:322
  24.9 11.1 %collective-permute-start.4 = (bf16[13,64,128]{2,1,0:T(8,128)(2,1)S(1)}, bf16[13,64,128]{2,1,0:T(8,128)(2,1)S(1)}, u32[]{:S(2)}, u32[]{:S(2)}) collective-permute-start(bf16[13,64,128]{2,1,0:T(8,128)(2,1)S(1)} %get-tuple-element.40), channel_id=1, source_target_pairs={{16,256},{17,257},{18,258},{19,259},{20,260},{21,261},{22,262},{23... | collective-permute-start | bytes 638984 | tf_op jit(solution)/shard_map/ppermute | solution.py:322
  27.3 0.7 %copy-start.5 = (s32[1,2,16]{2,1,0:T(2,128)S(1)}, s32[1,2,16]{2,1,0:T(2,128)}, u32[]{:S(2)}) copy-start(s32[1,2,16]{2,1,0:T(2,128)} %param.10) | copy-start | bytes 388
  27.3 0.7 %copy-start.6 = (bf16[2,64]{1,0:T(2,128)(2,1)S(1)}, bf16[2,64]{1,0:T(2,128)(2,1)}, u32[]{:S(2)}) copy-start(bf16[2,64]{1,0:T(2,128)(2,1)} %head_ref.5) | copy-start | bytes 772

commit v6 on v5

--- a/solution.py
+++ b/solution.py
@@ -12,15 +12,12 @@
 CH = 64
 HALO = MAXS + 1
 LANES = 128
+REACH = 2
 RING = 2 * LANES
 PITCH = 2 * HALO
 GROUPS = ((0, 7), (7, 9), (9, 16))
 
 
-def EXTRA(height):
-    return [0, 1, height - 2, height - 1]
-
-
 frac_scale = 256.0
 
 
@@ -28,16 +25,16 @@
     return lax.broadcasted_iota(jnp.int32, shape, len(shape) - 1)
 
 
-def packed_edge(value, slot):
-    return pltpu.roll(value, (PITCH * slot + HALO) % LANES, 1)
-
-
-def in_slot(lane, slot):
-    return (lane >= PITCH * slot) & (lane < PITCH * (slot + 1))
-
-
-def border_of(vector, slot):
-    return pltpu.roll(vector, (-PITCH * slot - HALO) % LANES, 1)
+def middle_of(slot):
+    return PITCH * slot + HALO
+
+
+def middle_of_extra(index):
+    return 2 * PITCH + 2 * REACH * index + REACH
+
+
+def border_of(vector, at):
+    return pltpu.roll(vector, -at % LANES, 1)
 
 
 def pack_kernel(feat_ref, tile_ref, edge_ref, rows_ref):
@@ -47,14 +44,14 @@
     lane = lane_iota((channels, lanes))
     for group, (first, last) in enumerate(GROUPS):
         packed = jnp.zeros((channels, lanes), jnp.float32)
-        taken = list(range(first, last))
+        taken = [(row, middle_of(row - first), HALO) for row in range(first, last)]
         if group == 1:
-            taken += EXTRA(height)
-        for slot, row in enumerate(taken):
+            taken += [(row, middle_of_extra(i), REACH) for i, row in enumerate((0, 1, height - 2, height - 1))]
+        for row, at, wide in taken:
             value = rows_ref[pl.ds(row, channels, stride=height), :]
-            if slot < last - first:
+            if wide == HALO:
                 tile_ref[row] = value.astype(jnp.bfloat16)
-            packed = jnp.where(in_slot(lane, slot), packed_edge(value, slot), packed)
+            packed = jnp.where((lane >= at - wide) & (lane < at + wide), pltpu.roll(value, at % lanes, 1), packed)
         edge_ref[group] = packed.astype(jnp.bfloat16)
 
 
@@ -106,8 +103,8 @@
     return total
 
 
-def lay_both(tile, vector, slot, *targets):
-    border = border_of(vector, slot).astype(jnp.bfloat16)
+def lay_both(tile, vector, at, *targets):
+    border = border_of(vector, at).astype(jnp.bfloat16)
     for ref, start in targets:
         block = pl.ds(start, tile.shape[0])
         ref[block, :LANES] = tile
@@ -116,11 +113,17 @@
 
 def middle_kernel(
     keep_ref, own_tile_ref, other_tile_ref, own_joined_ref, other_joined_ref,
-    w_first_ref, w_second_ref, head_ref, offsets_ref, fractions_ref, tissue_ref,
-    band_ref, side_ref, near_ref, base_ref, cover_ref, first_w_ref, second_w_ref, sums_ref, motion_ref, hats_ref,
-    window_ref, hidden_ref, second_ref, part_ref,
+    w_first_ref, w_second_ref, offsets_ref, fractions_ref, head_in_ref, tissue_in_ref,
+    band_ref, side_ref, near_ref, base_ref, cover_ref, first_w_ref, second_w_ref, sums_ref, motion_ref, hats_ref, head_ref,
+    window_ref, hidden_ref, second_ref, part_ref, tissue_ref, sems,
 ):
     height, channels, lanes = own_tile_ref.shape
+    copies = [
+        pltpu.make_async_copy(head_in_ref, head_ref, sems.at[0]),
+        pltpu.make_async_copy(tissue_in_ref, tissue_ref, sems.at[1]),
+    ]
+    for copy in copies:
+        copy.start()
     both = 2 * channels
     for b in range(3):
         block = pl.ds(b * channels, channels)
@@ -132,8 +135,8 @@
         own_vector = own_joined_ref[group].astype(jnp.float32)
         other_vector = other_joined_ref[group].astype(jnp.float32)
         for row in range(first, last):
-            lay_both(own_tile_ref[row], own_vector, row - first, (band_ref, row * channels), (window_ref, row * both))
-            lay_both(other_tile_ref[row], other_vector, row - first, (window_ref, row * both + channels))
+            lay_both(own_tile_ref[row], own_vector, middle_of(row - first), (band_ref, row * channels), (window_ref, row * both))
+            lay_both(other_tile_ref[row], other_vector, middle_of(row - first), (window_ref, row * both + channels))
     side_ref[: 2 * both] = window_ref[: 2 * both]
     side_ref[2 * both :] = window_ref[(height - 2) * both :]
     keep = keep_ref[0:1]
@@ -147,6 +150,8 @@
     for index in range(len(inner)):
         taken = hidden_ref[pl.ds(index * channels, 3 * channels), :]
         second_ref[:, index * lanes : (index + 1) * lanes] = second_row(taken, second_w_ref)
+    for copy in copies:
+        copy.wait()
     project(second_ref, inner, head_ref, part_ref)
 
     cells = tissue_ref[...].astype(jnp.float32)
@@ -188,21 +193,34 @@
     return jnp.where(is_fresh, fresh, inner_motion_ref[:, block, :])
 
 
+def message_row(ref, index, channels):
+    return ref[pl.ds(index * channels, channels), :]
+
+
+def message_borders(ref, channels):
+    last = (HALO + 3) * channels
+    folded = ref[last:, :].astype(jnp.float32)
+    unfolded = jnp.concatenate([folded, pltpu.roll(folded, LANES // 2, 1)])
+    return message_row(ref, HALO + 2, channels).astype(jnp.float32), unfolded
+
+
 def top_kernel(
     keep_ref, band_ref, near_side_ref, near_ref, base_ref, cover_ref, first_w_ref, second_w_ref, sums_ref,
     inner_motion_ref, hats_ref, above_ref, head_ref,
     top_ref, motion_ref, halo_ref, side_ref, hidden_ref, second_ref, residual_ref,
 ):
-    channels = above_ref.shape[1]
+    channels = head_ref.shape[1]
     both = 2 * channels
-    middle, last = above_ref[HALO + 2].astype(jnp.float32), above_ref[HALO + 3].astype(jnp.float32)
+    seven, two = message_borders(above_ref, channels)
     for index in range(HALO):
         targets = [(halo_ref, index * channels)]
         if index >= HALO - 2:
             targets.append((side_ref, (index - HALO + 2) * both))
-        lay_both(above_ref[index], *((middle, index) if index < 2 else (last, index - 2)), *targets)
+        strip = (two, middle_of(index)) if index < 2 else (seven, middle_of(index - 2))
+        lay_both(message_row(above_ref, index, channels), *strip, *targets)
     for index in range(2):
-        lay_both(above_ref[HALO + index], middle, 4 + index, (side_ref, index * both + channels))
+        tile = message_row(above_ref, HALO + index, channels)
+        lay_both(tile, two, middle_of_extra(2 + index), (side_ref, index * both + channels))
     side_ref[2 * both :] = near_side_ref[: 2 * both]
     hidden_ref[both:] = near_ref[:both]
     keeps = (keep_ref[1:2], keep_ref[0:1])
@@ -228,14 +246,16 @@
     channels, height, lanes = warped_ref.shape
     both = 2 * channels
     half = height // 2
-    first, center = below_ref[HALO + 2].astype(jnp.float32), below_ref[HALO + 3].astype(jnp.float32)
+    seven, two = message_borders(below_ref, channels)
     for index in range(HALO):
         targets = [(halo_ref, index * channels)]
         if index < 2:
             targets.append((side_ref, (2 + index) * both))
-        lay_both(below_ref[index], *((first, index) if index < 7 else (center, index - 7)), *targets)
+        strip = (seven, middle_of(index)) if index < 7 else (two, middle_of(index - 7))
+        lay_both(message_row(below_ref, index, channels), *strip, *targets)
     for index in range(2):
-        lay_both(below_ref[HALO + index], center, 2 + index, (side_ref, (2 + index) * both + channels))
+        tile = message_row(below_ref, HALO + index, channels)
+        lay_both(tile, two, middle_of_extra(index), (side_ref, (2 + index) * both + channels))
     side_ref[: 2 * both] = near_side_ref[2 * both :]
     hidden_ref[:both] = near_ref[both:]
     keeps = (keep_ref[0:1], keep_ref[2:3])
@@ -266,6 +286,9 @@
             for ch in range(channels):
                 value = rows_ref[pl.ds(ch, half, stride=channels), :]
                 staged_ref[ch, :half, :] = value.astype(jnp.bfloat16)
+            upper = pl.ds(0, half)
+            upper_copy = pltpu.make_async_copy(staged_ref.at[:, upper], warped_ref.at[:, upper], sems.at[5])
+            upper_copy.start()
     row = height - 2
     start = row - HALO
     hat = column_weights(motion_ref, row)
@@ -277,23 +300,24 @@
         for ch in range(part * piece, (part + 1) * piece):
             value = rows_ref[pl.ds(half * channels + ch, half, stride=channels), :]
             staged_ref[ch, half:, :] = value.astype(jnp.bfloat16)
-        block = pl.ds(part * piece, piece)
-        copies.append(pltpu.make_async_copy(staged_ref.at[block], warped_ref.at[block], sems.at[part]))
+        block, lower = pl.ds(part * piece, piece), pl.ds(half, half)
+        copies.append(pltpu.make_async_copy(staged_ref.at[block, lower], warped_ref.at[block, lower], sems.at[part]))
         copies[-1].start()
-    for copy in (field_copy, *copies):
+    for copy in (field_copy, upper_copy, *copies):
         copy.wait()
 
 
 VMEM = pl.BlockSpec(memory_space=pltpu.VMEM)
-
-
-def call(body, outputs, scratch, *operands, flops=0, placed=()):
+ANY = pl.BlockSpec(memory_space=pltpu.HBM)
+
+
+def call(body, outputs, scratch, *operands, flops=0, placed=(), far=0):
     moved = sum(x.size * x.dtype.itemsize for x in (*operands, *outputs))
     return pl.pallas_call(
         body,
         out_shape=outputs,
-        in_specs=[VMEM] * len(operands),
-        out_specs=[pl.BlockSpec(memory_space=pl.ANY) if i in placed else VMEM for i in range(len(outputs))],
+        in_specs=[VMEM] * (len(operands) - far) + [ANY] * far,
+        out_specs=[ANY if i in placed else VMEM for i in range(len(outputs))],
         scratch_shapes=scratch,
         compiler_params=pltpu.CompilerParams(vmem_limit_bytes=40 * 2**20),
         cost_estimate=pl.CostEstimate(flops=flops, bytes_accessed=moved, transcendentals=0),
@@ -340,19 +364,26 @@
     from_right = ring(edge, "col", -1)
     other_tile = lax.ppermute(own_tile, "pair", swap)
     lane = jnp.arange(columns)
+    group = jnp.arange(len(GROUPS))[:, None, None]
+    is_left = jnp.where((group == 1) & (lane >= 2 * PITCH), (lane - 2 * PITCH) % (2 * REACH) < REACH, lane % PITCH < HALO)
     joined = jnp.where(
-        lane % PITCH < HALO,
+        is_left,
         jnp.where(col == 0, jnp.zeros_like(from_left), from_left),
         jnp.where(col == cols - 1, jnp.zeros_like(from_right), from_right),
     )
     both_joined = lax.all_gather(joined, "pair")
     other_joined = jnp.where(lax.axis_index("pair") == 0, both_joined[1], both_joined[0])
-    mixed = jnp.where(lane < 2 * PITCH, other_joined[1], joined[1])[None]
-    above = across(jnp.concatenate([other_tile[height - HALO :], own_tile[height - 2 :], mixed, other_joined[2:]]), 1)
-    below = across(jnp.concatenate([other_tile[:HALO], own_tile[:2], other_joined[:1], mixed]), -1)
+    mixed = jnp.where(lane < 2 * PITCH, other_joined[1], joined[1])
+    folded = jnp.concatenate([mixed[: channels // 2, : columns // 2], mixed[channels // 2 :, : columns // 2]], axis=1)
+
+    def message(*parts):
+        return jnp.concatenate([*(part.reshape(-1, columns) for part in parts), folded])
+
+    above = across(message(other_tile[height - HALO :], own_tile[height - REACH :], other_joined[2]), 1)
+    below = across(message(other_tile[:HALO], own_tile[:REACH], other_joined[0]), -1)
 
     wide = height * channels
-    band, side, near, base, cover, first_w, second_w, sums, inner_motion, hats = call(
+    band, side, near, base, cover, first_w, second_w, sums, inner_motion, hats, head = call(
         middle_kernel,
         [
             of((wide, RING)),
@@ -365,16 +396,19 @@
             of(((height // 2 - 2) * channels, RING), f32),
             of((2, height, columns), f32),
             of((height // 2 - 2, RING, RING)),
+            of(head_weight.shape),
         ],
         [
             pltpu.VMEM((2 * wide, RING), bf16),
             pltpu.VMEM(((height - 2) * channels, RING), bf16),
             pltpu.VMEM((channels, (height - 4) * columns), bf16),
             pltpu.VMEM((2, height, columns), f32),
+            pltpu.VMEM(tissue.shape[1:], jnp.int32),
+            pltpu.SemaphoreType.DMA((2,)),
         ],
         keep, own_tile, other_tile, joined, other_joined,
-        w_first, w_second, head_weight, offsets[0], fractions[0], tissue[0],
-        flops=4 * 10**9,
+        w_first, w_second, offsets[0], fractions[0], head_weight, tissue[0],
+        flops=4 * 10**9, far=2,
     )
     common = (keep, band, side, near, base, cover, first_w, second_w, sums, inner_motion, hats)
     edge_scratch = [
@@ -388,7 +422,7 @@
         top_kernel,
         [of((5 * channels, RING), f32), of((2, height // 2, columns), f32)],
         edge_scratch,
-        *common, above, head_weight,
+        *common, above, head,
         flops=10**9,
     )
     warped, motion = call(
@@ -399,9 +433,9 @@
             pltpu.VMEM((2, height, columns), f32),
             pltpu.VMEM((wide, columns), f32),
             pltpu.VMEM((channels, height, columns), bf16),
-            pltpu.SemaphoreType.DMA((5,)),
+            pltpu.SemaphoreType.DMA((6,)),
         ],
-        *common, top, top_motion, below, head_weight,
+        *common, top, top_motion, below, head,
         flops=10**9, placed=(0, 1),
     )
     return (warped[None], motion[None])

time: 38.3 us -> 38.2 us (level)
  transfers between devices with their start and end apart: 5 -> 5, of which waited for: 3 -> 3; matrix products, arithmetic and copies ran while one was open for 0% -> 1% of each run, Pallas kernels for 10% -> 10%
where the time goes in v6:
time: 38.2 us; the launch traced here: 38 us
  starting transfers between devices  18.4 us (48%)
  Pallas kernels  6.4 us (17%)
  waiting for transfers between devices  5.6 us (15%)
  blocking collectives  4.77 us (12%)
  local copies, waits for them, and re-layouts  1.64 us (4%)
  between operations  0.88 us (2%)
    ppermute x2, starting transfers between devices, ring(): lax.ppermute(value, axis, [(i, (i + step) % peers) for i in range(peers)])  8.49 us
    ppermute x2, starting transfers between devices, across(): return lax.ppermute(value, ('pair', 'row', 'col'), pairs)  7.17 us
    pallas_call x4, Pallas kernels, call(): pl.pallas_call(body, out_shape=outputs, in_specs=[VMEM] * (len(operands)...  6.4 us
    all_gather x1, blocking collectives, shards(): both_joined = lax.all_gather(joined, 'pair')  4.77 us
    ppermute x2, waiting for transfers between devices, across(): return lax.ppermute(value, ('pair', 'row', 'col'), pairs)  3.87 us
    ppermute x1, starting transfers between devices, shards(): other_tile = lax.ppermute(own_tile, 'pair', swap)  2.73 us
    ppermute x2, waiting for transfers between devices, ring(): lax.ppermute(value, axis, [(i, (i + step) % peers) for i in range(peers)])  1.73 us
    unnamed x14, local copies, waits for them, and re-layouts  1.6 us
  transfers between devices with their start and end apart: 5, of which 3 were waited for; matrix products, arithmetic and copies ran while one was open for 1% of the time, Pallas kernels for 10%

profile of v6, /device:TPU:30, one launch (start us, length us, event | category | flops | bytes accessed | tf_op | source)
XLA Modules:
  0.0 38.0 jit_solution(4842522496082625116)
XLA Ops:
  0.6 0.0 copy-start
  0.6 0.9 %copy-done = bf16[1,64,16,128]{3,2,1,0:T(8,128)(2,1)S(1)} copy-done((bf16[1,64,16,128]{3,2,1,0:T(8,128)(2,1)S(1)}, bf16[1,64,16,128]{3,2,1,0:T(8,128)(2,1)}, u32[]{:S(2)}) %copy-start) | copy-done | bytes 262168
  1.6 0.3 shard_map.86
  1.9 8.5 %collective-permute-start.2 = (bf16[3,64,128]{2,1,0:T(8,128)(2,1)S(1)}, bf16[3,64,128]{2,1,0:T(8,128)(2,1)S(1)}, u32[]{:S(2)}, u32[]{:S(2)}) collective-permute-start(bf16[3,64,128]{2,1,0:T(8,128)(2,1)S(1)} %get-tuple-element.20), channel_id=1, source_target_pairs={{0,15},{1,0},{2,1},{3,2},{4,3},{5,4},{6,5},{7,6},{8,7},{9,8},{10,9... | collective-permute-start | bytes 147464 | tf_op jit(solution)/shard_map/ppermute | solution.py:333
  10.4 0.0 collective-permute-start.1
  10.4 2.7 %collective-permute-start = (bf16[16,64,128]{2,1,0:T(8,128)(2,1)S(1)}, bf16[16,64,128]{2,1,0:T(8,128)(2,1)S(1)}, u32[]{:S(2)}, u32[]{:S(2)}) collective-permute-start(bf16[16,64,128]{2,1,0:T(8,128)(2,1)S(1)} %get-tuple-element.19.own_tile_ref), channel_id=1, source_target_pairs={{0,256},{256,0},{1,257},{257,1},{2,258},{258,2},{3,259},{259,3},{4... | collective-permute-start | bytes 786440 | tf_op jit(solution)/shard_map/ppermute | solution.py:365
  13.2 0.1 and_convert_fusion.keep_ref
  13.3 0.1 and_select_fusion.2
  13.4 0.0 collective-permute-done.2
  13.4 1.7 %collective-permute-done.1 = bf16[3,64,128]{2,1,0:T(8,128)(2,1)S(1)} collective-permute-done((bf16[3,64,128]{2,1,0:T(8,128)(2,1)S(1)}, bf16[3,64,128]{2,1,0:T(8,128)(2,1)S(1)}, u32[]{:S(2)}, u32[]{:S(2)}) %collective-permute-start.1) | collective-permute-done | bytes 49184 | tf_op jit(solution)/shard_map/ppermute | solution.py:333
  15.1 4.8 %all-gather = bf16[6,64,128]{2,1,0:T(8,128)(2,1)S(1)} all-gather(bf16[3,64,128]{2,1,0:T(8,128)(2,1)S(1)} %select_select_fusion.own_joined_ref), channel_id=2, replica_groups=mesh['pair'=2,'row'=16,'col'=16] {'pair'}, dimensions={0}, use_global_device_ids=true | all-gather | bytes 147456 | tf_op jit(solution)/shard_map/all_gather | solution.py:374
  20.0 0.0 collective-permute-done.other_tile_ref
  20.0 0.0 copy-start.1
  20.0 0.0 copy-start.2
  20.0 0.0 copy-start.3
  20.0 0.0 copy-start.4
  20.1 0.1 fusion
  20.1 4.7 %collective-permute-start.3 = (bf16[800,128]{1,0:T(8,128)(2,1)S(1)}, bf16[800,128]{1,0:T(8,128)(2,1)S(1)}, u32[]{:S(2)}, u32[]{:S(2)}) collective-permute-start(bf16[800,128]{1,0:T(8,128)(2,1)S(1)} %get-tuple-element.43), channel_id=1, source_target_pairs={{0,272},{1,273},{2,274},{3,275},{4,276},{5,277},{6,278},{7,279},{8... | collective-permute-start | bytes 614408 | tf_op jit(solution)/shard_map/ppermute | solution.py:346
  24.9 2.4 %collective-permute-start.4 = (bf16[800,128]{1,0:T(8,128)(2,1)S(1)}, bf16[800,128]{1,0:T(8,128)(2,1)S(1)}, u32[]{:S(2)}, u32[]{:S(2)}) collective-permute-start(bf16[800,128]{1,0:T(8,128)(2,1)S(1)} %get-tuple-element.42), channel_id=1, source_target_pairs={{16,256},{17,257},{18,258},{19,259},{20,260},{21,261},{22,262},{23... | collective-permute-start | bytes 614408 | tf_op jit(solution)/shard_map/ppermute | solution.py:346
  27.3 0.0 copy-start.5
  27.3 0.0 copy-start.6
  27.3 0.0 copy-done.1
  27.4 0.0 copy-done.2
  27.4 0.0 copy-done.3
  27.4 0.0 copy-done.4
  27.4 0.6 %copy-done.5 = s32[1,2,16]{2,1,0:T(2,128)S(1)} copy-done((s32[1,2,16]{2,1,0:T(2,128)S(1)}, s32[1,2,16]{2,1,0:T(2,128)}, u32[]{:S(2)}) %copy-start.5) | copy-done | bytes 152
  28.0 0.0 copy-done.6
  28.0 2.7 %shard_map.87 = (bf16[1024,256]{1,0:T(8,128)(2,1)S(1)}, bf16[512,256]{1,0:T(8,128)(2,1)S(1)}, bf16[256,256]{1,0:T(8,128)(2,1)S(1)}, f32[2,16,128]{2,1,0:T(8,128)...) custom-call(f32[8,256]{1,0:T(8,128)S(1)} %and_convert_fusion.keep_re, ...), custom_call_target="tpu_custom_call" | custom-call | flops 4000000000 | bytes 3244672 | tf_op jit(solution)/shard_map/pallas_call | solution.py:316
  30.7 0.6 %collective-permute-done.3.above_ref = bf16[800,128]{1,0:T(8,128)(2,1)S(1)} collective-permute-done((bf16[800,128]{1,0:T(8,128)(2,1)S(1)}, bf16[800,128]{1,0:T(8,128)(2,1)S(1)}, u32[]{:S(2)}, u32[]{:S(2)}) %collective-permute-start.3) | collective-permute-done | bytes 204832 | tf_op jit(solution)/shard_map/ppermute | solution.py:346
  31.3 1.3 %shard_map.88 = (f32[320,256]{1,0:T(8,128)S(1)}, f32[2,8,128]{2,1,0:T(8,128)S(1)}) custom-call(f32[8,256]{1,0:T(8,128)S(1)} %and_convert_fusion.keep_ref, bf16[1024,256]{1,0:T(8,128)(2,1)S(1)} %get-tuple-element.21.band_ref, bf16[512,256]{1,0:T(8,128)(2,1)S(1)} %get-tuple-element.22.near_side_ref, bf16[256,256]{1,0:T(8,128)(2,1)S(1)} %get-tuple-element.23.near_ref, ...), custom_call_target="tpu_custom_call" | custom-call | flops 1000000000 | bytes 2908416 | tf_op jit(solution)/shard_map/pallas_call | solution.py:316
  32.6 3.2 %collective-permute-done.4.below_ref = bf16[800,128]{1,0:T(8,128)(2,1)S(1)} collective-permute-done((bf16[800,128]{1,0:T(8,128)(2,1)S(1)}, bf16[800,128]{1,0:T(8,128)(2,1)S(1)}, u32[]{:S(2)}, u32[]{:S(2)}) %collective-permute-start.4) | collective-permute-done | bytes 204832 | tf_op jit(solution)/shard_map/ppermute | solution.py:346
  35.8 2.1 %shard_map.89 = (bf16[64,16,128]{2,1,0:T(8,128)(2,1)}, f32[2,16,128]{2,1,0:T(8,128)}) custom-call(f32[8,256]{1,0:T(8,128)S(1)} %and_convert_fusion.keep_ref, bf16[1024,256]{1,0:T(8,128)(2,1)S(1)} %get-tuple-element.21.band_ref, bf16[512,256]{1,0:T(8,128)(2,1)S(1)} %get-tuple-element.22.near_side_ref, bf16[256,256]{1,0:T(8,128)(2,1)S(1)} %get-tuple-element.23.near_ref, ...), custom_call_target="tpu_custom_call" | custom-call | flops 1000000000 | bytes 3186944 | tf_op jit(solution)/shard_map/pallas_call | solution.py:316
  (14 shorter events, 0.1 us)
Async XLA Ops:
  0.6 1.0 %copy-start = (bf16[1,64,16,128]{3,2,1,0:T(8,128)(2,1)S(1)}, bf16[1,64,16,128]{3,2,1,0:T(8,128)(2,1)}, u32[]{:S(2)}) copy-start(bf16[1,64,16,128]{3,2,1,0:T(8,128)(2,1)} %param.7) | copy-start | bytes 786436
  1.9 11.5 %collective-permute-start.2 = (bf16[3,64,128]{2,1,0:T(8,128)(2,1)S(1)}, bf16[3,64,128]{2,1,0:T(8,128)(2,1)S(1)}, u32[]{:S(2)}, u32[]{:S(2)}) collective-permute-start(bf16[3,64,128]{2,1,0:T(8,128)(2,1)S(1)} %get-tuple-element.20), channel_id=1, source_target_pairs={{0,15},{1,0},{2,1},{3,2},{4,3},{5,4},{6,5},{7,6},{8,7},{9,8},{10,9... | collective-permute-start | bytes 147464 | tf_op jit(solution)/shard_map/ppermute | solution.py:333
  10.4 4.7 %collective-permute-start.1 = (bf16[3,64,128]{2,1,0:T(8,128)(2,1)S(1)}, bf16[3,64,128]{2,1,0:T(8,128)(2,1)S(1)}, u32[]{:S(2)}, u32[]{:S(2)}) collective-permute-start(bf16[3,64,128]{2,1,0:T(8,128)(2,1)S(1)} %get-tuple-element.20), channel_id=1, source_target_pairs={{0,1},{1,2},{2,3},{3,4},{4,5},{5,6},{6,7},{7,8},{8,9},{9,10},{10,1... | collective-permute-start | bytes 147464 | tf_op jit(solution)/shard_map/ppermute | solution.py:333
  10.4 9.6 %collective-permute-start = (bf16[16,64,128]{2,1,0:T(8,128)(2,1)S(1)}, bf16[16,64,128]{2,1,0:T(8,128)(2,1)S(1)}, u32[]{:S(2)}, u32[]{:S(2)}) collective-permute-start(bf16[16,64,128]{2,1,0:T(8,128)(2,1)S(1)} %get-tuple-element.19.own_tile_ref), channel_id=1, source_target_pairs={{0,256},{256,0},{1,257},{257,1},{2,258},{258,2},{3,259},{259,3},{4... | collective-permute-start | bytes 786440 | tf_op jit(solution)/shard_map/ppermute | solution.py:365
  20.0 7.3 %copy-start.1 = (bf16[9,64,128]{2,1,0:T(8,128)(2,1)S(1)}, bf16[9,64,128]{2,1,0:T(8,128)(2,1)}, u32[]{:S(2)}) copy-start(bf16[9,64,128]{2,1,0:T(8,128)(2,1)} %w_first_ref.1) | copy-start | bytes 442372
  20.0 7.3 %copy-start.2 = (bf16[9,64,64]{2,1,0:T(8,128)(2,1)S(1)}, bf16[9,64,64]{2,1,0:T(8,128)(2,1)}, u32[]{:S(2)}) copy-start(bf16[9,64,64]{2,1,0:T(8,128)(2,1)} %w_second_ref.1) | copy-start | bytes 221188
  20.0 7.3 %copy-start.3 = (s32[1,2,16,128]{3,2,1,0:T(8,128)S(1)}, s32[1,2,16,128]{3,2,1,0:T(8,128)}, u32[]{:S(2)}) copy-start(s32[1,2,16,128]{3,2,1,0:T(8,128)} %param.8) | copy-start | bytes 49156
  20.0 7.3 %copy-start.4 = (s32[1,2,16,128]{3,2,1,0:T(8,128)S(1)}, s32[1,2,16,128]{3,2,1,0:T(8,128)}, u32[]{:S(2)}) copy-start(s32[1,2,16,128]{3,2,1,0:T(8,128)} %param.9) | copy-start | bytes 49156
  20.1 11.2 %collective-permute-start.3 = (bf16[800,128]{1,0:T(8,128)(2,1)S(1)}, bf16[800,128]{1,0:T(8,128)(2,1)S(1)}, u32[]{:S(2)}, u32[]{:S(2)}) collective-permute-start(bf16[800,128]{1,0:T(8,128)(2,1)S(1)} %get-tuple-element.43), channel_id=1, source_target_pairs={{0,272},{1,273},{2,274},{3,275},{4,276},{5,277},{6,278},{7,279},{8... | collective-permute-start | bytes 614408 | tf_op jit(solution)/shard_map/ppermute | solution.py:346
  24.9 11.0 %collective-permute-start.4 = (bf16[800,128]{1,0:T(8,128)(2,1)S(1)}, bf16[800,128]{1,0:T(8,128)(2,1)S(1)}, u32[]{:S(2)}, u32[]{:S(2)}) collective-permute-start(bf16[800,128]{1,0:T(8,128)(2,1)S(1)} %get-tuple-element.42), channel_id=1, source_target_pairs={{16,256},{17,257},{18,258},{19,259},{20,260},{21,261},{22,262},{23... | collective-permute-start | bytes 614408 | tf_op jit(solution)/shard_map/ppermute | solution.py:346
  27.3 0.7 %copy-start.5 = (s32[1,2,16]{2,1,0:T(2,128)S(1)}, s32[1,2,16]{2,1,0:T(2,128)}, u32[]{:S(2)}) copy-start(s32[1,2,16]{2,1,0:T(2,128)} %param.10) | copy-start | bytes 388
  27.3 0.7 %copy-start.6 = (bf16[2,64]{1,0:T(2,128)(2,1)S(1)}, bf16[2,64]{1,0:T(2,128)(2,1)}, u32[]{:S(2)}) copy-start(bf16[2,64]{1,0:T(2,128)(2,1)} %head_in_ref.1) | copy-start | bytes 772

commit v7 on v6

--- a/solution.py
+++ b/solution.py
@@ -18,6 +18,7 @@
 GROUPS = ((0, 7), (7, 9), (9, 16))
 
 
+VECTOR = (0, 2, 1)
 frac_scale = 256.0
 
 
@@ -52,7 +53,10 @@
             if wide == HALO:
                 tile_ref[row] = value.astype(jnp.bfloat16)
             packed = jnp.where((lane >= at - wide) & (lane < at + wide), pltpu.roll(value, at % lanes, 1), packed)
-        edge_ref[group] = packed.astype(jnp.bfloat16)
+        if group == 1:
+            half = channels // 2
+            packed = jnp.where(lane[:half] < lanes // 2, packed[:half], pltpu.roll(packed[half:], lanes // 2, 1))
+        edge_ref[pl.ds(VECTOR[group] * channels, packed.shape[0]), :] = packed.astype(jnp.bfloat16)
 
 
 def shifted_sum(stacked):
@@ -132,8 +136,8 @@
         second_w_ref[block, :both] = jnp.concatenate([w_second_ref[b], w_second_ref[3 + b]], axis=1)
         second_w_ref[block, both:] = w_second_ref[6 + b]
     for group, (first, last) in enumerate(GROUPS):
-        own_vector = own_joined_ref[group].astype(jnp.float32)
-        other_vector = other_joined_ref[group].astype(jnp.float32)
+        own_vector = group_vector(own_joined_ref, group, channels)
+        other_vector = group_vector(other_joined_ref, group, channels)
         for row in range(first, last):
             lay_both(own_tile_ref[row], own_vector, middle_of(row - first), (band_ref, row * channels), (window_ref, row * both))
             lay_both(other_tile_ref[row], other_vector, middle_of(row - first), (window_ref, row * both + channels))
@@ -197,11 +201,19 @@
     return ref[pl.ds(index * channels, channels), :]
 
 
+def unfolded(ref, start):
+    folded = ref[start:, :].astype(jnp.float32)
+    return jnp.concatenate([folded, pltpu.roll(folded, LANES // 2, 1)])
+
+
 def message_borders(ref, channels):
-    last = (HALO + 3) * channels
-    folded = ref[last:, :].astype(jnp.float32)
-    unfolded = jnp.concatenate([folded, pltpu.roll(folded, LANES // 2, 1)])
-    return message_row(ref, HALO + 2, channels).astype(jnp.float32), unfolded
+    return message_row(ref, HALO + 2, channels).astype(jnp.float32), unfolded(ref, (HALO + 3) * channels)
+
+
+def group_vector(ref, group, channels):
+    if group == 1:
+        return unfolded(ref, VECTOR[group] * channels)
+    return message_row(ref, VECTOR[group], channels).astype(jnp.float32)
 
 
 def top_kernel(
@@ -359,28 +371,28 @@
     swap = [(0, 1), (1, 0)]
     tile_shape = (height, channels, columns)
     scratch = [pltpu.VMEM((height * channels, columns), f32)]
-    own_tile, edge = call(pack_kernel, [of(tile_shape), of((3, channels, columns))], scratch, features[0])
+    own_tile, edge = call(pack_kernel, [of(tile_shape), of((5 * channels // 2, columns))], scratch, features[0])
     from_left = ring(edge, "col", 1)
     from_right = ring(edge, "col", -1)
     other_tile = lax.ppermute(own_tile, "pair", swap)
-    lane = jnp.arange(columns)
-    group = jnp.arange(len(GROUPS))[:, None, None]
-    is_left = jnp.where((group == 1) & (lane >= 2 * PITCH), (lane - 2 * PITCH) % (2 * REACH) < REACH, lane % PITCH < HALO)
-    joined = jnp.where(
-        is_left,
-        jnp.where(col == 0, jnp.zeros_like(from_left), from_left),
-        jnp.where(col == cols - 1, jnp.zeros_like(from_right), from_right),
-    )
+    lane, line = jnp.arange(columns), jnp.arange(edge.shape[0])[:, None]
+    place = jnp.where(line < 2 * channels, lane, lane % (columns // 2))
+    is_extra = (line >= 2 * channels) & (place >= 2 * PITCH)
+    is_left = jnp.where(is_extra, (place - 2 * PITCH) % (2 * REACH) < REACH, place % PITCH < HALO)
+    masks = jnp.stack([is_left & (col > 0), ~is_left & (col < cols - 1)]).astype(bf16)
+    from_where = lax.optimization_barrier(masks)
+    zero = jnp.zeros_like(from_left)
+    joined = jnp.where(from_where[0] > 0, from_left, jnp.where(from_where[1] > 0, from_right, zero))
     both_joined = lax.all_gather(joined, "pair")
     other_joined = jnp.where(lax.axis_index("pair") == 0, both_joined[1], both_joined[0])
-    mixed = jnp.where(lane < 2 * PITCH, other_joined[1], joined[1])
-    folded = jnp.concatenate([mixed[: channels // 2, : columns // 2], mixed[channels // 2 :, : columns // 2]], axis=1)
-
-    def message(*parts):
-        return jnp.concatenate([*(part.reshape(-1, columns) for part in parts), folded])
-
-    above = across(message(other_tile[height - HALO :], own_tile[height - REACH :], other_joined[2]), 1)
-    below = across(message(other_tile[:HALO], own_tile[:REACH], other_joined[0]), -1)
+    start = 2 * channels
+    mixed = jnp.where(lane % (columns // 2) < 2 * PITCH, other_joined[start:], joined[start:])
+
+    def message(vector, *parts):
+        return jnp.concatenate([*(part.reshape(-1, columns) for part in parts), vector, mixed])
+
+    above = across(message(other_joined[channels:start], other_tile[height - HALO :], own_tile[height - REACH :]), 1)
+    below = across(message(other_joined[:channels], other_tile[:HALO], own_tile[:REACH]), -1)
 
     wide = height * channels
     band, side, near, base, cover, first_w, second_w, sums, inner_motion, hats, head = call(

time: 38.2 us -> 37.4 us (0.979)
  waiting for transfers between devices: 5.6 us -> 3.85 us
  blocking collectives: 4.77 us -> 5.53 us
    ppermute x2, waiting for transfers between devices: 1.73 us -> 0.01 us  [ring(): lax.ppermute(value, axis, [(i, (i + step) % peers) for i in range(peers)])]
    all_gather x1, blocking collectives: 4.77 us -> 5.53 us  [shards(): both_joined = lax.all_gather(joined, 'pair')]
  transfers between devices with their start and end apart: 5 -> 5, of which waited for: 3 -> 1; matrix products, arithmetic and copies ran while one was open for 1% -> 1% of each run, Pallas kernels for 10% -> 11%
where the time goes in v7:
time: 37.4 us; the launch traced here: 37.2 us
  starting transfers between devices  18.4 us (49%)
  Pallas kernels  6.43 us (17%)
  blocking collectives  5.53 us (15%)
  waiting for transfers between devices  3.85 us (10%)
  local copies, waits for them, and re-layouts  1.64 us (4%)
  between operations  0.9 us (2%)
  other arithmetic  0.4 us (1%)
    ppermute x2, starting transfers between devices, ring(): lax.ppermute(value, axis, [(i, (i + step) % peers) for i in range(peers)])  8.51 us
    ppermute x2, starting transfers between devices, across(): return lax.ppermute(value, ('pair', 'row', 'col'), pairs)  7.18 us
    pallas_call x4, Pallas kernels, call(): pl.pallas_call(body, out_shape=outputs, in_specs=[VMEM] * (len(operands)...  6.43 us
    all_gather x1, blocking collectives, shards(): both_joined = lax.all_gather(joined, 'pair')  5.53 us
    ppermute x2, waiting for transfers between devices, across(): return lax.ppermute(value, ('pair', 'row', 'col'), pairs)  3.84 us
    ppermute x1, starting transfers between devices, shards(): other_tile = lax.ppermute(own_tile, 'pair', swap)  2.72 us
    unnamed x14, local copies, waits for them, and re-layouts  1.6 us
  transfers between devices with their start and end apart: 5, of which 1 were waited for; matrix products, arithmetic and copies ran while one was open for 1% of the time, Pallas kernels for 11%

profile of v7, /device:TPU:30, one launch (start us, length us, event | category | flops | bytes accessed | tf_op | source)
XLA Modules:
  0.0 37.2 jit_solution(14836557629350548648)
XLA Ops:
  0.6 0.0 copy-start
  0.6 0.9 %copy-done = bf16[1,64,16,128]{3,2,1,0:T(8,128)(2,1)S(1)} copy-done((bf16[1,64,16,128]{3,2,1,0:T(8,128)(2,1)S(1)}, bf16[1,64,16,128]{3,2,1,0:T(8,128)(2,1)}, u32[]{:S(2)}) %copy-start) | copy-done | bytes 262168
  1.6 0.3 shard_map.86
  1.9 0.0 collective-permute-start.1
  1.9 8.5 %collective-permute-start.2 = (bf16[160,128]{1,0:T(8,128)(2,1)S(1)}, bf16[160,128]{1,0:T(8,128)(2,1)S(1)}, u32[]{:S(2)}, u32[]{:S(2)}) collective-permute-start(bf16[160,128]{1,0:T(8,128)(2,1)S(1)} %get-tuple-element.20), channel_id=1, source_target_pairs={{0,15},{1,0},{2,1},{3,2},{4,3},{5,4},{6,5},{7,6},{8,7},{9,8},{10,9... | collective-permute-start | bytes 122888 | tf_op jit(solution)/shard_map/ppermute | solution.py:345
  10.4 2.7 %collective-permute-start = (bf16[16,64,128]{2,1,0:T(8,128)(2,1)S(1)}, bf16[16,64,128]{2,1,0:T(8,128)(2,1)S(1)}, u32[]{:S(2)}, u32[]{:S(2)}) collective-permute-start(bf16[16,64,128]{2,1,0:T(8,128)(2,1)S(1)} %get-tuple-element.19.own_tile_ref), channel_id=1, source_target_pairs={{0,256},{256,0},{1,257},{257,1},{2,258},{258,2},{3,259},{259,3},{4... | collective-permute-start | bytes 786440 | tf_op jit(solution)/shard_map/ppermute | solution.py:377
  13.2 0.2 fusion.10
  13.5 0.1 and_convert_fusion.keep_ref
  13.5 0.0 collective-permute-done.1
  13.5 0.0 collective-permute-done.2
  13.6 5.5 %all-gather = bf16[320,128]{1,0:T(8,128)(2,1)S(1)} all-gather(bf16[160,128]{1,0:T(8,128)(2,1)S(1)} %bitcast_select_fusion.1.own_joined_ref), channel_id=2, replica_groups=mesh['pair'=2,'row'=16,'col'=16] {'pair'}, dimensions={0}, use_global_device_ids=true | all-gather | bytes 122880 | tf_op jit(solution)/shard_map/all_gather | solution.py:386
  19.2 0.0 collective-permute-done.other_tile_ref
  19.2 0.0 copy-start.1
  19.2 0.0 copy-start.2
  19.2 0.0 copy-start.3
  19.2 0.0 copy-start.4
  19.3 4.7 %collective-permute-start.3 = (bf16[800,128]{1,0:T(8,128)(2,1)S(1)}, bf16[800,128]{1,0:T(8,128)(2,1)S(1)}, u32[]{:S(2)}, u32[]{:S(2)}) collective-permute-start(bf16[800,128]{1,0:T(8,128)(2,1)S(1)} %get-tuple-element.43), channel_id=1, source_target_pairs={{0,272},{1,273},{2,274},{3,275},{4,276},{5,277},{6,278},{7,279},{8... | collective-permute-start | bytes 614408 | tf_op jit(solution)/shard_map/ppermute | solution.py:358
  24.0 2.4 %collective-permute-start.4 = (bf16[800,128]{1,0:T(8,128)(2,1)S(1)}, bf16[800,128]{1,0:T(8,128)(2,1)S(1)}, u32[]{:S(2)}, u32[]{:S(2)}) collective-permute-start(bf16[800,128]{1,0:T(8,128)(2,1)S(1)} %get-tuple-element.42), channel_id=1, source_target_pairs={{16,256},{17,257},{18,258},{19,259},{20,260},{21,261},{22,262},{23... | collective-permute-start | bytes 614408 | tf_op jit(solution)/shard_map/ppermute | solution.py:358
  26.5 0.0 copy-start.5
  26.5 0.0 copy-start.6
  26.5 0.0 copy-done.1
  26.5 0.0 copy-done.2
  26.5 0.0 copy-done.3
  26.5 0.0 copy-done.4
  26.5 0.6 %copy-done.5 = s32[1,2,16]{2,1,0:T(2,128)S(1)} copy-done((s32[1,2,16]{2,1,0:T(2,128)S(1)}, s32[1,2,16]{2,1,0:T(2,128)}, u32[]{:S(2)}) %copy-start.5) | copy-done | bytes 152
  27.2 0.0 copy-done.6
  27.2 2.7 %shard_map.87 = (bf16[1024,256]{1,0:T(8,128)(2,1)S(1)}, bf16[512,256]{1,0:T(8,128)(2,1)S(1)}, bf16[256,256]{1,0:T(8,128)(2,1)S(1)}, f32[2,16,128]{2,1,0:T(8,128)...) custom-call(f32[8,256]{1,0:T(8,128)S(1)} %and_convert_fusion.keep_re, ...), custom_call_target="tpu_custom_call" | custom-call | flops 4000000000 | bytes 3228288 | tf_op jit(solution)/shard_map/pallas_call | solution.py:328
  29.9 0.0 collective-permute-done.3.above_ref
  29.9 1.3 %shard_map.88 = (f32[320,256]{1,0:T(8,128)S(1)}, f32[2,8,128]{2,1,0:T(8,128)S(1)}) custom-call(f32[8,256]{1,0:T(8,128)S(1)} %and_convert_fusion.keep_ref, bf16[1024,256]{1,0:T(8,128)(2,1)S(1)} %get-tuple-element.21.band_ref, bf16[512,256]{1,0:T(8,128)(2,1)S(1)} %get-tuple-element.22.near_side_ref, bf16[256,256]{1,0:T(8,128)(2,1)S(1)} %get-tuple-element.23.near_ref, ...), custom_call_target="tpu_custom_call" | custom-call | flops 1000000000 | bytes 2908416 | tf_op jit(solution)/shard_map/pallas_call | solution.py:328
  31.2 3.8 %collective-permute-done.4.below_ref = bf16[800,128]{1,0:T(8,128)(2,1)S(1)} collective-permute-done((bf16[800,128]{1,0:T(8,128)(2,1)S(1)}, bf16[800,128]{1,0:T(8,128)(2,1)S(1)}, u32[]{:S(2)}, u32[]{:S(2)}) %collective-permute-start.4) | collective-permute-done | bytes 204832 | tf_op jit(solution)/shard_map/ppermute | solution.py:358
  35.0 2.1 %shard_map.89 = (bf16[64,16,128]{2,1,0:T(8,128)(2,1)}, f32[2,16,128]{2,1,0:T(8,128)}) custom-call(f32[8,256]{1,0:T(8,128)S(1)} %and_convert_fusion.keep_ref, bf16[1024,256]{1,0:T(8,128)(2,1)S(1)} %get-tuple-element.21.band_ref, bf16[512,256]{1,0:T(8,128)(2,1)S(1)} %get-tuple-element.22.near_side_ref, bf16[256,256]{1,0:T(8,128)(2,1)S(1)} %get-tuple-element.23.near_ref, ...), custom_call_target="tpu_custom_call" | custom-call | flops 1000000000 | bytes 3186944 | tf_op jit(solution)/shard_map/pallas_call | solution.py:328
  (14 shorter events, 0.2 us)
Async XLA Ops:
  0.6 1.0 %copy-start = (bf16[1,64,16,128]{3,2,1,0:T(8,128)(2,1)S(1)}, bf16[1,64,16,128]{3,2,1,0:T(8,128)(2,1)}, u32[]{:S(2)}) copy-start(bf16[1,64,16,128]{3,2,1,0:T(8,128)(2,1)} %param.7) | copy-start | bytes 786436
  1.9 11.7 %collective-permute-start.1 = (bf16[160,128]{1,0:T(8,128)(2,1)S(1)}, bf16[160,128]{1,0:T(8,128)(2,1)S(1)}, u32[]{:S(2)}, u32[]{:S(2)}) collective-permute-start(bf16[160,128]{1,0:T(8,128)(2,1)S(1)} %get-tuple-element.20), channel_id=1, source_target_pairs={{0,1},{1,2},{2,3},{3,4},{4,5},{5,6},{6,7},{7,8},{8,9},{9,10},{10,1... | collective-permute-start | bytes 122888 | tf_op jit(solution)/shard_map/ppermute | solution.py:345
  1.9 11.6 %collective-permute-start.2 = (bf16[160,128]{1,0:T(8,128)(2,1)S(1)}, bf16[160,128]{1,0:T(8,128)(2,1)S(1)}, u32[]{:S(2)}, u32[]{:S(2)}) collective-permute-start(bf16[160,128]{1,0:T(8,128)(2,1)S(1)} %get-tuple-element.20), channel_id=1, source_target_pairs={{0,15},{1,0},{2,1},{3,2},{4,3},{5,4},{6,5},{7,6},{8,7},{9,8},{10,9... | collective-permute-start | bytes 122888 | tf_op jit(solution)/shard_map/ppermute | solution.py:345
  10.4 8.8 %collective-permute-start = (bf16[16,64,128]{2,1,0:T(8,128)(2,1)S(1)}, bf16[16,64,128]{2,1,0:T(8,128)(2,1)S(1)}, u32[]{:S(2)}, u32[]{:S(2)}) collective-permute-start(bf16[16,64,128]{2,1,0:T(8,128)(2,1)S(1)} %get-tuple-element.19.own_tile_ref), channel_id=1, source_target_pairs={{0,256},{256,0},{1,257},{257,1},{2,258},{258,2},{3,259},{259,3},{4... | collective-permute-start | bytes 786440 | tf_op jit(solution)/shard_map/ppermute | solution.py:377
  19.2 7.3 %copy-start.1 = (bf16[9,64,128]{2,1,0:T(8,128)(2,1)S(1)}, bf16[9,64,128]{2,1,0:T(8,128)(2,1)}, u32[]{:S(2)}) copy-start(bf16[9,64,128]{2,1,0:T(8,128)(2,1)} %w_first_ref.1) | copy-start | bytes 442372
  19.2 7.3 %copy-start.2 = (bf16[9,64,64]{2,1,0:T(8,128)(2,1)S(1)}, bf16[9,64,64]{2,1,0:T(8,128)(2,1)}, u32[]{:S(2)}) copy-start(bf16[9,64,64]{2,1,0:T(8,128)(2,1)} %w_second_ref.1) | copy-start | bytes 221188
  19.2 7.3 %copy-start.3 = (s32[1,2,16,128]{3,2,1,0:T(8,128)S(1)}, s32[1,2,16,128]{3,2,1,0:T(8,128)}, u32[]{:S(2)}) copy-start(s32[1,2,16,128]{3,2,1,0:T(8,128)} %param.8) | copy-start | bytes 49156
  19.2 7.3 %copy-start.4 = (s32[1,2,16,128]{3,2,1,0:T(8,128)S(1)}, s32[1,2,16,128]{3,2,1,0:T(8,128)}, u32[]{:S(2)}) copy-start(s32[1,2,16,128]{3,2,1,0:T(8,128)} %param.9) | copy-start | bytes 49156
  19.3 10.6 %collective-permute-start.3 = (bf16[800,128]{1,0:T(8,128)(2,1)S(1)}, bf16[800,128]{1,0:T(8,128)(2,1)S(1)}, u32[]{:S(2)}, u32[]{:S(2)}) collective-permute-start(bf16[800,128]{1,0:T(8,128)(2,1)S(1)} %get-tuple-element.43), channel_id=1, source_target_pairs={{0,272},{1,273},{2,274},{3,275},{4,276},{5,277},{6,278},{7,279},{8... | collective-permute-start | bytes 614408 | tf_op jit(solution)/shard_map/ppermute | solution.py:358
  24.0 11.0 %collective-permute-start.4 = (bf16[800,128]{1,0:T(8,128)(2,1)S(1)}, bf16[800,128]{1,0:T(8,128)(2,1)S(1)}, u32[]{:S(2)}, u32[]{:S(2)}) collective-permute-start(bf16[800,128]{1,0:T(8,128)(2,1)S(1)} %get-tuple-element.42), channel_id=1, source_target_pairs={{16,256},{17,257},{18,258},{19,259},{20,260},{21,261},{22,262},{23... | collective-permute-start | bytes 614408 | tf_op jit(solution)/shard_map/ppermute | solution.py:358
  26.5 0.7 %copy-start.5 = (s32[1,2,16]{2,1,0:T(2,128)S(1)}, s32[1,2,16]{2,1,0:T(2,128)}, u32[]{:S(2)}) copy-start(s32[1,2,16]{2,1,0:T(2,128)} %param.10) | copy-start | bytes 388
  26.5 0.7 %copy-start.6 = (bf16[2,64]{1,0:T(2,128)(2,1)S(1)}, bf16[2,64]{1,0:T(2,128)(2,1)}, u32[]{:S(2)}) copy-start(bf16[2,64]{1,0:T(2,128)(2,1)} %head_in_ref.1) | copy-start | bytes 772

commit v8 on v7

--- a/solution.py
+++ b/solution.py
@@ -66,6 +66,15 @@
     return left + stacked[count : 2 * count] + right
 
 
+def keep_of(sides_ref, line=None):
+    def flag(index):
+        return jnp.concatenate([sides_ref[index : index + 1, :]] * 2, axis=1)
+
+    lane = lane_iota((1, RING))
+    keep = jnp.where(lane == RING - 1, flag(5), jnp.where(lane == LANES, flag(6), 1.0))
+    return keep if line is None else keep * flag(line)
+
+
 def hidden_row(taken, first_w_ref, keep):
     total = jnp.dot(first_w_ref[...], taken, preferred_element_type=jnp.float32)
     return (jnp.maximum(shifted_sum(total), 0.0) * keep).astype(jnp.bfloat16)
@@ -116,7 +125,7 @@
 
 
 def middle_kernel(
-    keep_ref, own_tile_ref, other_tile_ref, own_joined_ref, other_joined_ref,
+    sides_ref, own_tile_ref, other_tile_ref, own_joined_ref, other_joined_ref,
     w_first_ref, w_second_ref, offsets_ref, fractions_ref, head_in_ref, tissue_in_ref,
     band_ref, side_ref, near_ref, base_ref, cover_ref, first_w_ref, second_w_ref, sums_ref, motion_ref, hats_ref, head_ref,
     window_ref, hidden_ref, second_ref, part_ref, tissue_ref, sems,
@@ -143,7 +152,7 @@
             lay_both(other_tile_ref[row], other_vector, middle_of(row - first), (window_ref, row * both + channels))
     side_ref[: 2 * both] = window_ref[: 2 * both]
     side_ref[2 * both :] = window_ref[(height - 2) * both :]
-    keep = keep_ref[0:1]
+    keep = keep_of(sides_ref)
     for row in range(1, height - 1):
         taken = window_ref[pl.ds((row - 1) * both, 3 * both), :]
         hidden_ref[pl.ds((row - 1) * channels, channels), :] = hidden_row(taken, first_w_ref, keep)
@@ -217,7 +226,7 @@
 
 
 def top_kernel(
-    keep_ref, band_ref, near_side_ref, near_ref, base_ref, cover_ref, first_w_ref, second_w_ref, sums_ref,
+    sides_ref, band_ref, near_side_ref, near_ref, base_ref, cover_ref, first_w_ref, second_w_ref, sums_ref,
     inner_motion_ref, hats_ref, above_ref, head_ref,
     top_ref, motion_ref, halo_ref, side_ref, hidden_ref, second_ref, residual_ref,
 ):
@@ -235,7 +244,7 @@
         lay_both(tile, two, middle_of_extra(2 + index), (side_ref, index * both + channels))
     side_ref[2 * both :] = near_side_ref[: 2 * both]
     hidden_ref[both:] = near_ref[:both]
-    keeps = (keep_ref[1:2], keep_ref[0:1])
+    keeps = (keep_of(sides_ref, 7), keep_of(sides_ref))
     weights = (first_w_ref, second_w_ref, head_ref)
     motion_ref[...] = new_motion(
         side_ref, hidden_ref, second_ref, (0, 1), keeps, (0, 1), weights, (base_ref, cover_ref), 0, inner_motion_ref, residual_ref
@@ -251,7 +260,7 @@
 
 
 def bottom_kernel(
-    keep_ref, band_ref, near_side_ref, near_ref, base_ref, cover_ref, first_w_ref, second_w_ref, sums_ref,
+    sides_ref, band_ref, near_side_ref, near_ref, base_ref, cover_ref, first_w_ref, second_w_ref, sums_ref,
     inner_motion_ref, hats_ref, top_ref, top_motion_ref, below_ref, head_ref,
     warped_ref, field_ref, halo_ref, side_ref, hidden_ref, second_ref, residual_ref, motion_ref, rows_ref, staged_ref, sems,
 ):
@@ -270,7 +279,7 @@
         lay_both(tile, two, middle_of_extra(index), (side_ref, (2 + index) * both + channels))
     side_ref[: 2 * both] = near_side_ref[2 * both :]
     hidden_ref[:both] = near_ref[both:]
-    keeps = (keep_ref[0:1], keep_ref[2:3])
+    keeps = (keep_of(sides_ref), keep_of(sides_ref, 8))
     weights = (first_w_ref, second_w_ref, head_ref)
     motion_ref[:, :half, :] = top_motion_ref[...]
     motion_ref[:, half:, :] = new_motion(
@@ -363,11 +372,6 @@
     f32, bf16 = jnp.float32, jnp.bfloat16
     row, col = lax.axis_index("row"), lax.axis_index("col")
     rows, cols = lax.axis_size("row"), lax.axis_size("col")
-    ring_lane = jnp.arange(RING)[None]
-    inside = ((col > 0) | (ring_lane != RING - 1)) & ((col < cols - 1) | (ring_lane != LANES))
-    line = jnp.arange(8)[:, None]
-    keep = (inside & ((line != 1) | (row > 0)) & ((line != 2) | (row < rows - 1))).astype(f32)
-
     swap = [(0, 1), (1, 0)]
     tile_shape = (height, channels, columns)
     scratch = [pltpu.VMEM((height * channels, columns), f32)]
@@ -375,18 +379,21 @@
     from_left = ring(edge, "col", 1)
     from_right = ring(edge, "col", -1)
     other_tile = lax.ppermute(own_tile, "pair", swap)
-    lane, line = jnp.arange(columns), jnp.arange(edge.shape[0])[:, None]
-    place = jnp.where(line < 2 * channels, lane, lane % (columns // 2))
-    is_extra = (line >= 2 * channels) & (place >= 2 * PITCH)
-    is_left = jnp.where(is_extra, (place - 2 * PITCH) % (2 * REACH) < REACH, place % PITCH < HALO)
-    masks = jnp.stack([is_left & (col > 0), ~is_left & (col < cols - 1)]).astype(bf16)
-    from_where = lax.optimization_barrier(masks)
-    zero = jnp.zeros_like(from_left)
-    joined = jnp.where(from_where[0] > 0, from_left, jnp.where(from_where[1] > 0, from_right, zero))
+    lane = jnp.arange(columns)
+    place = lane % (columns // 2)
+    left = lane % PITCH < HALO
+    left_folded = jnp.where(place < 2 * PITCH, place % PITCH < HALO, (place - 2 * PITCH) % (2 * REACH) < REACH)
+    has_left, has_right = col > 0, col < cols - 1
+    sides = [left & has_left, ~left & has_right, left_folded & has_left, ~left_folded & has_right, place < 2 * PITCH]
+    sides += [jnp.broadcast_to(flag, lane.shape) for flag in (has_left, has_right, row > 0, row < rows - 1)]
+    sides = lax.optimization_barrier(jnp.stack(sides).astype(f32))
+    is_folded = jnp.arange(edge.shape[0])[:, None] >= 2 * channels
+    from_where = [jnp.where(is_folded, sides[2 + i], sides[i]) > 0 for i in range(2)]
+    joined = jnp.where(from_where[0], from_left, jnp.where(from_where[1], from_right, jnp.zeros_like(from_left)))
     both_joined = lax.all_gather(joined, "pair")
     other_joined = jnp.where(lax.axis_index("pair") == 0, both_joined[1], both_joined[0])
     start = 2 * channels
-    mixed = jnp.where(lane % (columns // 2) < 2 * PITCH, other_joined[start:], joined[start:])
+    mixed = jnp.where(sides[4] > 0, other_joined[start:], joined[start:])
 
     def message(vector, *parts):
         return jnp.concatenate([*(part.reshape(-1, columns) for part in parts), vector, mixed])
@@ -418,11 +425,11 @@
             pltpu.VMEM(tissue.shape[1:], jnp.int32),
             pltpu.SemaphoreType.DMA((2,)),
         ],
-        keep, own_tile, other_tile, joined, other_joined,
+        sides, own_tile, other_tile, joined, other_joined,
         w_first, w_second, offsets[0], fractions[0], head_weight, tissue[0],
         flops=4 * 10**9, far=2,
     )
-    common = (keep, band, side, near, base, cover, first_w, second_w, sums, inner_motion, hats)
+    common = (sides, band, side, near, base, cover, first_w, second_w, sums, inner_motion, hats)
     edge_scratch = [
         pltpu.VMEM((HALO * channels, RING), bf16),
         pltpu.VMEM((8 * channels, RING), bf16),

time: 37.4 us -> 37.4 us (level)
  no operation moved by 1% of the time
where the time goes in v8:
time: 37.4 us; the launch traced here: 37.2 us
  starting transfers between devices  18.4 us (49%)
  Pallas kernels  6.42 us (17%)
  blocking collectives  5.6 us (15%)
  waiting for transfers between devices  3.86 us (10%)
  local copies, waits for them, and re-layouts  1.72 us (5%)
  between operations  0.92 us (2%)
    ppermute x2, starting transfers between devices, ring(): lax.ppermute(value, axis, [(i, (i + step) % peers) for i in range(peers)])  8.51 us
    ppermute x2, starting transfers between devices, across(): return lax.ppermute(value, ('pair', 'row', 'col'), pairs)  7.18 us
    pallas_call x4, Pallas kernels, call(): pl.pallas_call(body, out_shape=outputs, in_specs=[VMEM] * (len(operands)...  6.42 us
    all_gather x1, blocking collectives, shards(): both_joined = lax.all_gather(joined, 'pair')  5.6 us
    ppermute x2, waiting for transfers between devices, across(): return lax.ppermute(value, ('pair', 'row', 'col'), pairs)  3.85 us
    ppermute x1, starting transfers between devices, shards(): other_tile = lax.ppermute(own_tile, 'pair', swap)  2.72 us
    unnamed x14, local copies, waits for them, and re-layouts  1.6 us
  transfers between devices with their start and end apart: 5, of which 1 were waited for; matrix products, arithmetic and copies ran while one was open for 1% of the time, Pallas kernels for 11%

profile of v8, /device:TPU:30, one launch (start us, length us, event | category | flops | bytes accessed | tf_op | source)
XLA Modules:
  0.0 37.2 jit_solution(7126355954759697252)
XLA Ops:
  0.6 0.0 copy-start
  0.6 0.9 %copy-done = bf16[1,64,16,128]{3,2,1,0:T(8,128)(2,1)S(1)} copy-done((bf16[1,64,16,128]{3,2,1,0:T(8,128)(2,1)S(1)}, bf16[1,64,16,128]{3,2,1,0:T(8,128)(2,1)}, u32[]{:S(2)}) %copy-start) | copy-done | bytes 262168
  1.6 0.3 shard_map.86
  1.9 0.0 collective-permute-start.1
  1.9 8.5 %collective-permute-start.2 = (bf16[160,128]{1,0:T(8,128)(2,1)S(1)}, bf16[160,128]{1,0:T(8,128)(2,1)S(1)}, u32[]{:S(2)}, u32[]{:S(2)}) collective-permute-start(bf16[160,128]{1,0:T(8,128)(2,1)S(1)} %get-tuple-element.20), channel_id=1, source_target_pairs={{0,15},{1,0},{2,1},{3,2},{4,3},{5,4},{6,5},{7,6},{8,7},{9,8},{10,9... | collective-permute-start | bytes 122888 | tf_op jit(solution)/shard_map/ppermute | solution.py:354
  10.4 2.7 %collective-permute-start = (bf16[16,64,128]{2,1,0:T(8,128)(2,1)S(1)}, bf16[16,64,128]{2,1,0:T(8,128)(2,1)S(1)}, u32[]{:S(2)}, u32[]{:S(2)}) collective-permute-start(bf16[16,64,128]{2,1,0:T(8,128)(2,1)S(1)} %get-tuple-element.19.own_tile_ref), channel_id=1, source_target_pairs={{0,256},{256,0},{1,257},{257,1},{2,258},{258,2},{3,259},{259,3},{4... | collective-permute-start | bytes 786440 | tf_op jit(solution)/shard_map/ppermute | solution.py:381
  13.3 0.1 stack.2
  13.4 0.0 collective-permute-done.1
  13.4 0.0 collective-permute-done.2
  13.4 0.1 fusion.own_joined_ref
  13.5 5.6 %all-gather = bf16[320,128]{1,0:T(8,128)(2,1)S(1)} all-gather(bf16[160,128]{1,0:T(8,128)(2,1)S(1)} %fusion.own_joined_ref), channel_id=2, replica_groups=mesh['pair'=2,'row'=16,'col'=16] {'pair'}, dimensions={0}, use_global_device_ids=true | all-gather | bytes 122880 | tf_op jit(solution)/shard_map/all_gather | solution.py:393
  19.2 0.0 collective-permute-done.other_tile_ref
  19.2 0.0 copy-start.1
  19.2 0.0 copy-start.2
  19.2 0.0 copy-start.3
  19.2 0.0 copy-start.4
  19.3 4.7 %collective-permute-start.3 = (bf16[800,128]{1,0:T(8,128)(2,1)S(1)}, bf16[800,128]{1,0:T(8,128)(2,1)S(1)}, u32[]{:S(2)}, u32[]{:S(2)}) collective-permute-start(bf16[800,128]{1,0:T(8,128)(2,1)S(1)} %get-tuple-element.43), channel_id=1, source_target_pairs={{0,272},{1,273},{2,274},{3,275},{4,276},{5,277},{6,278},{7,279},{8... | collective-permute-start | bytes 614408 | tf_op jit(solution)/shard_map/ppermute | solution.py:367
  24.0 2.4 %collective-permute-start.4 = (bf16[800,128]{1,0:T(8,128)(2,1)S(1)}, bf16[800,128]{1,0:T(8,128)(2,1)S(1)}, u32[]{:S(2)}, u32[]{:S(2)}) collective-permute-start(bf16[800,128]{1,0:T(8,128)(2,1)S(1)} %get-tuple-element.42), channel_id=1, source_target_pairs={{16,256},{17,257},{18,258},{19,259},{20,260},{21,261},{22,262},{23... | collective-permute-start | bytes 614408 | tf_op jit(solution)/shard_map/ppermute | solution.py:367
  26.5 0.0 copy-start.5
  26.5 0.0 copy-start.6
  26.5 0.0 copy-done.1
  26.5 0.0 copy-done.2
  26.5 0.0 copy-done.3
  26.5 0.0 copy-done.4
  26.5 0.6 %copy-done.5 = s32[1,2,16]{2,1,0:T(2,128)S(1)} copy-done((s32[1,2,16]{2,1,0:T(2,128)S(1)}, s32[1,2,16]{2,1,0:T(2,128)}, u32[]{:S(2)}) %copy-start.5) | copy-done | bytes 152
  27.2 0.0 copy-done.6
  27.2 2.7 %shard_map.87 = (bf16[1024,256]{1,0:T(8,128)(2,1)S(1)}, bf16[512,256]{1,0:T(8,128)(2,1)S(1)}, bf16[256,256]{1,0:T(8,128)(2,1)S(1)}, f32[2,16,128]{2,1,0:T(8,128)...) custom-call(f32[9,128]{1,0:T(8,128)S(1)} %convert_element_type.3.sid, ...), custom_call_target="tpu_custom_call" | custom-call | flops 4000000000 | bytes 3224704 | tf_op jit(solution)/shard_map/pallas_call | solution.py:337
  29.9 0.0 collective-permute-done.3.above_ref
  29.9 1.3 %shard_map.88 = (f32[320,256]{1,0:T(8,128)S(1)}, f32[2,8,128]{2,1,0:T(8,128)S(1)}) custom-call(f32[9,128]{1,0:T(8,128)S(1)} %convert_element_type.3.sides_ref, bf16[1024,256]{1,0:T(8,128)(2,1)S(1)} %get-tuple-element.21.band_ref, bf16[512,256]{1,0:T(8,128)(2,1)S(1)} %get-tuple-element.22.near_side_ref, bf16[256,256]{1,0:T(8,128)(2,1)S(1)} %get-tuple-element.23.near_ref, ...), custom_call_target="tpu_custom_call" | custom-call | flops 1000000000 | bytes 2904832 | tf_op jit(solution)/shard_map/pallas_call | solution.py:337
  31.2 3.8 %collective-permute-done.4.below_ref = bf16[800,128]{1,0:T(8,128)(2,1)S(1)} collective-permute-done((bf16[800,128]{1,0:T(8,128)(2,1)S(1)}, bf16[800,128]{1,0:T(8,128)(2,1)S(1)}, u32[]{:S(2)}, u32[]{:S(2)}) %collective-permute-start.4) | collective-permute-done | bytes 204832 | tf_op jit(solution)/shard_map/ppermute | solution.py:367
  35.0 2.1 %shard_map.89 = (bf16[64,16,128]{2,1,0:T(8,128)(2,1)}, f32[2,16,128]{2,1,0:T(8,128)}) custom-call(f32[9,128]{1,0:T(8,128)S(1)} %convert_element_type.3.sides_ref, bf16[1024,256]{1,0:T(8,128)(2,1)S(1)} %get-tuple-element.21.band_ref, bf16[512,256]{1,0:T(8,128)(2,1)S(1)} %get-tuple-element.22.near_side_ref, bf16[256,256]{1,0:T(8,128)(2,1)S(1)} %get-tuple-element.23.near_ref, ...), custom_call_target="tpu_custom_call" | custom-call | flops 1000000000 | bytes 3183360 | tf_op jit(solution)/shard_map/pallas_call | solution.py:337
  (18 shorter events, 0.2 us)
Async XLA Ops:
  0.6 1.0 %copy-start = (bf16[1,64,16,128]{3,2,1,0:T(8,128)(2,1)S(1)}, bf16[1,64,16,128]{3,2,1,0:T(8,128)(2,1)}, u32[]{:S(2)}) copy-start(bf16[1,64,16,128]{3,2,1,0:T(8,128)(2,1)} %param.7) | copy-start | bytes 786436
  1.9 11.5 %collective-permute-start.1 = (bf16[160,128]{1,0:T(8,128)(2,1)S(1)}, bf16[160,128]{1,0:T(8,128)(2,1)S(1)}, u32[]{:S(2)}, u32[]{:S(2)}) collective-permute-start(bf16[160,128]{1,0:T(8,128)(2,1)S(1)} %get-tuple-element.20), channel_id=1, source_target_pairs={{0,1},{1,2},{2,3},{3,4},{4,5},{5,6},{6,7},{7,8},{8,9},{9,10},{10,1... | collective-permute-start | bytes 122888 | tf_op jit(solution)/shard_map/ppermute | solution.py:354
  1.9 11.5 %collective-permute-start.2 = (bf16[160,128]{1,0:T(8,128)(2,1)S(1)}, bf16[160,128]{1,0:T(8,128)(2,1)S(1)}, u32[]{:S(2)}, u32[]{:S(2)}) collective-permute-start(bf16[160,128]{1,0:T(8,128)(2,1)S(1)} %get-tuple-element.20), channel_id=1, source_target_pairs={{0,15},{1,0},{2,1},{3,2},{4,3},{5,4},{6,5},{7,6},{8,7},{9,8},{10,9... | collective-permute-start | bytes 122888 | tf_op jit(solution)/shard_map/ppermute | solution.py:354
  10.4 8.8 %collective-permute-start = (bf16[16,64,128]{2,1,0:T(8,128)(2,1)S(1)}, bf16[16,64,128]{2,1,0:T(8,128)(2,1)S(1)}, u32[]{:S(2)}, u32[]{:S(2)}) collective-permute-start(bf16[16,64,128]{2,1,0:T(8,128)(2,1)S(1)} %get-tuple-element.19.own_tile_ref), channel_id=1, source_target_pairs={{0,256},{256,0},{1,257},{257,1},{2,258},{258,2},{3,259},{259,3},{4... | collective-permute-start | bytes 786440 | tf_op jit(solution)/shard_map/ppermute | solution.py:381
  19.2 7.3 %copy-start.1 = (bf16[9,64,128]{2,1,0:T(8,128)(2,1)S(1)}, bf16[9,64,128]{2,1,0:T(8,128)(2,1)}, u32[]{:S(2)}) copy-start(bf16[9,64,128]{2,1,0:T(8,128)(2,1)} %w_first_ref.1) | copy-start | bytes 442372
  19.2 7.3 %copy-start.2 = (bf16[9,64,64]{2,1,0:T(8,128)(2,1)S(1)}, bf16[9,64,64]{2,1,0:T(8,128)(2,1)}, u32[]{:S(2)}) copy-start(bf16[9,64,64]{2,1,0:T(8,128)(2,1)} %w_second_ref.1) | copy-start | bytes 221188
  19.2 7.3 %copy-start.3 = (s32[1,2,16,128]{3,2,1,0:T(8,128)S(1)}, s32[1,2,16,128]{3,2,1,0:T(8,128)}, u32[]{:S(2)}) copy-start(s32[1,2,16,128]{3,2,1,0:T(8,128)} %param.8) | copy-start | bytes 49156
  19.2 7.3 %copy-start.4 = (s32[1,2,16,128]{3,2,1,0:T(8,128)S(1)}, s32[1,2,16,128]{3,2,1,0:T(8,128)}, u32[]{:S(2)}) copy-start(s32[1,2,16,128]{3,2,1,0:T(8,128)} %param.9) | copy-start | bytes 49156
  19.3 10.6 %collective-permute-start.3 = (bf16[800,128]{1,0:T(8,128)(2,1)S(1)}, bf16[800,128]{1,0:T(8,128)(2,1)S(1)}, u32[]{:S(2)}, u32[]{:S(2)}) collective-permute-start(bf16[800,128]{1,0:T(8,128)(2,1)S(1)} %get-tuple-element.43), channel_id=1, source_target_pairs={{0,272},{1,273},{2,274},{3,275},{4,276},{5,277},{6,278},{7,279},{8... | collective-permute-start | bytes 614408 | tf_op jit(solution)/shard_map/ppermute | solution.py:367
  24.0 11.0 %collective-permute-start.4 = (bf16[800,128]{1,0:T(8,128)(2,1)S(1)}, bf16[800,128]{1,0:T(8,128)(2,1)S(1)}, u32[]{:S(2)}, u32[]{:S(2)}) collective-permute-start(bf16[800,128]{1,0:T(8,128)(2,1)S(1)} %get-tuple-element.42), channel_id=1, source_target_pairs={{16,256},{17,257},{18,258},{19,259},{20,260},{21,261},{22,262},{23... | collective-permute-start | bytes 614408 | tf_op jit(solution)/shard_map/ppermute | solution.py:367
  26.5 0.7 %copy-start.5 = (s32[1,2,16]{2,1,0:T(2,128)S(1)}, s32[1,2,16]{2,1,0:T(2,128)}, u32[]{:S(2)}) copy-start(s32[1,2,16]{2,1,0:T(2,128)} %param.10) | copy-start | bytes 388
  26.5 0.7 %copy-start.6 = (bf16[2,64]{1,0:T(2,128)(2,1)S(1)}, bf16[2,64]{1,0:T(2,128)(2,1)}, u32[]{:S(2)}) copy-start(bf16[2,64]{1,0:T(2,128)(2,1)} %head_in_ref.1) | copy-start | bytes 772

commit v9 on v7

--- a/solution.py
+++ b/solution.py
@@ -307,8 +307,8 @@
     total = warp_part(motion_ref, row, hat, band_ref[start * channels :, :], start, HALO + 2, None)
     keep_rows(row, warp_part(motion_ref, row, hat, halo_ref[...], height, HALO, total))
     copies = []
-    piece = channels // 4
-    for part in range(4):
+    piece = channels // 2
+    for part in range(2):
         for ch in range(part * piece, (part + 1) * piece):
             value = rows_ref[pl.ds(half * channels + ch, half, stride=channels), :]
             staged_ref[ch, half:, :] = value.astype(jnp.bfloat16)

time: 37.4 us -> 37.4 us (level)
  no operation moved by 1% of the time
where the time goes in v9:
time: 37.4 us; the launch traced here: 37.2 us
  starting transfers between devices  18.4 us (49%)
  Pallas kernels  6.44 us (17%)
  blocking collectives  5.53 us (15%)
  waiting for transfers between devices  3.85 us (10%)
  local copies, waits for them, and re-layouts  1.64 us (4%)
  between operations  0.9 us (2%)
  other arithmetic  0.4 us (1%)
    ppermute x2, starting transfers between devices, ring(): lax.ppermute(value, axis, [(i, (i + step) % peers) for i in range(peers)])  8.51 us
    ppermute x2, starting transfers between devices, across(): return lax.ppermute(value, ('pair', 'row', 'col'), pairs)  7.18 us
    pallas_call x4, Pallas kernels, call(): pl.pallas_call(body, out_shape=outputs, in_specs=[VMEM] * (len(operands)...  6.44 us
    all_gather x1, blocking collectives, shards(): both_joined = lax.all_gather(joined, 'pair')  5.53 us
    ppermute x2, waiting for transfers between devices, across(): return lax.ppermute(value, ('pair', 'row', 'col'), pairs)  3.84 us
    ppermute x1, starting transfers between devices, shards(): other_tile = lax.ppermute(own_tile, 'pair', swap)  2.72 us
    unnamed x14, local copies, waits for them, and re-layouts  1.6 us
  transfers between devices with their start and end apart: 5, of which 1 were waited for; matrix products, arithmetic and copies ran while one was open for 1% of the time, Pallas kernels for 11%

profile of v9, /device:TPU:30, one launch (start us, length us, event | category | flops | bytes accessed | tf_op | source)
XLA Modules:
  0.0 37.2 jit_solution(4643507729934023795)
XLA Ops:
  0.6 0.0 copy-start
  0.6 0.9 %copy-done = bf16[1,64,16,128]{3,2,1,0:T(8,128)(2,1)S(1)} copy-done((bf16[1,64,16,128]{3,2,1,0:T(8,128)(2,1)S(1)}, bf16[1,64,16,128]{3,2,1,0:T(8,128)(2,1)}, u32[]{:S(2)}) %copy-start) | copy-done | bytes 262168
  1.6 0.3 shard_map.86
  1.9 0.0 collective-permute-start.1
  1.9 8.5 %collective-permute-start.2 = (bf16[160,128]{1,0:T(8,128)(2,1)S(1)}, bf16[160,128]{1,0:T(8,128)(2,1)S(1)}, u32[]{:S(2)}, u32[]{:S(2)}) collective-permute-start(bf16[160,128]{1,0:T(8,128)(2,1)S(1)} %get-tuple-element.20), channel_id=1, source_target_pairs={{0,15},{1,0},{2,1},{3,2},{4,3},{5,4},{6,5},{7,6},{8,7},{9,8},{10,9... | collective-permute-start | bytes 122888 | tf_op jit(solution)/shard_map/ppermute | solution.py:345
  10.4 2.7 %collective-permute-start = (bf16[16,64,128]{2,1,0:T(8,128)(2,1)S(1)}, bf16[16,64,128]{2,1,0:T(8,128)(2,1)S(1)}, u32[]{:S(2)}, u32[]{:S(2)}) collective-permute-start(bf16[16,64,128]{2,1,0:T(8,128)(2,1)S(1)} %get-tuple-element.19.own_tile_ref), channel_id=1, source_target_pairs={{0,256},{256,0},{1,257},{257,1},{2,258},{258,2},{3,259},{259,3},{4... | collective-permute-start | bytes 786440 | tf_op jit(solution)/shard_map/ppermute | solution.py:377
  13.2 0.2 fusion.10
  13.5 0.1 and_convert_fusion.keep_ref
  13.5 0.0 collective-permute-done.1
  13.5 0.0 collective-permute-done.2
  13.6 5.5 %all-gather = bf16[320,128]{1,0:T(8,128)(2,1)S(1)} all-gather(bf16[160,128]{1,0:T(8,128)(2,1)S(1)} %bitcast_select_fusion.1.own_joined_ref), channel_id=2, replica_groups=mesh['pair'=2,'row'=16,'col'=16] {'pair'}, dimensions={0}, use_global_device_ids=true | all-gather | bytes 122880 | tf_op jit(solution)/shard_map/all_gather | solution.py:386
  19.2 0.0 collective-permute-done.other_tile_ref
  19.2 0.0 copy-start.1
  19.2 0.0 copy-start.2
  19.2 0.0 copy-start.3
  19.2 0.0 copy-start.4
  19.3 4.7 %collective-permute-start.3 = (bf16[800,128]{1,0:T(8,128)(2,1)S(1)}, bf16[800,128]{1,0:T(8,128)(2,1)S(1)}, u32[]{:S(2)}, u32[]{:S(2)}) collective-permute-start(bf16[800,128]{1,0:T(8,128)(2,1)S(1)} %get-tuple-element.43), channel_id=1, source_target_pairs={{0,272},{1,273},{2,274},{3,275},{4,276},{5,277},{6,278},{7,279},{8... | collective-permute-start | bytes 614408 | tf_op jit(solution)/shard_map/ppermute | solution.py:358
  24.0 2.4 %collective-permute-start.4 = (bf16[800,128]{1,0:T(8,128)(2,1)S(1)}, bf16[800,128]{1,0:T(8,128)(2,1)S(1)}, u32[]{:S(2)}, u32[]{:S(2)}) collective-permute-start(bf16[800,128]{1,0:T(8,128)(2,1)S(1)} %get-tuple-element.42), channel_id=1, source_target_pairs={{16,256},{17,257},{18,258},{19,259},{20,260},{21,261},{22,262},{23... | collective-permute-start | bytes 614408 | tf_op jit(solution)/shard_map/ppermute | solution.py:358
  26.5 0.0 copy-start.5
  26.5 0.0 copy-start.6
  26.5 0.0 copy-done.1
  26.5 0.0 copy-done.2
  26.5 0.0 copy-done.3
  26.5 0.0 copy-done.4
  26.5 0.6 %copy-done.5 = s32[1,2,16]{2,1,0:T(2,128)S(1)} copy-done((s32[1,2,16]{2,1,0:T(2,128)S(1)}, s32[1,2,16]{2,1,0:T(2,128)}, u32[]{:S(2)}) %copy-start.5) | copy-done | bytes 152
  27.2 0.0 copy-done.6
  27.2 2.7 %shard_map.87 = (bf16[1024,256]{1,0:T(8,128)(2,1)S(1)}, bf16[512,256]{1,0:T(8,128)(2,1)S(1)}, bf16[256,256]{1,0:T(8,128)(2,1)S(1)}, f32[2,16,128]{2,1,0:T(8,128)...) custom-call(f32[8,256]{1,0:T(8,128)S(1)} %and_convert_fusion.keep_re, ...), custom_call_target="tpu_custom_call" | custom-call | flops 4000000000 | bytes 3228288 | tf_op jit(solution)/shard_map/pallas_call | solution.py:328
  29.9 0.0 collective-permute-done.3.above_ref
  29.9 1.3 %shard_map.88 = (f32[320,256]{1,0:T(8,128)S(1)}, f32[2,8,128]{2,1,0:T(8,128)S(1)}) custom-call(f32[8,256]{1,0:T(8,128)S(1)} %and_convert_fusion.keep_ref, bf16[1024,256]{1,0:T(8,128)(2,1)S(1)} %get-tuple-element.21.band_ref, bf16[512,256]{1,0:T(8,128)(2,1)S(1)} %get-tuple-element.22.near_side_ref, bf16[256,256]{1,0:T(8,128)(2,1)S(1)} %get-tuple-element.23.near_ref, ...), custom_call_target="tpu_custom_call" | custom-call | flops 1000000000 | bytes 2908416 | tf_op jit(solution)/shard_map/pallas_call | solution.py:328
  31.2 3.8 %collective-permute-done.4.below_ref = bf16[800,128]{1,0:T(8,128)(2,1)S(1)} collective-permute-done((bf16[800,128]{1,0:T(8,128)(2,1)S(1)}, bf16[800,128]{1,0:T(8,128)(2,1)S(1)}, u32[]{:S(2)}, u32[]{:S(2)}) %collective-permute-start.4) | collective-permute-done | bytes 204832 | tf_op jit(solution)/shard_map/ppermute | solution.py:358
  35.0 2.2 %shard_map.89 = (bf16[64,16,128]{2,1,0:T(8,128)(2,1)}, f32[2,16,128]{2,1,0:T(8,128)}) custom-call(f32[8,256]{1,0:T(8,128)S(1)} %and_convert_fusion.keep_ref, bf16[1024,256]{1,0:T(8,128)(2,1)S(1)} %get-tuple-element.21.band_ref, bf16[512,256]{1,0:T(8,128)(2,1)S(1)} %get-tuple-element.22.near_side_ref, bf16[256,256]{1,0:T(8,128)(2,1)S(1)} %get-tuple-element.23.near_ref, ...), custom_call_target="tpu_custom_call" | custom-call | flops 1000000000 | bytes 3186944 | tf_op jit(solution)/shard_map/pallas_call | solution.py:328
  (14 shorter events, 0.2 us)
Async XLA Ops:
  0.6 1.0 %copy-start = (bf16[1,64,16,128]{3,2,1,0:T(8,128)(2,1)S(1)}, bf16[1,64,16,128]{3,2,1,0:T(8,128)(2,1)}, u32[]{:S(2)}) copy-start(bf16[1,64,16,128]{3,2,1,0:T(8,128)(2,1)} %param.7) | copy-start | bytes 786436
  1.9 11.7 %collective-permute-start.1 = (bf16[160,128]{1,0:T(8,128)(2,1)S(1)}, bf16[160,128]{1,0:T(8,128)(2,1)S(1)}, u32[]{:S(2)}, u32[]{:S(2)}) collective-permute-start(bf16[160,128]{1,0:T(8,128)(2,1)S(1)} %get-tuple-element.20), channel_id=1, source_target_pairs={{0,1},{1,2},{2,3},{3,4},{4,5},{5,6},{6,7},{7,8},{8,9},{9,10},{10,1... | collective-permute-start | bytes 122888 | tf_op jit(solution)/shard_map/ppermute | solution.py:345
  1.9 11.6 %collective-permute-start.2 = (bf16[160,128]{1,0:T(8,128)(2,1)S(1)}, bf16[160,128]{1,0:T(8,128)(2,1)S(1)}, u32[]{:S(2)}, u32[]{:S(2)}) collective-permute-start(bf16[160,128]{1,0:T(8,128)(2,1)S(1)} %get-tuple-element.20), channel_id=1, source_target_pairs={{0,15},{1,0},{2,1},{3,2},{4,3},{5,4},{6,5},{7,6},{8,7},{9,8},{10,9... | collective-permute-start | bytes 122888 | tf_op jit(solution)/shard_map/ppermute | solution.py:345
  10.4 8.8 %collective-permute-start = (bf16[16,64,128]{2,1,0:T(8,128)(2,1)S(1)}, bf16[16,64,128]{2,1,0:T(8,128)(2,1)S(1)}, u32[]{:S(2)}, u32[]{:S(2)}) collective-permute-start(bf16[16,64,128]{2,1,0:T(8,128)(2,1)S(1)} %get-tuple-element.19.own_tile_ref), channel_id=1, source_target_pairs={{0,256},{256,0},{1,257},{257,1},{2,258},{258,2},{3,259},{259,3},{4... | collective-permute-start | bytes 786440 | tf_op jit(solution)/shard_map/ppermute | solution.py:377
  19.2 7.3 %copy-start.1 = (bf16[9,64,128]{2,1,0:T(8,128)(2,1)S(1)}, bf16[9,64,128]{2,1,0:T(8,128)(2,1)}, u32[]{:S(2)}) copy-start(bf16[9,64,128]{2,1,0:T(8,128)(2,1)} %w_first_ref.1) | copy-start | bytes 442372
  19.2 7.3 %copy-start.2 = (bf16[9,64,64]{2,1,0:T(8,128)(2,1)S(1)}, bf16[9,64,64]{2,1,0:T(8,128)(2,1)}, u32[]{:S(2)}) copy-start(bf16[9,64,64]{2,1,0:T(8,128)(2,1)} %w_second_ref.1) | copy-start | bytes 221188
  19.2 7.3 %copy-start.3 = (s32[1,2,16,128]{3,2,1,0:T(8,128)S(1)}, s32[1,2,16,128]{3,2,1,0:T(8,128)}, u32[]{:S(2)}) copy-start(s32[1,2,16,128]{3,2,1,0:T(8,128)} %param.8) | copy-start | bytes 49156
  19.2 7.3 %copy-start.4 = (s32[1,2,16,128]{3,2,1,0:T(8,128)S(1)}, s32[1,2,16,128]{3,2,1,0:T(8,128)}, u32[]{:S(2)}) copy-start(s32[1,2,16,128]{3,2,1,0:T(8,128)} %param.9) | copy-start | bytes 49156
  19.3 10.6 %collective-permute-start.3 = (bf16[800,128]{1,0:T(8,128)(2,1)S(1)}, bf16[800,128]{1,0:T(8,128)(2,1)S(1)}, u32[]{:S(2)}, u32[]{:S(2)}) collective-permute-start(bf16[800,128]{1,0:T(8,128)(2,1)S(1)} %get-tuple-element.43), channel_id=1, source_target_pairs={{0,272},{1,273},{2,274},{3,275},{4,276},{5,277},{6,278},{7,279},{8... | collective-permute-start | bytes 614408 | tf_op jit(solution)/shard_map/ppermute | solution.py:358
  24.0 11.0 %collective-permute-start.4 = (bf16[800,128]{1,0:T(8,128)(2,1)S(1)}, bf16[800,128]{1,0:T(8,128)(2,1)S(1)}, u32[]{:S(2)}, u32[]{:S(2)}) collective-permute-start(bf16[800,128]{1,0:T(8,128)(2,1)S(1)} %get-tuple-element.42), channel_id=1, source_target_pairs={{16,256},{17,257},{18,258},{19,259},{20,260},{21,261},{22,262},{23... | collective-permute-start | bytes 614408 | tf_op jit(solution)/shard_map/ppermute | solution.py:358
  26.5 0.7 %copy-start.5 = (s32[1,2,16]{2,1,0:T(2,128)S(1)}, s32[1,2,16]{2,1,0:T(2,128)}, u32[]{:S(2)}) copy-start(s32[1,2,16]{2,1,0:T(2,128)} %param.10) | copy-start | bytes 388
  26.5 0.7 %copy-start.6 = (bf16[2,64]{1,0:T(2,128)(2,1)S(1)}, bf16[2,64]{1,0:T(2,128)(2,1)}, u32[]{:S(2)}) copy-start(bf16[2,64]{1,0:T(2,128)(2,1)} %head_in_ref.1) | copy-start | bytes 772
